TPU v7x, 128 devices: a whole 4x4x4 slice. The times are simulated.
128 devices in a mesh: seq: 16 (over x, z), text: 8 (over y, core).
Axes of the slice: x: 4, y: 4, z: 4, core: 2. Of those that a mesh axis runs over, the one named last changes fastest.
Arguments:
- queries: bfloat16 [49152, 4096], P('seq', 'text'), may hold values from -2.5 to 2.5
- keys: bfloat16 [57344, 4096], P('text', 'seq'), may hold values from -2.5 to 2.5
- values: bfloat16 [57344, 4096], P('text', 'seq'), may hold values from -6 to 6
- grad_out: bfloat16 [49152, 4096], P('seq', 'text'), may hold values from -6 to 6
- res_len: int32 [128], replicated, may hold values from 1 to 384, 30720 in all
- tok_len: int32 [128], replicated, may hold values from 1 to 448, 35840 in all
Outputs:
- grad_queries: bfloat16 [49152, 4096], P('seq', 'text')
- grad_keys: bfloat16 [57344, 4096], P('text', 'seq')
- grad_values: bfloat16 [57344, 4096], P('text', 'seq')
Inputs may be any that keep to these rules, and one draw needn't show every extreme that they name: Residue rows p * 384 + i with i >= res_len[p] are padding. Token rows of slot u(p) at positions j >= tok_len[p] are padding.
All inputs are finite; a program needn't handle non-finite values.
Results may differ from a plain program's by a relative error of at most 0.0054.
Values may be sent and summed in bfloat16 or wider, within the bound.
No kernel may reach another device: no remote copies, remote signals or barrier semaphores. Data moves between devices by JAX's collectives and lax.ppermute only.
A program may use at most 128 MiB of HBM per device.

v0:
```python
import math

import jax
import jax.numpy as jnp
from jax import lax
from jax.sharding import PartitionSpec as P

HEAD_DIM = 128
RES_TILES = 3
TOK_TILES = 7


def local_backward(queries, grad_out, keys, values, live_rows, live_tokens):
    res_slot = RES_TILES * 128
    tok_slot = TOK_TILES * 64
    feature_width = queries.shape[1]
    heads_here = feature_width // HEAD_DIM
    proteins_here = live_rows.shape[0]
    group = 2
    groups = proteins_here // group
    softmax_scale = 1.0 / math.sqrt(HEAD_DIM)
    row_index = jnp.arange(res_slot, dtype=jnp.int32)
    col_index = jnp.arange(tok_slot, dtype=jnp.int32)

    def per_group(carry, packed):
        query_part, grad_part, key_part, value_part, rows_live, tokens_live = packed
        col_ok = col_index[None, :] < tokens_live[:, None]
        row_ok = row_index[None, :] < rows_live[:, None]
        scores = (
            jnp.einsum("grhd,gthd->ghrt", query_part, key_part, preferred_element_type=jnp.float32)
            * softmax_scale
        )
        raised = jnp.where(col_ok[:, None, None, :], jnp.exp(scores), 0.0)
        total = jnp.sum(raised, axis=-1, keepdims=True)
        attention = jnp.where(row_ok[:, None, :, None], raised / total, 0.0)
        attention_b = attention.astype(jnp.bfloat16)
        output = jnp.einsum(
            "ghrt,gthd->grhd", attention_b, value_part, preferred_element_type=jnp.float32
        )
        delta = jnp.sum(grad_part.astype(jnp.float32) * output, axis=-1).transpose(0, 2, 1)
        grad_attention = jnp.einsum(
            "grhd,gthd->ghrt", grad_part, value_part, preferred_element_type=jnp.float32
        )
        scores_b = (softmax_scale * attention * (grad_attention - delta[:, :, :, None])).astype(
            jnp.bfloat16
        )
        query_grad = jnp.einsum(
            "ghrt,gthd->grhd", scores_b, key_part, preferred_element_type=jnp.float32
        ).astype(jnp.bfloat16)
        key_grad = jnp.einsum(
            "ghrt,grhd->gthd", scores_b, query_part, preferred_element_type=jnp.float32
        ).astype(jnp.bfloat16)
        value_grad = jnp.einsum(
            "ghrt,grhd->gthd", attention_b, grad_part, preferred_element_type=jnp.float32
        ).astype(jnp.bfloat16)
        return (carry, (query_grad, key_grad, value_grad))

    shaped = (
        queries.reshape(groups, group, res_slot, heads_here, HEAD_DIM),
        grad_out.reshape(groups, group, res_slot, heads_here, HEAD_DIM),
        keys.reshape(groups, group, tok_slot, heads_here, HEAD_DIM),
        values.reshape(groups, group, tok_slot, heads_here, HEAD_DIM),
        live_rows.reshape(groups, group),
        live_tokens.reshape(groups, group),
    )
    unused, (query_grads, key_grads, value_grads) = lax.scan(
        per_group, jnp.zeros((), jnp.float32), shaped
    )
    return (
        query_grads.reshape(queries.shape),
        key_grads.reshape(keys.shape),
        value_grads.reshape(values.shape),
    )


def body(queries, keys, values, grad_out, res_len, tok_len):
    text_ways = lax.axis_size("text")
    res_slot = RES_TILES * 128
    tok_slot = TOK_TILES * 64
    prot_seq = queries.shape[0] // res_slot
    feature_width = queries.shape[1]

    def by_block(field):
        return (
            field.reshape(prot_seq // text_ways, text_ways, res_slot, feature_width)
            .transpose(1, 0, 2, 3)
            .reshape(-1, feature_width)
        )

    middle_queries, middle_grads = (
        lax.all_to_all(by_block(queries), "text", split_axis=0, concat_axis=1, tiled=True),
        lax.all_to_all(by_block(grad_out), "text", split_axis=0, concat_axis=1, tiled=True),
    )
    far_queries, far_grads = (
        lax.all_to_all(middle_queries, "seq", split_axis=1, concat_axis=0, tiled=True),
        lax.all_to_all(middle_grads, "seq", split_axis=1, concat_axis=0, tiled=True),
    )
    text_block = lax.axis_index("text")
    proteins_here = keys.shape[0] // tok_slot
    live_rows = lax.dynamic_index_in_dim(
        res_len.reshape(proteins_here, text_ways), text_block, 1, keepdims=False
    )
    live_tokens = lax.dynamic_index_in_dim(
        tok_len.reshape(proteins_here, text_ways), text_block, 1, keepdims=False
    )
    far_query_grads, key_grads, value_grads = local_backward(
        far_queries, far_grads, keys, values, live_rows, live_tokens
    )
    returned = lax.all_to_all(
        lax.all_to_all(far_query_grads, "seq", split_axis=0, concat_axis=1, tiled=True),
        "text",
        split_axis=1,
        concat_axis=0,
        tiled=True,
    )
    query_grads = (
        returned.reshape(text_ways, prot_seq // text_ways, res_slot, feature_width)
        .transpose(1, 0, 2, 3)
        .reshape(-1, feature_width)
    )
    return (query_grads, key_grads, value_grads)


def solution(mesh):
    return jax.shard_map(
        body,
        mesh=mesh,
        in_specs=(P("seq", "text"), P("text", "seq"), P("text", "seq"), P("seq", "text"), P(), P()),
        out_specs=(P("seq", "text"), P("text", "seq"), P("text", "seq")),
        check_vma=False,
    )
```

profile of v0, /device:TPU:1, one launch (start us, length us, event | category | flops | bytes accessed | tf_op | source)
XLA Modules:
  0.0 385.3 jit_solution(11351983001921559295)
XLA Ops:
  0.6 43.5 %all_to_all.99 = bf16[8,384,512]{2,1,0:T(8,128)(2,1)} all-to-all(bf16[8,384,512]{2,1,0:T(8,128)(2,1)} %bitcast.128), channel_id=1, replica_groups=mesh['seq'=16,'text'=8] {'text'}, dimensions={0} | all-to-all | bytes 6291456 | tf_op jit(solution)/shard_map/all_to_all | solution.py:91
  44.1 4.6 %all-to-all-start.2 = ((bf16[8,384,512]{2,1,0:T(8,128)(2,1)}), bf16[8,384,512]{2,1,0:T(8,128)(2,1)S(1)}, u32[]{:S(2)}, u32[]{:S(2)}) async-start(bf16[8,384,512]{2,1,0:T(8,128)(2,1)} %bitcast.129), calls=%async_computation.2 | async-start | bytes 6291456 | tf_op jit(solution)/shard_map/all_to_all | solution.py:92
  48.7 4.6 %copy.20 = bf16[384,8,512]{0,2,1:T(8,128)(2,1)} copy(bf16[384,8,512]{2,0,1:T(8,128)(2,1)} %bitcast.122) | data formatting | bytes 6291456 | tf_op jit(solution)/shard_map/all_to_all | solution.py:91
  53.3 32.8 %all-to-all-done.2 = bf16[8,384,512]{2,1,0:T(8,128)(2,1)S(1)} async-done(((bf16[8,384,512]{2,1,0:T(8,128)(2,1)}), bf16[8,384,512]{2,1,0:T(8,128)(2,1)S(1)}, u32[]{:S(2)}, u32[]{:S(2)}) %all-to-all-start.2) | async-done | bytes 3145760 | tf_op jit(solution)/shard_map/all_to_all | solution.py:92
  86.2 7.6 %all-to-all-start.1 = ((bf16[384,16,256]{0,2,1:T(8,128)(2,1)}), bf16[384,16,256]{0,2,1:T(8,128)(2,1)}, u32[]{:S(2)}, u32[]{:S(2)}) async-start(bf16[384,16,256]{0,2,1:T(8,128)(2,1)} %bitcast.120), calls=%async_computation.1 | async-start | bytes 6291456 | tf_op jit(solution)/shard_map/all_to_all | solution.py:95
  93.8 2.8 copy.21
  96.7 37.8 %all-to-all-done.1 = bf16[384,16,256]{0,2,1:T(8,128)(2,1)} async-done(((bf16[384,16,256]{0,2,1:T(8,128)(2,1)}), bf16[384,16,256]{0,2,1:T(8,128)(2,1)}, u32[]{:S(2)}, u32[]{:S(2)}) %all-to-all-start.1) | async-done | bytes 3145760 | tf_op jit(solution)/shard_map/all_to_all | solution.py:95
  134.4 6.4 %all-to-all-start.3 = ((bf16[384,16,256]{0,2,1:T(8,128)(2,1)}), bf16[384,16,256]{0,2,1:T(8,128)(2,1)S(1)}, u32[]{:S(2)}, u32[]{:S(2)}) async-start(bf16[384,16,256]{0,2,1:T(8,128)(2,1)} %bitcast.7), calls=%async_computation.3 | async-start | bytes 6291456 | tf_op jit(solution)/shard_map/all_to_all | solution.py:96
  141.4 6.3 %reshape.122 = bf16[8,2,448,2,128]{4,3,2,1,0:T(2,128)(2,1)} reshape(bf16[7168,256]{1,0:T(8,128)(2,1)} %param.9) | data formatting | bytes 7340032 | tf_op jit(solution)/shard_map/reshape | solution.py:61
  147.7 6.3 %reshape.129 = bf16[8,2,448,2,128]{4,3,2,1,0:T(2,128)(2,1)} reshape(bf16[7168,256]{1,0:T(8,128)(2,1)} %param.10) | data formatting | bytes 7340032 | tf_op jit(solution)/shard_map/reshape | solution.py:62
  154.0 22.6 %all-to-all-done.3 = bf16[384,16,256]{0,2,1:T(8,128)(2,1)S(1)} async-done(((bf16[384,16,256]{0,2,1:T(8,128)(2,1)}), bf16[384,16,256]{0,2,1:T(8,128)(2,1)S(1)}, u32[]{:S(2)}, u32[]{:S(2)}) %all-to-all-start.3) | async-done | bytes 3145760 | tf_op jit(solution)/shard_map/all_to_all | solution.py:96
  176.6 115.9 %while.15 = (s32[]{:T(128)}, bf16[8,2,384,2,128]{2,4,3,1,0:T(8,128)(2,1)}, bf16[8,2,448,2,128]{4,3,2,1,0:T(2,128)(2,1)}, bf16[8,2,448,2,128]{4,3,2,1,0:T(2,128)(...) while((s32[]{:T(128)}, ...), condition=%wide.region_3.4_spmd.clone, body=%wide.region_0.3_spmd.clone.sunk | while | flops 1072659072 | bytes 50704000 | solution.py:66
  189.2 1.9 copy_dynamic-update-slice_fusion.3
  203.7 1.9 copy_dynamic-update-slice_fusion.3
  210.2 1.7 fusion.48
  218.1 1.9 copy_dynamic-update-slice_fusion.3
  224.7 1.7 fusion.48
  232.6 1.9 copy_dynamic-update-slice_fusion.3
  239.2 1.7 fusion.48
  247.1 1.9 copy_dynamic-update-slice_fusion.3
  253.7 1.7 fusion.48
  261.6 1.9 copy_dynamic-update-slice_fusion.3
  268.2 1.7 fusion.48
  276.1 1.9 copy_dynamic-update-slice_fusion.3
  282.7 1.7 fusion.48
  290.6 1.9 copy_dynamic-update-slice_fusion.3
  292.4 42.2 %all_to_all.100 = bf16[16,384,256]{1,2,0:T(8,128)(2,1)} all-to-all(bf16[16,384,256]{1,2,0:T(8,128)(2,1)} %bitcast.130), channel_id=1, replica_groups=mesh['seq'=16,'text'=8] {'seq'}, dimensions={0} | all-to-all | bytes 6291456 | tf_op jit(solution)/shard_map/all_to_all | solution.py:110
  334.7 10.3 %all-to-all-start.5 = ((bf16[384,8,512]{0,2,1:T(8,128)(2,1)}), bf16[384,8,512]{0,2,1:T(8,128)(2,1)S(1)}, u32[]{:S(2)}, u32[]{:S(2)}) async-start(bf16[384,8,512]{0,2,1:T(8,128)(2,1)} %bitcast.121), calls=%async_computation.5 | async-start | bytes 6291456 | tf_op jit(solution)/shard_map/all_to_all | solution.py:109
  345.0 4.5 %copy.52 = bf16[896,8,2,128]{3,1,2,0:T(8,128)(2,1)} copy(bf16[896,8,2,128]{3,2,1,0:T(2,128)(2,1)} %bitcast.124) | data formatting | bytes 7340032
  349.5 2.3 copy.53
  351.8 30.6 %all-to-all-done.5 = bf16[384,8,512]{0,2,1:T(8,128)(2,1)S(1)} async-done(((bf16[384,8,512]{0,2,1:T(8,128)(2,1)}), bf16[384,8,512]{0,2,1:T(8,128)(2,1)S(1)}, u32[]{:S(2)}, u32[]{:S(2)}) %all-to-all-start.5) | async-done | bytes 3145760 | tf_op jit(solution)/shard_map/all_to_all | solution.py:109
  382.4 2.9 copy.26
  (152 shorter events, 90.5 us)
Async XLA Ops:
  44.1 42.1 %all-to-all-start.2 = ((bf16[8,384,512]{2,1,0:T(8,128)(2,1)}), bf16[8,384,512]{2,1,0:T(8,128)(2,1)S(1)}, u32[]{:S(2)}, u32[]{:S(2)}) async-start(bf16[8,384,512]{2,1,0:T(8,128)(2,1)} %bitcast.129), calls=%async_computation.2 | async-start | bytes 6291456 | tf_op jit(solution)/shard_map/all_to_all | solution.py:92
  86.2 48.3 %all-to-all-start.1 = ((bf16[384,16,256]{0,2,1:T(8,128)(2,1)}), bf16[384,16,256]{0,2,1:T(8,128)(2,1)}, u32[]{:S(2)}, u32[]{:S(2)}) async-start(bf16[384,16,256]{0,2,1:T(8,128)(2,1)} %bitcast.120), calls=%async_computation.1 | async-start | bytes 6291456 | tf_op jit(solution)/shard_map/all_to_all | solution.py:95
  134.4 6.4 %copy-start.3 = (s32[128]{0:T(128)S(1)}, s32[128]{0:T(128)}, u32[]{:S(2)}) copy-start(s32[128]{0:T(128)} %param.12) | copy-start | bytes 1540
  134.4 6.5 %copy-start.4 = (s32[128]{0:T(128)S(1)}, s32[128]{0:T(128)}, u32[]{:S(2)}) copy-start(s32[128]{0:T(128)} %param.13) | copy-start | bytes 1540
  134.4 42.1 %all-to-all-start.3 = ((bf16[384,16,256]{0,2,1:T(8,128)(2,1)}), bf16[384,16,256]{0,2,1:T(8,128)(2,1)S(1)}, u32[]{:S(2)}, u32[]{:S(2)}) async-start(bf16[384,16,256]{0,2,1:T(8,128)(2,1)} %bitcast.7), calls=%async_computation.3 | async-start | bytes 6291456 | tf_op jit(solution)/shard_map/all_to_all | solution.py:96
  176.6 1.7 copy-start
  186.2 4.8 %copy-start.1 = (bf16[8,2,384,2,128]{2,4,3,1,0:T(8,128)(2,1)S(1)}, bf16[8,2,384,2,128]{2,4,3,1,0:T(8,128)(2,1)}, u32[]{:S(2)}) copy-start(bf16[8,2,384,2,128]{2,4,3,1,0:T(8,128)(2,1)} %copy-done) | copy-start | bytes 9437188 | tf_op jit(solution)/shard_map/while
  191.0 1.7 copy-start
  200.7 4.8 %copy-start.1 = (bf16[8,2,384,2,128]{2,4,3,1,0:T(8,128)(2,1)S(1)}, bf16[8,2,384,2,128]{2,4,3,1,0:T(8,128)(2,1)}, u32[]{:S(2)}) copy-start(bf16[8,2,384,2,128]{2,4,3,1,0:T(8,128)(2,1)} %copy-done) | copy-start | bytes 9437188 | tf_op jit(solution)/shard_map/while
  205.5 1.7 copy-start
  215.2 4.8 %copy-start.1 = (bf16[8,2,384,2,128]{2,4,3,1,0:T(8,128)(2,1)S(1)}, bf16[8,2,384,2,128]{2,4,3,1,0:T(8,128)(2,1)}, u32[]{:S(2)}) copy-start(bf16[8,2,384,2,128]{2,4,3,1,0:T(8,128)(2,1)} %copy-done) | copy-start | bytes 9437188 | tf_op jit(solution)/shard_map/while
  220.0 1.7 copy-start
  229.7 4.8 %copy-start.1 = (bf16[8,2,384,2,128]{2,4,3,1,0:T(8,128)(2,1)S(1)}, bf16[8,2,384,2,128]{2,4,3,1,0:T(8,128)(2,1)}, u32[]{:S(2)}) copy-start(bf16[8,2,384,2,128]{2,4,3,1,0:T(8,128)(2,1)} %copy-done) | copy-start | bytes 9437188 | tf_op jit(solution)/shard_map/while
  234.5 1.7 copy-start
  244.2 4.8 %copy-start.1 = (bf16[8,2,384,2,128]{2,4,3,1,0:T(8,128)(2,1)S(1)}, bf16[8,2,384,2,128]{2,4,3,1,0:T(8,128)(2,1)}, u32[]{:S(2)}) copy-start(bf16[8,2,384,2,128]{2,4,3,1,0:T(8,128)(2,1)} %copy-done) | copy-start | bytes 9437188 | tf_op jit(solution)/shard_map/while
  249.0 1.7 copy-start
  258.7 4.8 %copy-start.1 = (bf16[8,2,384,2,128]{2,4,3,1,0:T(8,128)(2,1)S(1)}, bf16[8,2,384,2,128]{2,4,3,1,0:T(8,128)(2,1)}, u32[]{:S(2)}) copy-start(bf16[8,2,384,2,128]{2,4,3,1,0:T(8,128)(2,1)} %copy-done) | copy-start | bytes 9437188 | tf_op jit(solution)/shard_map/while
  263.5 1.7 copy-start
  273.1 4.8 %copy-start.1 = (bf16[8,2,384,2,128]{2,4,3,1,0:T(8,128)(2,1)S(1)}, bf16[8,2,384,2,128]{2,4,3,1,0:T(8,128)(2,1)}, u32[]{:S(2)}) copy-start(bf16[8,2,384,2,128]{2,4,3,1,0:T(8,128)(2,1)} %copy-done) | copy-start | bytes 9437188 | tf_op jit(solution)/shard_map/while
  277.9 1.7 copy-start
  287.6 4.8 %copy-start.1 = (bf16[8,2,384,2,128]{2,4,3,1,0:T(8,128)(2,1)S(1)}, bf16[8,2,384,2,128]{2,4,3,1,0:T(8,128)(2,1)}, u32[]{:S(2)}) copy-start(bf16[8,2,384,2,128]{2,4,3,1,0:T(8,128)(2,1)} %copy-done) | copy-start | bytes 9437188 | tf_op jit(solution)/shard_map/while
  334.7 47.8 %all-to-all-start.5 = ((bf16[384,8,512]{0,2,1:T(8,128)(2,1)}), bf16[384,8,512]{0,2,1:T(8,128)(2,1)S(1)}, u32[]{:S(2)}, u32[]{:S(2)}) async-start(bf16[384,8,512]{0,2,1:T(8,128)(2,1)} %bitcast.121), calls=%async_computation.5 | async-start | bytes 6291456 | tf_op jit(solution)/shard_map/all_to_all | solution.py:109
  345.0 4.5 %copy-start.2 = (bf16[8,2,448,2,128]{4,3,2,1,0:T(2,128)(2,1)S(1)}, bf16[8,2,448,2,128]{4,3,2,1,0:T(2,128)(2,1)}, u32[]{:S(2)}) copy-start(bf16[8,2,448,2,128]{4,3,2,1,0:T(2,128)(2,1)} %get-tuple-element.68) | copy-start | bytes 11010052
where the time goes:
time: 387 us; the launch traced here: 385 us
  waiting for transfers between devices  124 us (32%)
  blocking collectives  85.7 us (22%)
  local copies, waits for them, and re-layouts  81.4 us (21%)
  matrix products  63 us (16%)
  starting transfers between devices  28.9 us (7%)
    all_to_all x1, blocking collectives, body(): lax.all_to_all(by_block(queries), 'text', split_axis=0, concat_axis=1, ti...  43.5 us
    all_to_all x1, blocking collectives, body(): lax.all_to_all(far_query_grads, 'seq', split_axis=0, concat_axis=1, tiled...  42.2 us
    all_to_all x1, waiting for transfers between devices, body(): lax.all_to_all(middle_queries, 'seq', split_axis=1, concat_axis=0, tiled=...  37.8 us
    all_to_all x1, waiting for transfers between devices, body(): lax.all_to_all(by_block(grad_out), 'text', split_axis=0, concat_axis=1, t...  32.8 us
    all_to_all x1, waiting for transfers between devices, body(): lax.all_to_all(lax.all_to_all(far_query_grads, 'seq', split_axis=0, conca...  30.6 us
    dynamic_slice x32, local copies, waits for them, and re-layouts, local_backward(): lax.scan(per_group, jnp.zeros((), jnp.float32), shaped)  23.6 us
    all_to_all x1, waiting for transfers between devices, body(): lax.all_to_all(middle_grads, 'seq', split_axis=1, concat_axis=0, tiled=True)  22.6 us
    dynamic_update_slice x8, local copies, waits for them, and re-layouts, local_backward(): lax.scan(per_group, jnp.zeros((), jnp.float32), shaped)  14.9 us
  transfers between devices with their start and end apart: 4, of which 4 were waited for; matrix products, arithmetic and copies ran while one was open for 7% of the time, Pallas kernels for 0%

commit v1 on v0

v1 whole, which is shorter than its diff:
```python
import math

import jax
import jax.numpy as jnp
from jax import lax
from jax.experimental import pallas as pl
from jax.experimental.pallas import tpu as pltpu
from jax.sharding import PartitionSpec as P

HEAD_DIM = 128
RES = 384
TOK = 448
RB = 128
CASES = (128, 192, 256, 320, 384, 448)
SCALE = 1.0 / math.sqrt(HEAD_DIM)
LOG2E = 1.4426950408889634
NT = (((1,), (1,)), ((), ()))
NN = (((1,), (0,)), ((), ()))
TN = (((0,), (0,)), ((), ()))


def dot(a, b, dims):
    return lax.dot_general(a, b, dims, preferred_element_type=jnp.float32)


def attention_kernel(info, q_ref, g_ref, k_ref, v_ref, dq_ref, dk_ref, dv_ref, acc_k, acc_v):
    i = pl.program_id(0)
    rows, toks = info[1, i], info[2, i]
    heads = q_ref.shape[-1] // HEAD_DIM
    live_blocks = lax.div(rows + (RB - 1), RB)

    def run(t):
        token_ok = lax.broadcasted_iota(jnp.int32, (t, RB), 0) < toks
        lane = lax.broadcasted_iota(jnp.int32, (1, RB), 1)
        acc_k[:t, :] = jnp.zeros((t, heads * HEAD_DIM), jnp.float32)
        acc_v[:t, :] = jnp.zeros((t, heads * HEAD_DIM), jnp.float32)

        def block(r, carry):
            start = pl.multiple_of(r * RB, RB)
            row_ok = lane + start < rows
            for h in range(heads):
                cols = slice(h * HEAD_DIM, (h + 1) * HEAD_DIM)
                q = q_ref[0, pl.ds(start, RB), cols]
                g = g_ref[0, pl.ds(start, RB), cols]
                k = k_ref[:t, cols]
                v = v_ref[:t, cols]
                raised = jnp.where(token_ok, jnp.exp2(dot(k, q, NT) * (SCALE * LOG2E)), 0.0)
                total = jnp.sum(raised, axis=0, keepdims=True)
                share = raised * jnp.where(row_ok, 1.0 / total, 0.0)
                share_b = share.astype(jnp.bfloat16)
                slope = dot(v, g, NT)
                delta = jnp.sum(share_b.astype(jnp.float32) * slope, axis=0, keepdims=True)
                scores_b = (share * (slope * SCALE - delta * SCALE)).astype(jnp.bfloat16)
                acc_v[:t, cols] += dot(share_b, g, NN)
                acc_k[:t, cols] += dot(scores_b, q, NN)
                dq_ref[0, pl.ds(start, RB), cols] = dot(scores_b, k, TN).astype(jnp.bfloat16)
            return carry

        lax.fori_loop(0, live_blocks, block, 0)
        dk_ref[:t, :] = acc_k[:t, :].astype(jnp.bfloat16)
        dv_ref[:t, :] = acc_v[:t, :].astype(jnp.bfloat16)
        if t < TOK:
            dk_ref[t:, :] = jnp.zeros((TOK - t, heads * HEAD_DIM), jnp.bfloat16)
            dv_ref[t:, :] = jnp.zeros((TOK - t, heads * HEAD_DIM), jnp.bfloat16)

    low = 0
    for t in CASES:
        pl.when((toks > low) & (toks <= t))(lambda t=t: run(t))
        low = t

    def clear(r, carry):
        start = pl.multiple_of(r * RB, RB)
        dq_ref[0, pl.ds(start, RB), :] = jnp.zeros((RB, heads * HEAD_DIM), jnp.bfloat16)
        return carry

    lax.fori_loop(live_blocks, RES // RB, clear, 0)


def attention_backward(info, queries, grads, keys, values):
    count, width = queries.shape[0], queries.shape[2]
    res_spec = pl.BlockSpec((1, RES, width), lambda i, info: (i, 0, 0))
    tok_spec = pl.BlockSpec((TOK, width), lambda i, info: (info[0, i], 0))
    return pl.pallas_call(
        attention_kernel,
        grid_spec=pltpu.PrefetchScalarGridSpec(
            num_scalar_prefetch=1,
            grid=(count,),
            in_specs=[res_spec, res_spec, tok_spec, tok_spec],
            out_specs=[res_spec, tok_spec, tok_spec],
            scratch_shapes=[pltpu.VMEM((TOK, width), jnp.float32)] * 2,
        ),
        out_shape=[
            jax.ShapeDtypeStruct(queries.shape, jnp.bfloat16),
            jax.ShapeDtypeStruct(keys.shape, jnp.bfloat16),
            jax.ShapeDtypeStruct(values.shape, jnp.bfloat16),
        ],
    )(info, queries, grads, keys, values)


def body(queries, keys, values, grad_out, res_len, tok_len):
    ways = lax.axis_size("text")
    width = keys.shape[1]
    count = keys.shape[0] // TOK

    def inward(field):
        mid = lax.all_to_all(field.reshape(ways, RES, -1), "text", 0, 0, tiled=True)
        mid = mid.reshape(ways, RES, -1, width).transpose(0, 2, 1, 3).reshape(count, RES, width)
        return lax.all_to_all(mid, "seq", 0, 0, tiled=True)

    far_queries, far_grads = inward(queries), inward(grad_out)
    mine = lax.axis_index("text")

    def lens(field):
        return lax.dynamic_index_in_dim(field.reshape(count, ways), mine, 1, keepdims=False)

    info = jnp.stack([jnp.arange(count, dtype=jnp.int32), lens(res_len), lens(tok_len)])
    far_dq, key_grads, value_grads = attention_backward(info, far_queries, far_grads, keys, values)
    back = lax.all_to_all(far_dq, "seq", 0, 0, tiled=True)
    back = back.reshape(ways, -1, RES, width).transpose(0, 2, 1, 3).reshape(ways, RES, -1)
    query_grads = lax.all_to_all(back, "text", 0, 0, tiled=True).reshape(queries.shape)
    return (query_grads, key_grads, value_grads)


def solution(mesh):
    return jax.shard_map(
        body,
        mesh=mesh,
        in_specs=(P("seq", "text"), P("text", "seq"), P("text", "seq"), P("seq", "text"), P(), P()),
        out_specs=(P("seq", "text"), P("text", "seq"), P("text", "seq")),
        check_vma=False,
    )
```

time: 387 us -> 311 us (0.80)
  local copies, waits for them, and re-layouts: 81.4 us -> 10.1 us
  matrix products: 63 us -> 0 us
  blocking collectives: 85.7 us -> 133 us
  Pallas kernels: 0 us -> 35.6 us
  waiting for transfers between devices: 124 us -> 107 us
  starting transfers between devices: 28.9 us -> 18.6 us
    dot_general x48 -> x0, matrix products: 63 us -> none  [the longest x8 14 us: per_group(): jnp.einsum('grhd,gthd->ghrt', query_part, key_part, preferred_element_typ...]
    all_to_all x2 -> x3, blocking collectives: 85.7 us -> 133 us  [the longest x1 47.9 us: body(): lax.all_to_all(back, 'text', 0, 0, tiled=True).reshape(queries.shape)]
    pallas_call x0 -> x1, Pallas kernels: none -> 35.6 us  [attention_backward(): pl.pallas_call(attention_kernel, grid_spec=pltpu.PrefetchScalarGridSpec(n...]
    dynamic_slice x33 -> x1, local copies, waits for them, and re-layouts: 23.8 us -> 0.19 us  [lens(): lax.dynamic_index_in_dim(field.reshape(count, ways), mine, 1, keepdims=Fa...]
    all_to_all x4 -> x3, waiting for transfers between devices: 124 us -> 107 us  [the longest x2 73.1 us: inward(): return lax.all_to_all(mid, 'seq', 0, 0, tiled=True)]
    dynamic_update_slice x8 -> x0, local copies, waits for them, and re-layouts: 14.9 us -> none  [local_backward(): lax.scan(per_group, jnp.zeros((), jnp.float32), shaped)]
    while x32 -> x0, local copies, waits for them, and re-layouts: 12.6 us -> none
    all_to_all x4 -> x3, starting transfers between devices: 28.9 us -> 18.6 us  [the longest x2 14 us: inward(): return lax.all_to_all(mid, 'seq', 0, 0, tiled=True)]
  transfers between devices with their start and end apart: 4 -> 3, of which waited for: 4 -> 3; matrix products, arithmetic and copies ran while one was open for 7% -> 2% of each run, Pallas kernels for 0% -> 0%
where the time goes in v1:
time: 311 us; the launch traced here: 309 us
  blocking collectives  133 us (43%)
  waiting for transfers between devices  107 us (34%)
  Pallas kernels  35.6 us (11%)
  starting transfers between devices  18.6 us (6%)
  local copies, waits for them, and re-layouts  10.1 us (3%)
  other arithmetic  4.38 us (1%)
    all_to_all x2, waiting for transfers between devices, inward(): return lax.all_to_all(mid, 'seq', 0, 0, tiled=True)  73.1 us
    all_to_all x1, blocking collectives, body(): lax.all_to_all(back, 'text', 0, 0, tiled=True).reshape(queries.shape)  47.9 us
    all_to_all x1, blocking collectives, inward(): mid = lax.all_to_all(field.reshape(ways, RES, -1), 'text', 0, 0, tiled=True)  43.5 us
    all_to_all x1, blocking collectives, body(): back = lax.all_to_all(far_dq, 'seq', 0, 0, tiled=True)  41.4 us
    pallas_call x1, Pallas kernels, attention_backward(): pl.pallas_call(attention_kernel, grid_spec=pltpu.PrefetchScalarGridSpec(n...  35.6 us
    all_to_all x1, waiting for transfers between devices, inward(): mid = lax.all_to_all(field.reshape(ways, RES, -1), 'text', 0, 0, tiled=True)  33.4 us
    all_to_all x2, starting transfers between devices, inward(): return lax.all_to_all(mid, 'seq', 0, 0, tiled=True)  14 us
  transfers between devices with their start and end apart: 3, of which 3 were waited for; matrix products, arithmetic and copies ran while one was open for 2% of the time, Pallas kernels for 0%

profile of v1, /device:TPU:1, one launch (start us, length us, event | category | flops | bytes accessed | tf_op | source)
XLA Modules:
  0.0 308.8 jit_solution(4506608020513891660)
XLA Ops:
  0.6 43.5 %all_to_all.30 = bf16[8,384,512]{2,1,0:T(8,128)(2,1)} all-to-all(bf16[8,384,512]{2,1,0:T(8,128)(2,1)} %bitcast.14), channel_id=1, replica_groups=mesh['seq'=16,'text'=8] {'text'}, dimensions={0} | all-to-all | bytes 6291456 | tf_op jit(solution)/shard_map/all_to_all | solution.py:106
  44.1 4.6 %all-to-all-start.2 = ((bf16[8,384,512]{2,1,0:T(8,128)(2,1)}), bf16[8,384,512]{2,1,0:T(8,128)(2,1)S(1)}, u32[]{:S(2)}, u32[]{:S(2)}) async-start(bf16[8,384,512]{2,1,0:T(8,128)(2,1)} %bitcast.15), calls=%async_computation.2 | async-start | bytes 6291456 | tf_op jit(solution)/shard_map/all_to_all | solution.py:106
  48.7 2.2 fusion.1
  50.9 1.9 pad_maximum_fusion
  52.8 33.4 %all-to-all-done.2 = bf16[8,384,512]{2,1,0:T(8,128)(2,1)S(1)} async-done(((bf16[8,384,512]{2,1,0:T(8,128)(2,1)}), bf16[8,384,512]{2,1,0:T(8,128)(2,1)S(1)}, u32[]{:S(2)}, u32[]{:S(2)}) %all-to-all-start.2) | async-done | bytes 3145760 | tf_op jit(solution)/shard_map/all_to_all | solution.py:106
  86.2 7.6 %all-to-all-start.1 = ((bf16[16,384,256]{2,1,0:T(8,128)(2,1)}), bf16[16,384,256]{2,1,0:T(8,128)(2,1)}, u32[]{:S(2)}, u32[]{:S(2)}) async-start(bf16[16,384,256]{2,1,0:T(8,128)(2,1)} %bitcast.11), calls=%async_computation.1 | async-start | bytes 6291456 | tf_op jit(solution)/shard_map/all_to_all | solution.py:108
  93.8 0.3 fusion
  94.2 1.9 pad_maximum_fusion.1
  96.1 38.4 %all-to-all-done.1.q_ref = bf16[16,384,256]{2,1,0:T(8,128)(2,1)} async-done(((bf16[16,384,256]{2,1,0:T(8,128)(2,1)}), bf16[16,384,256]{2,1,0:T(8,128)(2,1)}, u32[]{:S(2)}, u32[]{:S(2)}) %all-to-all-start.1) | async-done | bytes 3145760 | tf_op jit(solution)/shard_map/all_to_all | solution.py:108
  134.4 0.0 copy-start.1
  134.4 0.0 copy-start.2
  134.4 6.4 %all-to-all-start.3 = ((bf16[16,384,256]{2,1,0:T(8,128)(2,1)}), bf16[16,384,256]{2,1,0:T(8,128)(2,1)S(1)}, u32[]{:S(2)}, u32[]{:S(2)}) async-start(bf16[16,384,256]{2,1,0:T(8,128)(2,1)} %bitcast.3), calls=%async_computation.3 | async-start | bytes 6291456 | tf_op jit(solution)/shard_map/all_to_all | solution.py:108
  140.8 0.0 copy-done.1
  140.8 0.1 reshape.37
  140.9 0.0 copy-done.2
  140.9 0.1 reshape.38
  141.0 0.2 dynamic-slice_reduce_fusion
  141.2 0.6 pad_add_fusion.info
  141.8 34.8 %all-to-all-done.3.g_ref = bf16[16,384,256]{2,1,0:T(8,128)(2,1)S(1)} async-done(((bf16[16,384,256]{2,1,0:T(8,128)(2,1)}), bf16[16,384,256]{2,1,0:T(8,128)(2,1)S(1)}, u32[]{:S(2)}, u32[]{:S(2)}) %all-to-all-start.3) | async-done | bytes 3145760 | tf_op jit(solution)/shard_map/all_to_all | solution.py:108
  176.6 0.0 copy-start
  176.6 1.7 copy-done
  178.2 35.6 %shard_map.85 = (bf16[16,384,256]{2,1,0:T(8,128)(2,1)}, bf16[7168,256]{1,0:T(8,128)(2,1)}, bf16[7168,256]{1,0:T(8,128)(2,1)}) custom-call(s32[3,16]{1,0:T(4,128)} %pad_add_fusion.info, bf16[16,384,256]{2,1,0:T(8,128)(2,1)} %all-to-all-done.1.q_ref, bf16[16,384,256]{2,1,0:T(8,128)(2,1)} %copy-done, bf16[7168,256]{1,0:T(8,128)(2,1)} %k_ref.1, ...), custom_call_target="tpu_custom_call" | custom-call | tf_op jit(solution)/shard_map/pallas_call | solution.py:83
  213.9 41.4 %all_to_all.31 = bf16[16,384,256]{2,1,0:T(8,128)(2,1)S(1)} all-to-all(bf16[16,384,256]{2,1,0:T(8,128)(2,1)} %get-tuple-element.6), channel_id=1, replica_groups=mesh['seq'=16,'text'=8] {'seq'}, dimensions={0} | all-to-all | bytes 6291456 | tf_op jit(solution)/shard_map/all_to_all | solution.py:118
  255.3 2.8 copy.10
  258.0 47.9 %all_to_all.32 = bf16[8,384,512]{1,2,0:T(8,128)(2,1)S(1)} all-to-all(bf16[8,384,512]{1,2,0:T(8,128)(2,1)} %bitcast.13), channel_id=1, replica_groups=mesh['seq'=16,'text'=8] {'text'}, dimensions={0} | all-to-all | bytes 6291456 | tf_op jit(solution)/shard_map/all_to_all | solution.py:120
  306.0 2.9 copy.11
  (1 shorter events, 0.0 us)
Async XLA Ops:
  44.1 42.1 %all-to-all-start.2 = ((bf16[8,384,512]{2,1,0:T(8,128)(2,1)}), bf16[8,384,512]{2,1,0:T(8,128)(2,1)S(1)}, u32[]{:S(2)}, u32[]{:S(2)}) async-start(bf16[8,384,512]{2,1,0:T(8,128)(2,1)} %bitcast.15), calls=%async_computation.2 | async-start | bytes 6291456 | tf_op jit(solution)/shard_map/all_to_all | solution.py:106
  86.2 48.3 %all-to-all-start.1 = ((bf16[16,384,256]{2,1,0:T(8,128)(2,1)}), bf16[16,384,256]{2,1,0:T(8,128)(2,1)}, u32[]{:S(2)}, u32[]{:S(2)}) async-start(bf16[16,384,256]{2,1,0:T(8,128)(2,1)} %bitcast.11), calls=%async_computation.1 | async-start | bytes 6291456 | tf_op jit(solution)/shard_map/all_to_all | solution.py:108
  134.4 6.4 %copy-start.1 = (s32[128]{0:T(128)S(1)}, s32[128]{0:T(128)}, u32[]{:S(2)}) copy-start(s32[128]{0:T(128)} %param.10) | copy-start | bytes 1540
  134.4 6.5 %copy-start.2 = (s32[128]{0:T(128)S(1)}, s32[128]{0:T(128)}, u32[]{:S(2)}) copy-start(s32[128]{0:T(128)} %param.11) | copy-start | bytes 1540
  134.4 42.1 %all-to-all-start.3 = ((bf16[16,384,256]{2,1,0:T(8,128)(2,1)}), bf16[16,384,256]{2,1,0:T(8,128)(2,1)S(1)}, u32[]{:S(2)}, u32[]{:S(2)}) async-start(bf16[16,384,256]{2,1,0:T(8,128)(2,1)} %bitcast.3), calls=%async_computation.3 | async-start | bytes 6291456 | tf_op jit(solution)/shard_map/all_to_all | solution.py:108
  176.6 1.7 copy-start

commit v2 on v1

v2 whole, which is shorter than its diff:
```python
import functools
import math

import jax
import jax.numpy as jnp
from jax import lax
from jax.experimental import pallas as pl
from jax.experimental.pallas import tpu as pltpu
from jax.sharding import PartitionSpec as P


HEAD_DIM = 128
RES = 384
TOK = 448
TB = 224
CASES = (192, 320, 448)
ROW_CASES = (256, 384)
SCALE = 1.0 / math.sqrt(HEAD_DIM)
LOG2E = 1.4426950408889634
NT = (((1,), (1,)), ((), ()))
NN = (((1,), (0,)), ((), ()))
TN = (((0,), (0,)), ((), ()))
BOTH = ("seq", "text")
RING = 4
SHIFTS = (1, 3, 2)
PAIRS = ((0, 1), (3, 2))


def dot(a, b, dims):
    return lax.dot_general(a, b, dims, preferred_element_type=jnp.float32)


def one_protein(q_ref, g_ref, k_ref, v_ref, dq_ref, dk_ref, dv_ref, work, rows, toks, t, r):
    raised_ref, slope_ref, share_ref, scores_ref = work
    q, g = q_ref[:r, :], g_ref[:r, :]
    row_ok = lax.broadcasted_iota(jnp.int32, (1, r), 1) < rows
    size = t if t <= TB else t // 2
    blocks = [slice(start, start + size) for start in range(0, t, size)]
    total = jnp.zeros((1, r), jnp.float32)
    weighed = jnp.zeros((1, r), jnp.float32)
    for here in blocks:
        token_ok = lax.broadcasted_iota(jnp.int32, (size, r), 0) + here.start < toks
        raised = jnp.exp2(dot(k_ref[here, :], q, NT) * (SCALE * LOG2E))
        raised = jnp.where(token_ok, raised, 0.0)
        slope = dot(v_ref[here, :], g, NT)
        raised_ref[here, :r] = raised
        slope_ref[here, :r] = slope
        total += jnp.sum(raised, axis=0, keepdims=True)
        weighed += jnp.sum(raised * slope, axis=0, keepdims=True)
    inverse = jnp.where(row_ok, 1.0 / total, 0.0)
    scaled, delta = inverse * SCALE, weighed * inverse
    for here in blocks:
        raised = raised_ref[here, :r]
        share_ref[here, :r] = (raised * inverse).astype(jnp.bfloat16)
        scores = (raised * scaled) * (slope_ref[here, :r] - delta)
        scores_ref[here, :r] = scores.astype(jnp.bfloat16)
    dv_ref[:t, :] = dot(share_ref[:t, :r], g, NN).astype(jnp.bfloat16)
    dk_ref[:t, :] = dot(scores_ref[:t, :r], q, NN).astype(jnp.bfloat16)
    dq_ref[:r, :] = dot(k_ref[:t, :], scores_ref[:t, :r], TN).T.astype(jnp.bfloat16)
    if t < TOK:
        dk_ref[t:, :] = jnp.zeros((TOK - t, HEAD_DIM), jnp.bfloat16)
        dv_ref[t:, :] = jnp.zeros((TOK - t, HEAD_DIM), jnp.bfloat16)
    if r < RES:
        dq_ref[r:, :] = jnp.zeros((RES - r, HEAD_DIM), jnp.bfloat16)


def attention_kernel(head, own, parts, info, *refs):
    q_refs, g_refs, key_ref, value_ref = refs[:2], refs[2:4], refs[4], refs[5]
    dq_outs, dk_out, dv_out = refs[-16:-14], refs[-14], refs[-13]
    field_q, field_g, keys, values, dq, dk, dv, raised, slope, share, scores = refs[-12:-1]
    copies = refs[-1]
    work = (raised, slope, share, scores)
    count = field_q.shape[0]
    cols = slice(head * HEAD_DIM, (head + 1) * HEAD_DIM)

    def source(ref, chunk, i, part):
        return ref.at[info[3, 0], i, part] if own and chunk == 0 else ref.at[i]

    def fetch(chunk, within, i):
        here = pl.ds(pl.multiple_of(info[0, i] * TOK, TOK), TOK)
        return (
            pltpu.make_async_copy(
                source(q_refs[chunk], chunk, within, parts[0]), field_q.at[i], copies.at[0, i]
            ),
            pltpu.make_async_copy(
                source(g_refs[chunk], chunk, within, parts[1]), field_g.at[i], copies.at[1, i]
            ),
            pltpu.make_async_copy(key_ref.at[here, cols], keys.at[i], copies.at[2, i]),
            pltpu.make_async_copy(value_ref.at[here, cols], values.at[i], copies.at[3, i]),
        )

    def store(chunk, within, i):
        here = pl.ds(pl.multiple_of(info[0, i] * TOK, TOK), TOK)
        out = dq_outs[chunk]
        target = out.at[info[3, 0], within] if own and chunk == 0 else out.at[within]
        return (
            pltpu.make_async_copy(dq.at[i], target, copies.at[4, i]),
            pltpu.make_async_copy(dk.at[i], dk_out.at[here, cols], copies.at[5, i]),
            pltpu.make_async_copy(dv.at[i], dv_out.at[here, cols], copies.at[6, i]),
        )

    for i in range(count):
        for copy in fetch(i // RING, i % RING, i):
            copy.start()

    def both(i, carry):
        chunk, within = lax.div(i, RING), lax.rem(i, RING)
        rows, toks = info[1, i], info[2, i]
        for copy in fetch(1, within, i):
            copy.wait()
        low_t = 0
        for t in CASES:
            low_r = 0
            for r in ROW_CASES:
                fits = (toks > low_t) & (toks <= t) & (rows > low_r) & (rows <= r)
                pl.when(fits)(
                    lambda t=t, r=r: one_protein(
                        field_q.at[i], field_g.at[i], keys.at[i], values.at[i], dq.at[i], dk.at[i],
                        dv.at[i], work, rows, toks, t, r,
                    )
                )
                low_r = r
            low_t = t
        for which in range(2):

            @pl.when(chunk == which)
            def _(which=which):
                for copy in store(which, within, i):
                    copy.start()

        return carry

    lax.fori_loop(0, count, both, 0)
    for i in range(count):
        for copy in store(i // RING, i % RING, i):
            copy.wait()


def attention_backward(info, head, own, parts, q_fields, g_fields, keys, values, grads_so_far):
    any_spec = pl.BlockSpec(memory_space=pl.ANY)
    hbm_spec = pl.BlockSpec(memory_space=pltpu.HBM)
    chunk = (RING, RES, HEAD_DIM)
    held = list(grads_so_far)
    count = 2 * RING
    tokens, residues = (count, TOK, HEAD_DIM), (count, RES, HEAD_DIM)
    bf16 = jnp.bfloat16
    return pl.pallas_call(
        functools.partial(attention_kernel, head, own, parts),
        compiler_params=pltpu.CompilerParams(vmem_limit_bytes=50 << 20),
        grid_spec=pltpu.PrefetchScalarGridSpec(
            num_scalar_prefetch=1,
            grid=(1,),
            in_specs=[any_spec] * 4 + [hbm_spec] * (2 + len(held)),
            out_specs=[any_spec] * 2 + [hbm_spec] * 2,
            scratch_shapes=[pltpu.VMEM(residues, bf16)] * 2
            + [pltpu.VMEM(tokens, bf16)] * 2
            + [pltpu.VMEM(residues, bf16)]
            + [pltpu.VMEM(tokens, bf16)] * 2
            + [pltpu.VMEM((TOK, RES), jnp.float32)] * 2
            + [pltpu.VMEM((TOK, RES), bf16)] * 2
            + [pltpu.SemaphoreType.DMA((7, count))],
        ),
        out_shape=[
            jax.ShapeDtypeStruct(((RING,) if own else ()) + chunk, bf16),
            jax.ShapeDtypeStruct(chunk, bf16),
            jax.ShapeDtypeStruct(keys.shape, bf16),
            jax.ShapeDtypeStruct(values.shape, bf16),
        ],
        input_output_aliases={7: 2, 8: 3} if held else {},
        cost_estimate=pl.CostEstimate(
            flops=count * 10 * RES * TOK * HEAD_DIM,
            bytes_accessed=count * 14 * RES * HEAD_DIM,
            transcendentals=count * RES * TOK,
        ),
    )(info, *q_fields, *g_fields, keys, values, *held)


def pack_kernel(heads, core, *refs):
    fields, (joined_ref, send_ref, held, sems_in, sems_out) = refs[:-5], refs[-5:]
    c = core[0]
    steps = [(w, y) for w in (1, 0) for y in range(RING)]
    ins = {}
    for n, (w, y) in enumerate(steps):
        t = 2 * y + (c if w == 0 else 1 - c)
        for f, ref in enumerate(fields):
            for b in range(2):
                at = (2 * b + heads[f]) * HEAD_DIM
                ins[w, y, f, b] = pltpu.make_async_copy(
                    ref.at[t, :, at : at + HEAD_DIM], held.at[w, y, b, f], sems_in.at[n, f, b]
                )
                ins[w, y, f, b].start()
    outs = []
    for n, (w, y) in enumerate(steps):
        for f in range(len(fields)):
            for b in range(2):
                ins[w, y, f, b].wait()
        outs.append(
            pltpu.make_async_copy(
                held.at[w, y], send_ref.at[y] if w else joined_ref.at[y, 0], sems_out.at[n]
            )
        )
        outs[-1].start()
    for out in outs:
        out.wait()


def pack(core, fields, heads):
    any_spec = pl.BlockSpec(memory_space=pl.ANY)
    hbm_spec = pl.BlockSpec(memory_space=pltpu.HBM)
    count = len(fields)
    block = (2, count, RES, HEAD_DIM)
    return pl.pallas_call(
        functools.partial(pack_kernel, heads),
        compiler_params=pltpu.CompilerParams(vmem_limit_bytes=58 << 20),
        grid_spec=pltpu.PrefetchScalarGridSpec(
            num_scalar_prefetch=1,
            grid=(1,),
            in_specs=[hbm_spec] * count,
            out_specs=[any_spec] * 2,
            scratch_shapes=[
                pltpu.VMEM((2, RING) + block, jnp.bfloat16),
                pltpu.SemaphoreType.DMA((2 * RING, count, 2)),
                pltpu.SemaphoreType.DMA((2 * RING,)),
            ],
        ),
        out_shape=[
            jax.ShapeDtypeStruct((RING, 2) + block, jnp.bfloat16),
            jax.ShapeDtypeStruct((RING,) + block, jnp.bfloat16),
        ],
    )(core, *[field.reshape(8, RES, -1) for field in fields])


def unpack_kernel(head, core, home_ref, got_ref, *rest):
    out_ref, held, sems_in, sems_out = rest[-4:]
    c = core[0]
    steps = [(w, y) for w in range(2) for y in range(RING)]
    ins, outs = [], []
    for n, (w, y) in enumerate(steps):
        ins.append(
            pltpu.make_async_copy(
                home_ref.at[y, 0] if w == 0 else got_ref.at[y], held.at[w, y], sems_in.at[n]
            )
        )
        ins[-1].start()
    for n, (w, y) in enumerate(steps):
        ins[n].wait()
        t = 2 * y + (c if w == 0 else 1 - c)
        for b in range(2):
            outs.append(
                pltpu.make_async_copy(
                    held.at[w, y, b],
                    out_ref.at[t, :, (2 * b + head) * HEAD_DIM : (2 * b + head + 1) * HEAD_DIM],
                    sems_out.at[n, b],
                )
            )
            outs[-1].start()
    for out in outs:
        out.wait()


def unpack(core, head, home, got, shape, held):
    any_spec = pl.BlockSpec(memory_space=pl.ANY)
    hbm_spec = pl.BlockSpec(memory_space=pltpu.HBM)
    return pl.pallas_call(
        functools.partial(unpack_kernel, head),
        compiler_params=pltpu.CompilerParams(vmem_limit_bytes=58 << 20),
        grid_spec=pltpu.PrefetchScalarGridSpec(
            num_scalar_prefetch=1,
            grid=(1,),
            in_specs=[any_spec] * 2 + [hbm_spec] * len(held),
            out_specs=hbm_spec,
            scratch_shapes=[
                pltpu.VMEM((2, RING, 2, RES, HEAD_DIM), jnp.bfloat16),
                pltpu.SemaphoreType.DMA((2 * RING,)),
                pltpu.SemaphoreType.DMA((2 * RING, 2)),
            ],
        ),
        out_shape=jax.ShapeDtypeStruct((8, RES, shape[1]), jnp.bfloat16),
        input_output_aliases={3: 0} if held else {},
    )(core, home, got, *held)


def device(x, y, z, core):
    return (x % RING * RING + z % RING) * 8 + y % RING * 2 + core


COORDS = [(x, y, z, c) for x in range(RING) for z in range(RING) for y in range(RING) for c in range(2)]
PLANES = [
    [device(x, y, zeta ^ (2 * c), c) for y in range(RING) for zeta in range(RING)]
    for x in range(RING)
    for c in range(2)
]
SWAP = [(device(*p), device(p[0], p[1], p[2], 1 - p[3])) for p in COORDS]


def shift(by):
    return [(device(*p), device(p[0] + by, *p[1:])) for p in COORDS]


def plane_exchange(field):
    return lax.all_to_all(field, BOTH, 0, 0, axis_index_groups=PLANES, tiled=True)


def body(queries, keys, values, grad_out, res_len, tok_len):
    text = lax.axis_index("text")
    seq = lax.axis_index("seq")
    c, x = text % 2, seq // RING
    core = c.reshape(1).astype(jnp.int32)

    def lens(field):
        mine = lax.dynamic_index_in_dim(field.reshape(RING, RING, 8), text, 2, keepdims=False)
        turned = jnp.concatenate([mine[:, 2:], mine[:, :2]], axis=1)
        return jnp.where(c == 0, mine, turned)

    rows, toks = lens(res_len), lens(tok_len)
    zeta = jnp.arange(RING, dtype=jnp.int32) ^ (2 * c)

    def info_of(shifts):
        columns = []
        for s in shifts:
            xs = (x - s) % RING
            pick = lambda f: lax.dynamic_index_in_dim(f, xs, 0, keepdims=False)
            columns.append(
                jnp.stack([xs * RING + zeta, pick(rows), pick(toks), jnp.full_like(zeta, x)])
            )
        return jnp.concatenate(columns, axis=1).astype(jnp.int32)

    infos = {pair: info_of(pair) for pair in PAIRS}

    def into(fields, heads):
        joined, send = pack(core, fields, heads)
        got = lax.ppermute(send, BOTH, SWAP)
        joined = lax.dynamic_update_slice(joined, got[:, None], (0, 1, 0, 0, 0, 0))
        field = plane_exchange(joined.reshape(16, len(fields), RES, HEAD_DIM))
        return field.reshape(RING, RING, len(fields), RES, HEAD_DIM)

    landed = [
        into((queries,), (0,)),
        into((grad_out,), (0,)),
        into((queries,), (1,)),
        into((grad_out,), (1,)),
    ]

    def spread(field):
        chunks = {}
        for s in SHIFTS:
            piece = lax.dynamic_slice(
                field, ((x + s) % RING, 0, 0, 0, 0), (1, RING, 1, RES, HEAD_DIM)
            ).reshape(RING, RES, HEAD_DIM)
            chunks[s] = lax.ppermute(piece, BOTH, shift(s))
        return chunks

    q_chunks = [spread(landed[0]), spread(landed[2])]
    g_chunks = [spread(landed[1]), spread(landed[3])]
    sources = [((landed[0], 0), (landed[1], 0)), ((landed[2], 0), (landed[3], 0))]
    grads = ()
    query_grads = ()
    for h in range(2):
        (own_q, part_q), (own_g, part_g) = sources[h]
        back = None
        for pair in PAIRS:
            q_fields = [own_q if s == 0 else q_chunks[h][s] for s in pair]
            g_fields = [own_g if s == 0 else g_chunks[h][s] for s in pair]
            *dqs, dk, dv = attention_backward(
                infos[pair], h, pair[0] == 0, (part_q, part_g), q_fields, g_fields, keys, values, grads
            )
            grads = (dk, dv)
            for s, dq in zip(pair, dqs):
                if s == 0:
                    back = dq
                    continue
                dq = lax.ppermute(dq, BOTH, shift(-s))
                back = lax.dynamic_update_index_in_dim(back, dq, (x + s) % RING, 0)
        home = plane_exchange(back.reshape(16, RES, HEAD_DIM))
        home = home.reshape(RING, 2, 2, RES, HEAD_DIM)
        got = lax.ppermute(home[:, 1], BOTH, SWAP)
        query_grads = (unpack(core, h, home, got, queries.shape, query_grads),)
    return (query_grads[0].reshape(queries.shape), *grads)


def solution(mesh):
    return jax.shard_map(
        body,
        mesh=mesh,
        in_specs=(P("seq", "text"), P("text", "seq"), P("text", "seq"), P("seq", "text"), P(), P()),
        out_specs=(P("seq", "text"), P("text", "seq"), P("text", "seq")),
        check_vma=False,
    )
```

time: 311 us -> 293 us (0.942)
  blocking collectives: 133 us -> 0 us
  starting transfers between devices: 18.6 us -> 69 us
  waiting for transfers between devices: 107 us -> 142 us
  Pallas kernels: 35.6 us -> 57.1 us
  local copies, waits for them, and re-layouts: 10.1 us -> 22.3 us
  other arithmetic: 4.38 us -> 0.24 us
    all_to_all x3 -> x0, blocking collectives: 133 us -> none  [the longest x1 47.9 us: body(): lax.all_to_all(back, 'text', 0, 0, tiled=True).reshape(queries.shape)]
    ppermute x0 -> x24, waiting for transfers between devices: none -> 85 us  [the longest x6 43.5 us: body(): dq = lax.ppermute(dq, BOTH, shift(-s))]
    all_to_all x3 -> x6, waiting for transfers between devices: 107 us -> 57 us  [plane_exchange(): lax.all_to_all(field, BOTH, 0, 0, axis_index_groups=PLANES, tiled=True)]
    ppermute x0 -> x24, starting transfers between devices: none -> 29.3 us  [the longest x12 14.8 us: spread(): chunks[s] = lax.ppermute(piece, BOTH, shift(s))]
    pallas_call x1 -> x10, Pallas kernels: 35.6 us -> 57.1 us  [the longest x4 42.9 us: attention_backward(): pl.pallas_call(functools.partial(attention_kernel, head, own, parts), com...]
    all_to_all x3 -> x6, starting transfers between devices: 18.6 us -> 39.7 us  [plane_exchange(): lax.all_to_all(field, BOTH, 0, 0, axis_index_groups=PLANES, tiled=True)]
    dynamic_update_slice x0 -> x10, local copies, waits for them, and re-layouts: none -> 11.9 us  [the longest x6 6.72 us: body(): back = lax.dynamic_update_index_in_dim(back, dq, (x + s) % RING, 0)]
    reshape x3 -> x6, local copies, waits for them, and re-layouts: 2.92 us -> 6.68 us  [the longest x4 6.5 us: spread(): piece = lax.dynamic_slice(field, ((x + s) % RING, 0, 0, 0, 0), (1, RING,...]
  transfers between devices with their start and end apart: 3 -> 30, of which waited for: 3 -> 18; matrix products, arithmetic and copies ran while one was open for 2% -> 7% of each run, Pallas kernels for 0% -> 18%
where the time goes in v2:
time: 293 us; the launch traced here: 292 us
  waiting for transfers between devices  142 us (48%)
  starting transfers between devices  69 us (24%)
  Pallas kernels  57.1 us (19%)
  local copies, waits for them, and re-layouts  22.3 us (8%)
    all_to_all x6, waiting for transfers between devices, plane_exchange(): lax.all_to_all(field, BOTH, 0, 0, axis_index_groups=PLANES, tiled=True)  57 us
    ppermute x6, waiting for transfers between devices, body(): dq = lax.ppermute(dq, BOTH, shift(-s))  43.5 us
    pallas_call x4, Pallas kernels, attention_backward(): pl.pallas_call(functools.partial(attention_kernel, head, own, parts), com...  42.9 us
    all_to_all x6, starting transfers between devices, plane_exchange(): lax.all_to_all(field, BOTH, 0, 0, axis_index_groups=PLANES, tiled=True)  39.7 us
    ppermute x12, waiting for transfers between devices, spread(): chunks[s] = lax.ppermute(piece, BOTH, shift(s))  32.7 us
    ppermute x12, starting transfers between devices, spread(): chunks[s] = lax.ppermute(piece, BOTH, shift(s))  14.8 us
    pallas_call x4, Pallas kernels, pack(): pl.pallas_call(functools.partial(pack_kernel, heads), compiler_params=plt...  9.55 us
    ppermute x4, waiting for transfers between devices, into(): got = lax.ppermute(send, BOTH, SWAP)  8.8 us
  transfers between devices with their start and end apart: 30, of which 18 were waited for; matrix products, arithmetic and copies ran while one was open for 7% of the time, Pallas kernels for 18%

profile of v2, /device:TPU:1, one launch (start us, length us, event | category | flops | bytes accessed | tf_op | source)
XLA Modules:
  0.0 291.9 jit_solution(586586047382736534)
XLA Ops:
  0.6 2.4 shard_map.87
  7.6 9.0 %all-to-all-start.2 = ((bf16[16,1,384,128]{3,2,1,0:T(8,128)(2,1)}), bf16[16,1,384,128]{3,2,1,0:T(8,128)(2,1)S(1)}, u32[]{:S(2)}, u32[]{:S(2)}) async-start(bf16[16,1,384,128]{3,2,1,0:T(8,128)(2,1)} %bitcast.96), calls=%async_computation.2 | async-start | bytes 3145728 | tf_op jit(solution)/shard_map/all_to_all | solution.py:301
  16.6 2.4 shard_map.85
  19.1 2.5 collective-permute-done
  22.6 14.3 %all-to-all-done.2 = bf16[16,1,384,128]{3,2,1,0:T(8,128)(2,1)S(1)} async-done(((bf16[16,1,384,128]{3,2,1,0:T(8,128)(2,1)}), bf16[16,1,384,128]{3,2,1,0:T(8,128)(2,1)S(1)}, u32[]{:S(2)}, u32[]{:S(2)}) %all-to-all-start.2) | async-done | bytes 1572896 | tf_op jit(solution)/shard_map/all_to_all | solution.py:301
  36.9 6.3 %all-to-all-start = ((bf16[16,1,384,128]{3,2,1,0:T(8,128)(2,1)}), bf16[16,1,384,128]{3,2,1,0:T(8,128)(2,1)S(1)}, u32[]{:S(2)}, u32[]{:S(2)}) async-start(bf16[16,1,384,128]{3,2,1,0:T(8,128)(2,1)} %bitcast.97), calls=%async_computation | async-start | bytes 3145728 | tf_op jit(solution)/shard_map/all_to_all | solution.py:301
  43.2 2.4 shard_map.88
  45.7 2.5 collective-permute-done.7
  49.2 13.6 %all-to-all-done = bf16[16,1,384,128]{3,2,1,0:T(8,128)(2,1)S(1)} async-done(((bf16[16,1,384,128]{3,2,1,0:T(8,128)(2,1)}), bf16[16,1,384,128]{3,2,1,0:T(8,128)(2,1)S(1)}, u32[]{:S(2)}, u32[]{:S(2)}) %all-to-all-start) | async-done | bytes 1572896 | tf_op jit(solution)/shard_map/all_to_all | solution.py:301
  62.8 7.6 %all-to-all-start.3 = ((bf16[16,1,384,128]{3,2,1,0:T(8,128)(2,1)}), bf16[16,1,384,128]{3,2,1,0:T(8,128)(2,1)}, u32[]{:S(2)}, u32[]{:S(2)}) async-start(bf16[16,1,384,128]{3,2,1,0:T(8,128)(2,1)} %bitcast.98), calls=%async_computation.3 | async-start | bytes 3145728 | tf_op jit(solution)/shard_map/all_to_all | solution.py:301
  70.5 2.4 shard_map.86
  77.8 12.3 %all-to-all-done.3 = bf16[16,1,384,128]{3,2,1,0:T(8,128)(2,1)} async-done(((bf16[16,1,384,128]{3,2,1,0:T(8,128)(2,1)}), bf16[16,1,384,128]{3,2,1,0:T(8,128)(2,1)}, u32[]{:S(2)}, u32[]{:S(2)}) %all-to-all-start.3) | async-done | bytes 1572896 | tf_op jit(solution)/shard_map/all_to_all | solution.py:301
  90.1 7.4 %all-to-all-start.1 = ((bf16[16,1,384,128]{3,2,1,0:T(8,128)(2,1)}), bf16[16,1,384,128]{3,2,1,0:T(8,128)(2,1)}, u32[]{:S(2)}, u32[]{:S(2)}) async-start(bf16[16,1,384,128]{3,2,1,0:T(8,128)(2,1)} %bitcast.95), calls=%async_computation.1 | async-start | bytes 3145728 | tf_op jit(solution)/shard_map/all_to_all | solution.py:301
  107.3 3.3 %collective-permute-done.10.refs_1_ = bf16[4,384,128]{2,1,0:T(8,128)(2,1)S(1)} collective-permute-done((bf16[4,384,128]{2,1,0:T(8,128)(2,1)}, bf16[4,384,128]{2,1,0:T(8,128)(2,1)S(1)}, u32[]{:S(2)}, u32[]{:S(2)}) %collective-permute-start.10) | collective-permute-done | bytes 393248 | tf_op jit(solution)/shard_map/ppermute | solution.py:350
  112.0 6.9 %collective-permute-done.11.refs_3_ = bf16[4,384,128]{2,1,0:T(8,128)(2,1)S(1)} collective-permute-done((bf16[4,384,128]{2,1,0:T(8,128)(2,1)S(1)}, bf16[4,384,128]{2,1,0:T(8,128)(2,1)S(1)}, u32[]{:S(2)}, u32[]{:S(2)}) %collective-permute-start.11) | collective-permute-done | bytes 393248 | tf_op jit(solution)/shard_map/ppermute | solution.py:350
  118.9 10.5 %shard_map.89 = (bf16[4,4,384,128]{3,2,1,0:T(8,128)(2,1)}, bf16[4,384,128]{2,1,0:T(8,128)(2,1)S(1)}, bf16[7168,256]{1,0:T(8,128)(2,1)}, bf16[7168,256]{1,0:T(8,128)(2,1)}) custom-call(s32[4,8]{1,0:T(4,128)S(1)} %fusion.info, bf16[4,4,1,384,128]{4,3,2,1,0:T(8,128)(2,1)} %bitcast.92, bf16[4,384,128]{2,1,0:T(8,128)(2,1)S(1)} %collective-permute-done.10.refs_1_, ...), custom_call_target="tpu_custom_call" | custom-call | flops 1761607680 | bytes 5505024 | tf_op jit(solution)/shard_map/pallas_call | solution.py:147
  130.2 6.6 %collective-permute-done.9.refs_3_ = bf16[4,384,128]{2,1,0:T(8,128)(2,1)S(1)} collective-permute-done((bf16[4,384,128]{2,1,0:T(8,128)(2,1)}, bf16[4,384,128]{2,1,0:T(8,128)(2,1)S(1)}, u32[]{:S(2)}, u32[]{:S(2)}) %collective-permute-start.9) | collective-permute-done | bytes 393248 | tf_op jit(solution)/shard_map/ppermute | solution.py:350
  136.8 2.9 collective-permute-done.8.refs_2_
  139.6 10.9 %shard_map.90 = (bf16[4,384,128]{2,1,0:T(8,128)(2,1)S(1)}, bf16[4,384,128]{2,1,0:T(8,128)(2,1)S(1)}, bf16[7168,256]{1,0:T(8,128)(2,1)}, bf16[7168,256]{1,0:T(8,128)(2,1)}) custom-call(s32[4,8]{1,0:T(4,128)S(1)} %fusion.1.info, bf16[4,384,128]{2,1,0:T(8,128)(2,1)S(1)} %collective-permute-done.5.refs_0_, ...), custom_call_target="tpu_custom_call", output_to_operand_aliasing={{2}: (7, {}), {3}: (8, {})} | custom-call | flops 1761607680 | bytes 5505024 | tf_op jit(solution)/shard_map/pallas_call | solution.py:147
  164.8 25.8 %collective-permute-done.22 = bf16[4,384,128]{2,1,0:T(8,128)(2,1)S(1)} collective-permute-done((bf16[4,384,128]{2,1,0:T(8,128)(2,1)S(1)}, bf16[4,384,128]{2,1,0:T(8,128)(2,1)S(1)}, u32[]{:S(2)}, u32[]{:S(2)}) %collective-permute-start.22) | collective-permute-done | bytes 393248 | tf_op jit(solution)/shard_map/ppermute | solution.py:372
  191.3 5.1 %all-to-all-start.5 = ((bf16[16,384,128]{2,1,0:T(8,128)(2,1)}), bf16[16,384,128]{2,1,0:T(8,128)(2,1)S(1)}, u32[]{:S(2)}, u32[]{:S(2)}) async-start(bf16[16,384,128]{2,1,0:T(8,128)(2,1)} %bitcast.44), calls=%async_computation.5 | async-start | bytes 3145728 | tf_op jit(solution)/shard_map/all_to_all | solution.py:301
  196.6 2.9 collective-permute-start.16
  200.4 10.5 %shard_map.91 = (bf16[4,4,384,128]{3,2,1,0:T(8,128)(2,1)}, bf16[4,384,128]{2,1,0:T(8,128)(2,1)S(1)}, bf16[7168,256]{1,0:T(8,128)(2,1)}, bf16[7168,256]{1,0:T(8,128)(2,1)}) custom-call(s32[4,8]{1,0:T(4,128)S(1)} %fusion.info, bf16[4,4,1,384,128]{4,3,2,1,0:T(8,128)(2,1)} %bitcast.90, ...), custom_call_target="tpu_custom_call", output_to_operand_aliasing={{2}: (7, {}), {3}: (8, {})} | custom-call | flops 1761607680 | bytes 5505024 | tf_op jit(solution)/shard_map/pallas_call | solution.py:147
  211.3 6.2 %collective-permute-done.16.refs_3_ = bf16[4,384,128]{2,1,0:T(8,128)(2,1)S(1)} collective-permute-done((bf16[4,384,128]{2,1,0:T(8,128)(2,1)}, bf16[4,384,128]{2,1,0:T(8,128)(2,1)S(1)}, u32[]{:S(2)}, u32[]{:S(2)}) %collective-permute-start.16) | collective-permute-done | bytes 393248 | tf_op jit(solution)/shard_map/ppermute | solution.py:350
  217.5 6.8 %collective-permute-done.15.refs_2_ = bf16[4,384,128]{2,1,0:T(8,128)(2,1)S(1)} collective-permute-done((bf16[4,384,128]{2,1,0:T(8,128)(2,1)S(1)}, bf16[4,384,128]{2,1,0:T(8,128)(2,1)S(1)}, u32[]{:S(2)}, u32[]{:S(2)}) %collective-permute-start.15) | collective-permute-done | bytes 393248 | tf_op jit(solution)/shard_map/ppermute | solution.py:350
  224.3 10.9 %shard_map.92 = (bf16[4,384,128]{2,1,0:T(8,128)(2,1)S(1)}, bf16[4,384,128]{2,1,0:T(8,128)(2,1)S(1)}, bf16[7168,256]{1,0:T(8,128)(2,1)}, bf16[7168,256]{1,0:T(8,128)(2,1)}) custom-call(s32[4,8]{1,0:T(4,128)S(1)} %fusion.1.info, bf16[4,384,128]{2,1,0:T(8,128)(2,1)S(1)} %collective-permute-done.13.refs_0_, ...), custom_call_target="tpu_custom_call", output_to_operand_aliasing={{2}: (7, {}), {3}: (8, {})} | custom-call | flops 1761607680 | bytes 5505024 | tf_op jit(solution)/shard_map/pallas_call | solution.py:147
  236.9 2.5 collective-permute-start.18
  240.2 6.2 %collective-permute-done.17 = bf16[4,384,128]{2,1,0:T(8,128)(2,1)S(1)} collective-permute-done((bf16[4,384,128]{2,1,0:T(8,128)(2,1)S(1)}, bf16[4,384,128]{2,1,0:T(8,128)(2,1)S(1)}, u32[]{:S(2)}, u32[]{:S(2)}) %collective-permute-start.17) | collective-permute-done | bytes 393248 | tf_op jit(solution)/shard_map/ppermute | solution.py:372
  247.2 9.9 %collective-permute-done.18 = bf16[4,384,128]{2,1,0:T(8,128)(2,1)S(1)} collective-permute-done((bf16[4,384,128]{2,1,0:T(8,128)(2,1)S(1)}, bf16[4,384,128]{2,1,0:T(8,128)(2,1)S(1)}, u32[]{:S(2)}, u32[]{:S(2)}) %collective-permute-start.18) | collective-permute-done | bytes 393248 | tf_op jit(solution)/shard_map/ppermute | solution.py:372
  257.9 4.3 %all-to-all-start.4 = ((bf16[16,384,128]{2,1,0:T(8,128)(2,1)}), bf16[16,384,128]{2,1,0:T(8,128)(2,1)}, u32[]{:S(2)}, u32[]{:S(2)}) async-start(bf16[16,384,128]{2,1,0:T(8,128)(2,1)} %bitcast.38), calls=%async_computation.4 | async-start | bytes 3145728 | tf_op jit(solution)/shard_map/all_to_all | solution.py:301
  263.2 16.8 %all-to-all-done.4 = bf16[16,384,128]{2,1,0:T(8,128)(2,1)} async-done(((bf16[16,384,128]{2,1,0:T(8,128)(2,1)}), bf16[16,384,128]{2,1,0:T(8,128)(2,1)}, u32[]{:S(2)}, u32[]{:S(2)}) %all-to-all-start.4) | async-done | bytes 1572896 | tf_op jit(solution)/shard_map/all_to_all | solution.py:301
  281.2 4.0 %collective-permute-start.19 = (bf16[4,2,384,128]{3,2,1,0:T(8,128)(2,1)S(1)}, bf16[4,2,384,128]{3,2,1,0:T(8,128)(2,1)S(1)}, u32[]{:S(2)}, u32[]{:S(2)}) collective-permute-start(bf16[4,2,384,128]{3,2,1,0:T(8,128)(2,1)S(1)} %slice_bitcast_fusion.1), channel_id=1, source_target_pairs={{0,1},{1,0},{2,3},{3,2},{4,5},{5,4},{6,7},{7,6},{8,9},{9,8},{10,11... | collective-permute-start | bytes 2359304 | tf_op jit(solution)/shard_map/ppermute | solution.py:376
  (86 shorter events, 52.6 us)
Async XLA Ops:
  3.0 3.6 %collective-permute-start.4 = (bf16[4,2,1,384,128]{4,3,2,1,0:T(8,128)(2,1)}, bf16[4,2,1,384,128]{4,3,2,1,0:T(8,128)(2,1)S(1)}, u32[]{:S(2)}, u32[]{:S(2)}) collective-permute-start(bf16[4,2,1,384,128]{4,3,2,1,0:T(8,128)(2,1)} %get-tuple-element.32), channel_id=1, source_target_pairs={{0,1},{1,0},{2,3},{3,2},{4,5},{5,4},{6,7},{7,6},{8,9},{9,8},{10,11... | collective-permute-start | bytes 2359304 | tf_op jit(solution)/shard_map/ppermute | solution.py:332
  7.6 29.3 %all-to-all-start.2 = ((bf16[16,1,384,128]{3,2,1,0:T(8,128)(2,1)}), bf16[16,1,384,128]{3,2,1,0:T(8,128)(2,1)S(1)}, u32[]{:S(2)}, u32[]{:S(2)}) async-start(bf16[16,1,384,128]{3,2,1,0:T(8,128)(2,1)} %bitcast.96), calls=%async_computation.2 | async-start | bytes 3145728 | tf_op jit(solution)/shard_map/all_to_all | solution.py:301
  19.0 2.6 collective-permute-start
  36.9 60.8 %copy-start.1 = (bf16[16,1,384,128]{3,2,1,0:T(8,128)(2,1)}, bf16[16,1,384,128]{3,2,1,0:T(8,128)(2,1)S(1)}, u32[]{:S(2)}) copy-start(bf16[16,1,384,128]{3,2,1,0:T(8,128)(2,1)S(1)} %all-to-all-done.2) | copy-start | bytes 4718596
  36.9 25.9 %all-to-all-start = ((bf16[16,1,384,128]{3,2,1,0:T(8,128)(2,1)}), bf16[16,1,384,128]{3,2,1,0:T(8,128)(2,1)S(1)}, u32[]{:S(2)}, u32[]{:S(2)}) async-start(bf16[16,1,384,128]{3,2,1,0:T(8,128)(2,1)} %bitcast.97), calls=%async_computation | async-start | bytes 3145728 | tf_op jit(solution)/shard_map/all_to_all | solution.py:301
  45.6 2.6 collective-permute-start.7
  62.8 89.6 %copy-start = (bf16[16,1,384,128]{3,2,1,0:T(8,128)(2,1)}, bf16[16,1,384,128]{3,2,1,0:T(8,128)(2,1)S(1)}, u32[]{:S(2)}) copy-start(bf16[16,1,384,128]{3,2,1,0:T(8,128)(2,1)S(1)} %all-to-all-done) | copy-start | bytes 4718596
  62.8 27.3 %all-to-all-start.3 = ((bf16[16,1,384,128]{3,2,1,0:T(8,128)(2,1)}), bf16[16,1,384,128]{3,2,1,0:T(8,128)(2,1)}, u32[]{:S(2)}, u32[]{:S(2)}) async-start(bf16[16,1,384,128]{3,2,1,0:T(8,128)(2,1)} %bitcast.98), calls=%async_computation.3 | async-start | bytes 3145728 | tf_op jit(solution)/shard_map/all_to_all | solution.py:301
  72.9 2.7 collective-permute-start.2
  90.1 64.6 %all-to-all-start.1 = ((bf16[16,1,384,128]{3,2,1,0:T(8,128)(2,1)}), bf16[16,1,384,128]{3,2,1,0:T(8,128)(2,1)}, u32[]{:S(2)}, u32[]{:S(2)}) async-start(bf16[16,1,384,128]{3,2,1,0:T(8,128)(2,1)} %bitcast.95), calls=%async_computation.1 | async-start | bytes 3145728 | tf_op jit(solution)/shard_map/all_to_all | solution.py:301
  98.7 11.9 %collective-permute-start.10 = (bf16[4,384,128]{2,1,0:T(8,128)(2,1)}, bf16[4,384,128]{2,1,0:T(8,128)(2,1)S(1)}, u32[]{:S(2)}, u32[]{:S(2)}) collective-permute-start(bf16[4,384,128]{2,1,0:T(8,128)(2,1)} %get-tuple-element.60), channel_id=1, source_target_pairs={{0,32},{1,33},{2,34},{3,35},{4,36},{5,37},{6,38},{7,39},{8,40},{9,... | collective-permute-start | bytes 1179656 | tf_op jit(solution)/shard_map/ppermute | solution.py:350
  102.2 16.7 %collective-permute-start.11 = (bf16[4,384,128]{2,1,0:T(8,128)(2,1)S(1)}, bf16[4,384,128]{2,1,0:T(8,128)(2,1)S(1)}, u32[]{:S(2)}, u32[]{:S(2)}) collective-permute-start(bf16[4,384,128]{2,1,0:T(8,128)(2,1)S(1)} %get-tuple-element.57), channel_id=1, source_target_pairs={{0,32},{1,33},{2,34},{3,35},{4,36},{5,37},{6,38},{7,39},{8,40},{9,... | collective-permute-start | bytes 1179656 | tf_op jit(solution)/shard_map/ppermute | solution.py:350
  103.4 26.8 %collective-permute-start.6 = (bf16[4,384,128]{2,1,0:T(8,128)(2,1)}, bf16[4,384,128]{2,1,0:T(8,128)(2,1)S(1)}, u32[]{:S(2)}, u32[]{:S(2)}) collective-permute-start(bf16[4,384,128]{2,1,0:T(8,128)(2,1)} %get-tuple-element.61), channel_id=1, source_target_pairs={{0,64},{1,65},{2,66},{3,67},{4,68},{5,69},{6,70},{7,71},{8,72},{9,... | collective-permute-start | bytes 1179656 | tf_op jit(solution)/shard_map/ppermute | solution.py:350
  104.9 25.3 %collective-permute-start.5 = (bf16[4,384,128]{2,1,0:T(8,128)(2,1)S(1)}, bf16[4,384,128]{2,1,0:T(8,128)(2,1)S(1)}, u32[]{:S(2)}, u32[]{:S(2)}) collective-permute-start(bf16[4,384,128]{2,1,0:T(8,128)(2,1)S(1)} %get-tuple-element.62), channel_id=1, source_target_pairs={{0,96},{1,97},{2,98},{3,99},{4,100},{5,101},{6,102},{7,103},{8,104... | collective-permute-start | bytes 1179656 | tf_op jit(solution)/shard_map/ppermute | solution.py:350
  106.7 30.0 %collective-permute-start.9 = (bf16[4,384,128]{2,1,0:T(8,128)(2,1)}, bf16[4,384,128]{2,1,0:T(8,128)(2,1)S(1)}, u32[]{:S(2)}, u32[]{:S(2)}) collective-permute-start(bf16[4,384,128]{2,1,0:T(8,128)(2,1)} %get-tuple-element.58), channel_id=1, source_target_pairs={{0,64},{1,65},{2,66},{3,67},{4,68},{5,69},{6,70},{7,71},{8,72},{9,... | collective-permute-start | bytes 1179656 | tf_op jit(solution)/shard_map/ppermute | solution.py:350
  110.6 29.0 %collective-permute-start.8 = (bf16[4,384,128]{2,1,0:T(8,128)(2,1)}, bf16[4,384,128]{2,1,0:T(8,128)(2,1)S(1)}, u32[]{:S(2)}, u32[]{:S(2)}) collective-permute-start(bf16[4,384,128]{2,1,0:T(8,128)(2,1)} %get-tuple-element.59), channel_id=1, source_target_pairs={{0,96},{1,97},{2,98},{3,99},{4,100},{5,101},{6,102},{7,103},{8,104... | collective-permute-start | bytes 1179656 | tf_op jit(solution)/shard_map/ppermute | solution.py:350
  129.5 30.1 %collective-permute-start.20 = (bf16[4,384,128]{2,1,0:T(8,128)(2,1)S(1)}, bf16[4,384,128]{2,1,0:T(8,128)(2,1)}, u32[]{:S(2)}, u32[]{:S(2)}) collective-permute-start(bf16[4,384,128]{2,1,0:T(8,128)(2,1)S(1)} %get-tuple-element.46), channel_id=1, source_target_pairs={{0,96},{1,97},{2,98},{3,99},{4,100},{5,101},{6,102},{7,103},{8,104... | collective-permute-start | bytes 1179656 | tf_op jit(solution)/shard_map/ppermute | solution.py:372
  150.5 12.4 %collective-permute-start.21 = (bf16[4,384,128]{2,1,0:T(8,128)(2,1)S(1)}, bf16[4,384,128]{2,1,0:T(8,128)(2,1)}, u32[]{:S(2)}, u32[]{:S(2)}) collective-permute-start(bf16[4,384,128]{2,1,0:T(8,128)(2,1)S(1)} %get-tuple-element.47), channel_id=1, source_target_pairs={{0,32},{1,33},{2,34},{3,35},{4,36},{5,37},{6,38},{7,39},{8,40},{9,... | collective-permute-start | bytes 1179656 | tf_op jit(solution)/shard_map/ppermute | solution.py:372
  153.5 46.0 %collective-permute-start.1 = (bf16[4,384,128]{2,1,0:T(8,128)(2,1)}, bf16[4,384,128]{2,1,0:T(8,128)(2,1)S(1)}, u32[]{:S(2)}, u32[]{:S(2)}) collective-permute-start(bf16[4,384,128]{2,1,0:T(8,128)(2,1)} %get-tuple-element.56), channel_id=1, source_target_pairs={{0,32},{1,33},{2,34},{3,35},{4,36},{5,37},{6,38},{7,39},{8,40},{9,... | collective-permute-start | bytes 1179656 | tf_op jit(solution)/shard_map/ppermute | solution.py:350
  156.9 43.5 %collective-permute-start.3 = (bf16[4,384,128]{2,1,0:T(8,128)(2,1)}, bf16[4,384,128]{2,1,0:T(8,128)(2,1)S(1)}, u32[]{:S(2)}, u32[]{:S(2)}) collective-permute-start(bf16[4,384,128]{2,1,0:T(8,128)(2,1)} %get-tuple-element.53), channel_id=1, source_target_pairs={{0,32},{1,33},{2,34},{3,35},{4,36},{5,37},{6,38},{7,39},{8,40},{9,... | collective-permute-start | bytes 1179656 | tf_op jit(solution)/shard_map/ppermute | solution.py:350
  158.9 31.6 %collective-permute-start.22 = (bf16[4,384,128]{2,1,0:T(8,128)(2,1)S(1)}, bf16[4,384,128]{2,1,0:T(8,128)(2,1)S(1)}, u32[]{:S(2)}, u32[]{:S(2)}) collective-permute-start(bf16[4,384,128]{2,1,0:T(8,128)(2,1)S(1)} %get-tuple-element.48), channel_id=1, source_target_pairs={{0,64},{1,65},{2,66},{3,67},{4,68},{5,69},{6,70},{7,71},{8,72},{9,... | collective-permute-start | bytes 1179656 | tf_op jit(solution)/shard_map/ppermute | solution.py:372
  191.3 66.6 %all-to-all-start.5 = ((bf16[16,384,128]{2,1,0:T(8,128)(2,1)}), bf16[16,384,128]{2,1,0:T(8,128)(2,1)S(1)}, u32[]{:S(2)}, u32[]{:S(2)}) async-start(bf16[16,384,128]{2,1,0:T(8,128)(2,1)} %bitcast.44), calls=%async_computation.5 | async-start | bytes 3145728 | tf_op jit(solution)/shard_map/all_to_all | solution.py:301
  196.4 14.9 %collective-permute-start.14 = (bf16[4,384,128]{2,1,0:T(8,128)(2,1)S(1)}, bf16[4,384,128]{2,1,0:T(8,128)(2,1)S(1)}, u32[]{:S(2)}, u32[]{:S(2)}) collective-permute-start(bf16[4,384,128]{2,1,0:T(8,128)(2,1)S(1)} %copy-done.6), channel_id=1, source_target_pairs={{0,64},{1,65},{2,66},{3,67},{4,68},{5,69},{6,70},{7,71},{8,72},{9,... | collective-permute-start | bytes 1179656 | tf_op jit(solution)/shard_map/ppermute | solution.py:350
  196.5 14.8 %collective-permute-start.13 = (bf16[4,384,128]{2,1,0:T(8,128)(2,1)S(1)}, bf16[4,384,128]{2,1,0:T(8,128)(2,1)S(1)}, u32[]{:S(2)}, u32[]{:S(2)}) collective-permute-start(bf16[4,384,128]{2,1,0:T(8,128)(2,1)S(1)} %copy-done.5), channel_id=1, source_target_pairs={{0,96},{1,97},{2,98},{3,99},{4,100},{5,101},{6,102},{7,103},{8,104... | collective-permute-start | bytes 1179656 | tf_op jit(solution)/shard_map/ppermute | solution.py:350
  196.6 20.9 %collective-permute-start.16 = (bf16[4,384,128]{2,1,0:T(8,128)(2,1)}, bf16[4,384,128]{2,1,0:T(8,128)(2,1)S(1)}, u32[]{:S(2)}, u32[]{:S(2)}) collective-permute-start(bf16[4,384,128]{2,1,0:T(8,128)(2,1)} %get-tuple-element.51), channel_id=1, source_target_pairs={{0,64},{1,65},{2,66},{3,67},{4,68},{5,69},{6,70},{7,71},{8,72},{9,... | collective-permute-start | bytes 1179656 | tf_op jit(solution)/shard_map/ppermute | solution.py:350
  199.5 24.9 %collective-permute-start.15 = (bf16[4,384,128]{2,1,0:T(8,128)(2,1)S(1)}, bf16[4,384,128]{2,1,0:T(8,128)(2,1)S(1)}, u32[]{:S(2)}, u32[]{:S(2)}) collective-permute-start(bf16[4,384,128]{2,1,0:T(8,128)(2,1)S(1)} %get-tuple-element.52), channel_id=1, source_target_pairs={{0,96},{1,97},{2,98},{3,99},{4,100},{5,101},{6,102},{7,103},{8,104... | collective-permute-start | bytes 1179656 | tf_op jit(solution)/shard_map/ppermute | solution.py:350
  211.0 28.4 %collective-permute-start.12 = (bf16[4,384,128]{2,1,0:T(8,128)(2,1)S(1)}, bf16[4,384,128]{2,1,0:T(8,128)(2,1)S(1)}, u32[]{:S(2)}, u32[]{:S(2)}) collective-permute-start(bf16[4,384,128]{2,1,0:T(8,128)(2,1)S(1)} %get-tuple-element.40), channel_id=1, source_target_pairs={{0,96},{1,97},{2,98},{3,99},{4,100},{5,101},{6,102},{7,103},{8,104... | collective-permute-start | bytes 1179656 | tf_op jit(solution)/shard_map/ppermute | solution.py:372
  235.3 11.2 %collective-permute-start.17 = (bf16[4,384,128]{2,1,0:T(8,128)(2,1)S(1)}, bf16[4,384,128]{2,1,0:T(8,128)(2,1)S(1)}, u32[]{:S(2)}, u32[]{:S(2)}) collective-permute-start(bf16[4,384,128]{2,1,0:T(8,128)(2,1)S(1)} %get-tuple-element.43), channel_id=1, source_target_pairs={{0,32},{1,33},{2,34},{3,35},{4,36},{5,37},{6,38},{7,39},{8,40},{9,... | collective-permute-start | bytes 1179656 | tf_op jit(solution)/shard_map/ppermute | solution.py:372
  236.9 20.2 %collective-permute-start.18 = (bf16[4,384,128]{2,1,0:T(8,128)(2,1)S(1)}, bf16[4,384,128]{2,1,0:T(8,128)(2,1)S(1)}, u32[]{:S(2)}, u32[]{:S(2)}) collective-permute-start(bf16[4,384,128]{2,1,0:T(8,128)(2,1)S(1)} %get-tuple-element.44), channel_id=1, source_target_pairs={{0,64},{1,65},{2,66},{3,67},{4,68},{5,69},{6,70},{7,71},{8,72},{9,... | collective-permute-start | bytes 1179656 | tf_op jit(solution)/shard_map/ppermute | solution.py:372
  257.9 22.1 %all-to-all-start.4 = ((bf16[16,384,128]{2,1,0:T(8,128)(2,1)}), bf16[16,384,128]{2,1,0:T(8,128)(2,1)}, u32[]{:S(2)}, u32[]{:S(2)}) async-start(bf16[16,384,128]{2,1,0:T(8,128)(2,1)} %bitcast.38), calls=%async_computation.4 | async-start | bytes 3145728 | tf_op jit(solution)/shard_map/all_to_all | solution.py:301
  262.3 22.9 %collective-permute-start.23 = (bf16[4,2,384,128]{3,2,1,0:T(8,128)(2,1)S(1)}, bf16[4,2,384,128]{3,2,1,0:T(8,128)(2,1)S(1)}, u32[]{:S(2)}, u32[]{:S(2)}) collective-permute-start(bf16[4,2,384,128]{3,2,1,0:T(8,128)(2,1)S(1)} %slice_bitcast_fusion), channel_id=1, source_target_pairs={{0,1},{1,0},{2,3},{3,2},{4,5},{5,4},{6,7},{7,6},{8,9},{9,8},{10,11... | collective-permute-start | bytes 2359304 | tf_op jit(solution)/shard_map/ppermute | solution.py:376
  281.2 7.3 %collective-permute-start.19 = (bf16[4,2,384,128]{3,2,1,0:T(8,128)(2,1)S(1)}, bf16[4,2,384,128]{3,2,1,0:T(8,128)(2,1)S(1)}, u32[]{:S(2)}, u32[]{:S(2)}) collective-permute-start(bf16[4,2,384,128]{3,2,1,0:T(8,128)(2,1)S(1)} %slice_bitcast_fusion.1), channel_id=1, source_target_pairs={{0,1},{1,0},{2,3},{3,2},{4,5},{5,4},{6,7},{7,6},{8,9},{9,8},{10,11... | collective-permute-start | bytes 2359304 | tf_op jit(solution)/shard_map/ppermute | solution.py:376
  (7 other events, 21.8 us)

commit v3 on v2

--- a/solution.py
+++ b/solution.py
@@ -23,7 +23,7 @@
 BOTH = ("seq", "text")
 RING = 4
 SHIFTS = (1, 3, 2)
-PAIRS = ((0, 1), (3, 2))
+GROUPS = (((0,), (1,), (3, 2)), ((0,), (1, 3), (2,)))
 
 
 def dot(a, b, dims):
@@ -65,8 +65,11 @@
 
 
 def attention_kernel(head, own, parts, info, *refs):
-    q_refs, g_refs, key_ref, value_ref = refs[:2], refs[2:4], refs[4], refs[5]
-    dq_outs, dk_out, dv_out = refs[-16:-14], refs[-14], refs[-13]
+    chunks = info.shape[1] // RING
+    q_refs, g_refs, key_ref, value_ref = (
+        refs[:chunks], refs[chunks : 2 * chunks], refs[2 * chunks], refs[2 * chunks + 1]
+    )
+    dq_outs, dk_out, dv_out = refs[-14 - chunks : -14], refs[-14], refs[-13]
     field_q, field_g, keys, values, dq, dk, dv, raised, slope, share, scores = refs[-12:-1]
     copies = refs[-1]
     work = (raised, slope, share, scores)
@@ -106,7 +109,7 @@
     def both(i, carry):
         chunk, within = lax.div(i, RING), lax.rem(i, RING)
         rows, toks = info[1, i], info[2, i]
-        for copy in fetch(1, within, i):
+        for copy in fetch(chunks - 1, within, i):
             copy.wait()
         low_t = 0
         for t in CASES:
@@ -121,7 +124,7 @@
                 )
                 low_r = r
             low_t = t
-        for which in range(2):
+        for which in range(chunks):
 
             @pl.when(chunk == which)
             def _(which=which):
@@ -141,7 +144,8 @@
     hbm_spec = pl.BlockSpec(memory_space=pltpu.HBM)
     chunk = (RING, RES, HEAD_DIM)
     held = list(grads_so_far)
-    count = 2 * RING
+    chunks = len(q_fields)
+    count = chunks * RING
     tokens, residues = (count, TOK, HEAD_DIM), (count, RES, HEAD_DIM)
     bf16 = jnp.bfloat16
     return pl.pallas_call(
@@ -150,8 +154,8 @@
         grid_spec=pltpu.PrefetchScalarGridSpec(
             num_scalar_prefetch=1,
             grid=(1,),
-            in_specs=[any_spec] * 4 + [hbm_spec] * (2 + len(held)),
-            out_specs=[any_spec] * 2 + [hbm_spec] * 2,
+            in_specs=[any_spec] * (2 * chunks) + [hbm_spec] * (2 + len(held)),
+            out_specs=[any_spec] * chunks + [hbm_spec] * 2,
             scratch_shapes=[pltpu.VMEM(residues, bf16)] * 2
             + [pltpu.VMEM(tokens, bf16)] * 2
             + [pltpu.VMEM(residues, bf16)]
@@ -161,12 +165,14 @@
             + [pltpu.SemaphoreType.DMA((7, count))],
         ),
         out_shape=[
-            jax.ShapeDtypeStruct(((RING,) if own else ()) + chunk, bf16),
-            jax.ShapeDtypeStruct(chunk, bf16),
+            jax.ShapeDtypeStruct(((RING,) if own and n == 0 else ()) + chunk, bf16)
+            for n in range(chunks)
+        ]
+        + [
             jax.ShapeDtypeStruct(keys.shape, bf16),
             jax.ShapeDtypeStruct(values.shape, bf16),
         ],
-        input_output_aliases={7: 2, 8: 3} if held else {},
+        input_output_aliases={2 * chunks + 3 + n: chunks + n for n in range(len(held))},
         cost_estimate=pl.CostEstimate(
             flops=count * 10 * RES * TOK * HEAD_DIM,
             bytes_accessed=count * 14 * RES * HEAD_DIM,
@@ -325,7 +331,7 @@
             )
         return jnp.concatenate(columns, axis=1).astype(jnp.int32)
 
-    infos = {pair: info_of(pair) for pair in PAIRS}
+    infos = {group: info_of(group) for groups in GROUPS for group in groups}
 
     def into(fields, heads):
         joined, send = pack(core, fields, heads)
@@ -358,14 +364,14 @@
     for h in range(2):
         (own_q, part_q), (own_g, part_g) = sources[h]
         back = None
-        for pair in PAIRS:
-            q_fields = [own_q if s == 0 else q_chunks[h][s] for s in pair]
-            g_fields = [own_g if s == 0 else g_chunks[h][s] for s in pair]
+        for group in GROUPS[h]:
+            q_fields = [own_q if s == 0 else q_chunks[h][s] for s in group]
+            g_fields = [own_g if s == 0 else g_chunks[h][s] for s in group]
             *dqs, dk, dv = attention_backward(
-                infos[pair], h, pair[0] == 0, (part_q, part_g), q_fields, g_fields, keys, values, grads
+                infos[group], h, group[0] == 0, (part_q, part_g), q_fields, g_fields, keys, values, grads
             )
             grads = (dk, dv)
-            for s, dq in zip(pair, dqs):
+            for s, dq in zip(group, dqs):
                 if s == 0:
                     back = dq
                     continue

time: 293 us -> 278 us (0.949)
  waiting for transfers between devices: 142 us -> 122 us
  Pallas kernels: 57.1 us -> 61.5 us
  other arithmetic: 0.24 us -> 4.52 us
  starting transfers between devices: 69 us -> 65.9 us
    ppermute x12, waiting for transfers between devices: 32.7 us -> 22 us  [spread(): chunks[s] = lax.ppermute(piece, BOTH, shift(s))]
    ppermute x6, waiting for transfers between devices: 43.5 us -> 32.9 us  [body(): dq = lax.ppermute(dq, BOTH, shift(-s))]
    pallas_call x4 -> x6, Pallas kernels: 42.9 us -> 47.2 us  [attention_backward(): pl.pallas_call(functools.partial(attention_kernel, head, own, parts), com...]
    ppermute x2, starting transfers between devices: 4.94 us -> 1.75 us  [body(): got = lax.ppermute(home[:, 1], BOTH, SWAP)]
  transfers between devices with their start and end apart: 30 -> 30, of which waited for: 18 -> 13; matrix products, arithmetic and copies ran while one was open for 7% -> 9% of each run, Pallas kernels for 18% -> 21%
where the time goes in v3:
time: 278 us; the launch traced here: 276 us
  waiting for transfers between devices  122 us (44%)
  starting transfers between devices  65.9 us (24%)
  Pallas kernels  61.5 us (22%)
  local copies, waits for them, and re-layouts  21.1 us (8%)
  other arithmetic  4.52 us (2%)
    all_to_all x6, waiting for transfers between devices, plane_exchange(): lax.all_to_all(field, BOTH, 0, 0, axis_index_groups=PLANES, tiled=True)  59.6 us
    pallas_call x6, Pallas kernels, attention_backward(): pl.pallas_call(functools.partial(attention_kernel, head, own, parts), com...  47.2 us
    all_to_all x6, starting transfers between devices, plane_exchange(): lax.all_to_all(field, BOTH, 0, 0, axis_index_groups=PLANES, tiled=True)  41 us
    ppermute x6, waiting for transfers between devices, body(): dq = lax.ppermute(dq, BOTH, shift(-s))  32.9 us
    ppermute x12, waiting for transfers between devices, spread(): chunks[s] = lax.ppermute(piece, BOTH, shift(s))  22 us
    ppermute x12, starting transfers between devices, spread(): chunks[s] = lax.ppermute(piece, BOTH, shift(s))  12.9 us
    pallas_call x4, Pallas kernels, pack(): pl.pallas_call(functools.partial(pack_kernel, heads), compiler_params=plt...  9.55 us
    ppermute x6, starting transfers between devices, body(): dq = lax.ppermute(dq, BOTH, shift(-s))  8.44 us
  transfers between devices with their start and end apart: 30, of which 13 were waited for; matrix products, arithmetic and copies ran while one was open for 9% of the time, Pallas kernels for 21%

profile of v3, /device:TPU:1, one launch (start us, length us, event | category | flops | bytes accessed | tf_op | source)
XLA Modules:
  0.0 276.3 jit_solution(1778552528846931527)
XLA Ops:
  0.6 2.4 shard_map.85
  7.6 9.0 %all-to-all-start = ((bf16[16,1,384,128]{3,2,1,0:T(8,128)(2,1)}), bf16[16,1,384,128]{3,2,1,0:T(8,128)(2,1)S(1)}, u32[]{:S(2)}, u32[]{:S(2)}) async-start(bf16[16,1,384,128]{3,2,1,0:T(8,128)(2,1)} %bitcast.96), calls=%async_computation | async-start | bytes 3145728 | tf_op jit(solution)/shard_map/all_to_all | solution.py:307
  16.6 2.4 shard_map.87
  19.1 2.5 collective-permute-done.2
  22.6 14.3 %all-to-all-done = bf16[16,1,384,128]{3,2,1,0:T(8,128)(2,1)S(1)} async-done(((bf16[16,1,384,128]{3,2,1,0:T(8,128)(2,1)}), bf16[16,1,384,128]{3,2,1,0:T(8,128)(2,1)S(1)}, u32[]{:S(2)}, u32[]{:S(2)}) %all-to-all-start) | async-done | bytes 1572896 | tf_op jit(solution)/shard_map/all_to_all | solution.py:307
  36.9 6.3 %all-to-all-start.2 = ((bf16[16,1,384,128]{3,2,1,0:T(8,128)(2,1)}), bf16[16,1,384,128]{3,2,1,0:T(8,128)(2,1)S(1)}, u32[]{:S(2)}, u32[]{:S(2)}) async-start(bf16[16,1,384,128]{3,2,1,0:T(8,128)(2,1)} %bitcast.97), calls=%async_computation.2 | async-start | bytes 3145728 | tf_op jit(solution)/shard_map/all_to_all | solution.py:307
  43.2 2.4 shard_map.88
  45.7 2.5 collective-permute-done.5
  49.2 13.6 %all-to-all-done.2 = bf16[16,1,384,128]{3,2,1,0:T(8,128)(2,1)S(1)} async-done(((bf16[16,1,384,128]{3,2,1,0:T(8,128)(2,1)}), bf16[16,1,384,128]{3,2,1,0:T(8,128)(2,1)S(1)}, u32[]{:S(2)}, u32[]{:S(2)}) %all-to-all-start.2) | async-done | bytes 1572896 | tf_op jit(solution)/shard_map/all_to_all | solution.py:307
  62.8 7.6 %all-to-all-start.3 = ((bf16[16,1,384,128]{3,2,1,0:T(8,128)(2,1)}), bf16[16,1,384,128]{3,2,1,0:T(8,128)(2,1)}, u32[]{:S(2)}, u32[]{:S(2)}) async-start(bf16[16,1,384,128]{3,2,1,0:T(8,128)(2,1)} %bitcast.98), calls=%async_computation.3 | async-start | bytes 3145728 | tf_op jit(solution)/shard_map/all_to_all | solution.py:307
  70.5 2.4 shard_map.86
  77.8 12.4 %all-to-all-done.3 = bf16[16,1,384,128]{3,2,1,0:T(8,128)(2,1)} async-done(((bf16[16,1,384,128]{3,2,1,0:T(8,128)(2,1)}), bf16[16,1,384,128]{3,2,1,0:T(8,128)(2,1)}, u32[]{:S(2)}, u32[]{:S(2)}) %all-to-all-start.3) | async-done | bytes 1572896 | tf_op jit(solution)/shard_map/all_to_all | solution.py:307
  90.1 7.4 %all-to-all-start.1 = ((bf16[16,1,384,128]{3,2,1,0:T(8,128)(2,1)}), bf16[16,1,384,128]{3,2,1,0:T(8,128)(2,1)}, u32[]{:S(2)}, u32[]{:S(2)}) async-start(bf16[16,1,384,128]{3,2,1,0:T(8,128)(2,1)} %bitcast.95), calls=%async_computation.1 | async-start | bytes 3145728 | tf_op jit(solution)/shard_map/all_to_all | solution.py:307
  108.1 2.9 %collective-permute-done.8.refs_0_ = bf16[4,384,128]{2,1,0:T(8,128)(2,1)S(1)} collective-permute-done((bf16[4,384,128]{2,1,0:T(8,128)(2,1)}, bf16[4,384,128]{2,1,0:T(8,128)(2,1)S(1)}, u32[]{:S(2)}, u32[]{:S(2)}) %collective-permute-start.8) | collective-permute-done | bytes 393248 | tf_op jit(solution)/shard_map/ppermute | solution.py:356
  112.4 6.3 %shard_map.89 = (bf16[4,4,384,128]{3,2,1,0:T(8,128)(2,1)}, bf16[7168,256]{1,0:T(8,128)(2,1)}, bf16[7168,256]{1,0:T(8,128)(2,1)}) custom-call(s32[4,4]{1,0:T(4,128)S(1)} %pad_add_fusion.2.info, bf16[4,4,1,384,128]{4,3,2,1,0:T(8,128)(2,1)S(1)} %bitcast.87, bf16[4,4,1,384,128]{4,3,2,1,0:T(8,128)(2,1)} %bitcast.24.refs_1_, bf16[7168,256]{1,0:T(8,128)(2,1)} %refs_2_.7, ...), custom_call_target="tpu_custom_call" | custom-call | flops 880803840 | bytes 2752512 | tf_op jit(solution)/shard_map/pallas_call | solution.py:151
  118.7 19.1 %collective-permute-done.9.refs_1_ = bf16[4,384,128]{2,1,0:T(8,128)(2,1)S(1)} collective-permute-done((bf16[4,384,128]{2,1,0:T(8,128)(2,1)S(1)}, bf16[4,384,128]{2,1,0:T(8,128)(2,1)S(1)}, u32[]{:S(2)}, u32[]{:S(2)}) %collective-permute-start.9) | collective-permute-done | bytes 393248 | tf_op jit(solution)/shard_map/ppermute | solution.py:356
  137.8 6.7 %shard_map.90 = (bf16[4,384,128]{2,1,0:T(8,128)(2,1)S(1)}, bf16[7168,256]{1,0:T(8,128)(2,1)}, bf16[7168,256]{1,0:T(8,128)(2,1)}) custom-call(s32[4,4]{1,0:T(4,128)S(1)} %get-tuple-element.84.info, bf16[4,384,128]{2,1,0:T(8,128)(2,1)S(1)} %collective-permute-done.8.refs_0_, ...), custom_call_target="tpu_custom_call", output_to_operand_aliasing={{1}: (5, {}), {2}: (6, {})} | custom-call | flops 880803840 | bytes 2752512 | tf_op jit(solution)/shard_map/pallas_call | solution.py:151
  144.6 10.4 %shard_map.91 = (bf16[4,384,128]{2,1,0:T(8,128)(2,1)}, bf16[4,384,128]{2,1,0:T(8,128)(2,1)S(1)}, bf16[7168,256]{1,0:T(8,128)(2,1)}, bf16[7168,256]{1,0:T(8,128)(2,1)}) custom-call(s32[4,8]{1,0:T(4,128)S(1)} %fusion.info, bf16[4,384,128]{2,1,0:T(8,128)(2,1)S(1)} %collective-permute-done.3.refs_0_, ...), custom_call_target="tpu_custom_call", output_to_operand_aliasing={{2}: (7, {}), {3}: (8, {})} | custom-call | flops 1761607680 | bytes 5505024 | tf_op jit(solution)/shard_map/pallas_call | solution.py:151
  157.9 2.7 collective-permute-start.11
  160.6 2.3 dynamic-slice_bitcast_fusion
  169.7 23.1 %collective-permute-done.22 = bf16[4,384,128]{2,1,0:T(8,128)(2,1)S(1)} collective-permute-done((bf16[4,384,128]{2,1,0:T(8,128)(2,1)S(1)}, bf16[4,384,128]{2,1,0:T(8,128)(2,1)S(1)}, u32[]{:S(2)}, u32[]{:S(2)}) %collective-permute-start.22) | collective-permute-done | bytes 393248 | tf_op jit(solution)/shard_map/ppermute | solution.py:378
  193.6 5.2 %all-to-all-start.5 = ((bf16[16,384,128]{2,1,0:T(8,128)(2,1)}), bf16[16,384,128]{2,1,0:T(8,128)(2,1)}, u32[]{:S(2)}, u32[]{:S(2)}) async-start(bf16[16,384,128]{2,1,0:T(8,128)(2,1)} %bitcast.44), calls=%async_computation.5 | async-start | bytes 3145728 | tf_op jit(solution)/shard_map/all_to_all | solution.py:307
  199.6 2.8 collective-permute-start.16
  202.3 6.3 %shard_map.92 = (bf16[4,4,384,128]{3,2,1,0:T(8,128)(2,1)}, bf16[7168,256]{1,0:T(8,128)(2,1)}, bf16[7168,256]{1,0:T(8,128)(2,1)}) custom-call(s32[4,4]{1,0:T(4,128)S(1)} %pad_add_fusion.2.info, bf16[4,4,1,384,128]{4,3,2,1,0:T(8,128)(2,1)S(1)} %bitcast.85, bf16[4,4,1,384,128]{4,3,2,1,0:T(8,128)(2,1)} %bitcast.12.refs_1_, ...), custom_call_target="tpu_custom_call", output_to_operand_aliasing={{1}: (5, {}), {2}: (6, {})} | custom-call | flops 880803840 | bytes 2752512 | tf_op jit(solution)/shard_map/pallas_call | solution.py:151
  208.8 11.7 %shard_map.93 = (bf16[4,384,128]{2,1,0:T(8,128)(2,1)S(1)}, bf16[4,384,128]{2,1,0:T(8,128)(2,1)S(1)}, bf16[7168,256]{1,0:T(8,128)(2,1)}, bf16[7168,256]{1,0:T(8,128)(2,1)}) custom-call(s32[4,8]{1,0:T(4,128)S(1)} %fusion.1.info, bf16[4,384,128]{2,1,0:T(8,128)(2,1)S(1)} %collective-permute-done.10.refs_0_, ...), custom_call_target="tpu_custom_call", output_to_operand_aliasing={{2}: (7, {}), {3}: (8, {})} | custom-call | flops 1761607680 | bytes 5505024 | tf_op jit(solution)/shard_map/pallas_call | solution.py:151
  222.0 5.9 %shard_map.94 = (bf16[4,384,128]{2,1,0:T(8,128)(2,1)S(1)}, bf16[7168,256]{1,0:T(8,128)(2,1)}, bf16[7168,256]{1,0:T(8,128)(2,1)}) custom-call(s32[4,4]{1,0:T(4,128)S(1)} %get-tuple-element.83.info, bf16[4,384,128]{2,1,0:T(8,128)(2,1)S(1)} %collective-permute-done.16.refs_0_, ...), custom_call_target="tpu_custom_call", output_to_operand_aliasing={{1}: (5, {}), {2}: (6, {})} | custom-call | flops 880803840 | bytes 2752512 | tf_op jit(solution)/shard_map/pallas_call | solution.py:151
  228.0 3.9 %collective-permute-start.18 = (bf16[4,384,128]{2,1,0:T(8,128)(2,1)S(1)}, bf16[4,384,128]{2,1,0:T(8,128)(2,1)S(1)}, u32[]{:S(2)}, u32[]{:S(2)}) collective-permute-start(bf16[4,384,128]{2,1,0:T(8,128)(2,1)S(1)} %get-tuple-element.52), channel_id=1, source_target_pairs={{0,64},{1,65},{2,66},{3,67},{4,68},{5,69},{6,70},{7,71},{8,72},{9,... | collective-permute-start | bytes 1179656 | tf_op jit(solution)/shard_map/ppermute | solution.py:378
  233.4 8.6 %collective-permute-done.18 = bf16[4,384,128]{2,1,0:T(8,128)(2,1)S(1)} collective-permute-done((bf16[4,384,128]{2,1,0:T(8,128)(2,1)S(1)}, bf16[4,384,128]{2,1,0:T(8,128)(2,1)S(1)}, u32[]{:S(2)}, u32[]{:S(2)}) %collective-permute-start.18) | collective-permute-done | bytes 393248 | tf_op jit(solution)/shard_map/ppermute | solution.py:378
  242.8 5.5 %all-to-all-start.4 = ((bf16[16,384,128]{2,1,0:T(8,128)(2,1)}), bf16[16,384,128]{2,1,0:T(8,128)(2,1)S(1)}, u32[]{:S(2)}, u32[]{:S(2)}) async-start(bf16[16,384,128]{2,1,0:T(8,128)(2,1)} %bitcast.38), calls=%async_computation.4 | async-start | bytes 3145728 | tf_op jit(solution)/shard_map/all_to_all | solution.py:307
  249.5 19.2 %all-to-all-done.4 = bf16[16,384,128]{2,1,0:T(8,128)(2,1)S(1)} async-done(((bf16[16,384,128]{2,1,0:T(8,128)(2,1)}), bf16[16,384,128]{2,1,0:T(8,128)(2,1)S(1)}, u32[]{:S(2)}, u32[]{:S(2)}) %all-to-all-start.4) | async-done | bytes 1572896 | tf_op jit(solution)/shard_map/all_to_all | solution.py:307
  270.5 2.4 shard_map.95.rest_0_
  273.8 2.4 shard_map.96
  (94 shorter events, 42.8 us)
Async XLA Ops:
  3.0 3.6 %collective-permute-start = (bf16[4,2,1,384,128]{4,3,2,1,0:T(8,128)(2,1)}, bf16[4,2,1,384,128]{4,3,2,1,0:T(8,128)(2,1)S(1)}, u32[]{:S(2)}, u32[]{:S(2)}) collective-permute-start(bf16[4,2,1,384,128]{4,3,2,1,0:T(8,128)(2,1)} %get-tuple-element.32), channel_id=1, source_target_pairs={{0,1},{1,0},{2,3},{3,2},{4,5},{5,4},{6,7},{7,6},{8,9},{9,8},{10,11... | collective-permute-start | bytes 2359304 | tf_op jit(solution)/shard_map/ppermute | solution.py:338
  7.6 29.3 %all-to-all-start = ((bf16[16,1,384,128]{3,2,1,0:T(8,128)(2,1)}), bf16[16,1,384,128]{3,2,1,0:T(8,128)(2,1)S(1)}, u32[]{:S(2)}, u32[]{:S(2)}) async-start(bf16[16,1,384,128]{3,2,1,0:T(8,128)(2,1)} %bitcast.96), calls=%async_computation | async-start | bytes 3145728 | tf_op jit(solution)/shard_map/all_to_all | solution.py:307
  19.0 2.6 collective-permute-start.2
  36.9 25.9 %all-to-all-start.2 = ((bf16[16,1,384,128]{3,2,1,0:T(8,128)(2,1)}), bf16[16,1,384,128]{3,2,1,0:T(8,128)(2,1)S(1)}, u32[]{:S(2)}, u32[]{:S(2)}) async-start(bf16[16,1,384,128]{3,2,1,0:T(8,128)(2,1)} %bitcast.97), calls=%async_computation.2 | async-start | bytes 3145728 | tf_op jit(solution)/shard_map/all_to_all | solution.py:307
  45.6 2.6 collective-permute-start.5
  62.8 27.3 %all-to-all-start.3 = ((bf16[16,1,384,128]{3,2,1,0:T(8,128)(2,1)}), bf16[16,1,384,128]{3,2,1,0:T(8,128)(2,1)}, u32[]{:S(2)}, u32[]{:S(2)}) async-start(bf16[16,1,384,128]{3,2,1,0:T(8,128)(2,1)} %bitcast.98), calls=%async_computation.3 | async-start | bytes 3145728 | tf_op jit(solution)/shard_map/all_to_all | solution.py:307
  72.9 2.7 collective-permute-start.1
  90.1 70.4 %all-to-all-start.1 = ((bf16[16,1,384,128]{3,2,1,0:T(8,128)(2,1)}), bf16[16,1,384,128]{3,2,1,0:T(8,128)(2,1)}, u32[]{:S(2)}, u32[]{:S(2)}) async-start(bf16[16,1,384,128]{3,2,1,0:T(8,128)(2,1)} %bitcast.95), calls=%async_computation.1 | async-start | bytes 3145728 | tf_op jit(solution)/shard_map/all_to_all | solution.py:307
  99.1 11.9 %collective-permute-start.8 = (bf16[4,384,128]{2,1,0:T(8,128)(2,1)}, bf16[4,384,128]{2,1,0:T(8,128)(2,1)S(1)}, u32[]{:S(2)}, u32[]{:S(2)}) collective-permute-start(bf16[4,384,128]{2,1,0:T(8,128)(2,1)} %get-tuple-element.68), channel_id=1, source_target_pairs={{0,32},{1,33},{2,34},{3,35},{4,36},{5,37},{6,38},{7,39},{8,40},{9,... | collective-permute-start | bytes 1179656 | tf_op jit(solution)/shard_map/ppermute | solution.py:356
  100.8 10.9 %copy-start.4 = (s32[1,4]{1,0:T(1,128)}, s32[1,4]{1,0:T(1,128)S(1)}, u32[]{:S(2)}) copy-start(s32[1,4]{1,0:T(1,128)S(1)} %get-tuple-element.73) | copy-start | bytes 52
  100.8 10.9 %copy-start.5 = (s32[1,4]{1,0:T(1,128)}, s32[1,4]{1,0:T(1,128)S(1)}, u32[]{:S(2)}) copy-start(s32[1,4]{1,0:T(1,128)S(1)} %get-tuple-element.71) | copy-start | bytes 52
  101.5 43.1 %collective-permute-start.3 = (bf16[4,384,128]{2,1,0:T(8,128)(2,1)}, bf16[4,384,128]{2,1,0:T(8,128)(2,1)S(1)}, u32[]{:S(2)}, u32[]{:S(2)}) collective-permute-start(bf16[4,384,128]{2,1,0:T(8,128)(2,1)} %get-tuple-element.70), channel_id=1, source_target_pairs={{0,96},{1,97},{2,98},{3,99},{4,100},{5,101},{6,102},{7,103},{8,104... | collective-permute-start | bytes 1179656 | tf_op jit(solution)/shard_map/ppermute | solution.py:356
  103.0 41.5 %collective-permute-start.4 = (bf16[4,384,128]{2,1,0:T(8,128)(2,1)}, bf16[4,384,128]{2,1,0:T(8,128)(2,1)S(1)}, u32[]{:S(2)}, u32[]{:S(2)}) collective-permute-start(bf16[4,384,128]{2,1,0:T(8,128)(2,1)} %get-tuple-element.69), channel_id=1, source_target_pairs={{0,64},{1,65},{2,66},{3,67},{4,68},{5,69},{6,70},{7,71},{8,72},{9,... | collective-permute-start | bytes 1179656 | tf_op jit(solution)/shard_map/ppermute | solution.py:356
  105.9 38.7 %collective-permute-start.6 = (bf16[4,384,128]{2,1,0:T(8,128)(2,1)S(1)}, bf16[4,384,128]{2,1,0:T(8,128)(2,1)S(1)}, u32[]{:S(2)}, u32[]{:S(2)}) collective-permute-start(bf16[4,384,128]{2,1,0:T(8,128)(2,1)S(1)} %get-tuple-element.67), channel_id=1, source_target_pairs={{0,96},{1,97},{2,98},{3,99},{4,100},{5,101},{6,102},{7,103},{8,104... | collective-permute-start | bytes 1179656 | tf_op jit(solution)/shard_map/ppermute | solution.py:356
  106.8 37.8 %collective-permute-start.7 = (bf16[4,384,128]{2,1,0:T(8,128)(2,1)S(1)}, bf16[4,384,128]{2,1,0:T(8,128)(2,1)S(1)}, u32[]{:S(2)}, u32[]{:S(2)}) collective-permute-start(bf16[4,384,128]{2,1,0:T(8,128)(2,1)S(1)} %get-tuple-element.66), channel_id=1, source_target_pairs={{0,64},{1,65},{2,66},{3,67},{4,68},{5,69},{6,70},{7,71},{8,72},{9,... | collective-permute-start | bytes 1179656 | tf_op jit(solution)/shard_map/ppermute | solution.py:356
  110.9 26.9 %collective-permute-start.9 = (bf16[4,384,128]{2,1,0:T(8,128)(2,1)S(1)}, bf16[4,384,128]{2,1,0:T(8,128)(2,1)S(1)}, u32[]{:S(2)}, u32[]{:S(2)}) collective-permute-start(bf16[4,384,128]{2,1,0:T(8,128)(2,1)S(1)} %get-tuple-element.65), channel_id=1, source_target_pairs={{0,32},{1,33},{2,34},{3,35},{4,36},{5,37},{6,38},{7,39},{8,40},{9,... | collective-permute-start | bytes 1179656 | tf_op jit(solution)/shard_map/ppermute | solution.py:356
  144.5 18.4 %collective-permute-start.20 = (bf16[4,384,128]{2,1,0:T(8,128)(2,1)S(1)}, bf16[4,384,128]{2,1,0:T(8,128)(2,1)}, u32[]{:S(2)}, u32[]{:S(2)}) collective-permute-start(bf16[4,384,128]{2,1,0:T(8,128)(2,1)S(1)} %get-tuple-element.54), channel_id=1, source_target_pairs={{0,96},{1,97},{2,98},{3,99},{4,100},{5,101},{6,102},{7,103},{8,104... | collective-permute-start | bytes 1179656 | tf_op jit(solution)/shard_map/ppermute | solution.py:378
  155.0 12.0 %collective-permute-start.21 = (bf16[4,384,128]{2,1,0:T(8,128)(2,1)}, bf16[4,384,128]{2,1,0:T(8,128)(2,1)}, u32[]{:S(2)}, u32[]{:S(2)}) collective-permute-start(bf16[4,384,128]{2,1,0:T(8,128)(2,1)} %get-tuple-element.55), channel_id=1, source_target_pairs={{0,32},{1,33},{2,34},{3,35},{4,36},{5,37},{6,38},{7,39},{8,40},{9,... | collective-permute-start | bytes 1179656 | tf_op jit(solution)/shard_map/ppermute | solution.py:378
  157.9 50.7 %collective-permute-start.10 = (bf16[4,384,128]{2,1,0:T(8,128)(2,1)}, bf16[4,384,128]{2,1,0:T(8,128)(2,1)S(1)}, u32[]{:S(2)}, u32[]{:S(2)}) collective-permute-start(bf16[4,384,128]{2,1,0:T(8,128)(2,1)} %get-tuple-element.64), channel_id=1, source_target_pairs={{0,32},{1,33},{2,34},{3,35},{4,36},{5,37},{6,38},{7,39},{8,40},{9,... | collective-permute-start | bytes 1179656 | tf_op jit(solution)/shard_map/ppermute | solution.py:356
  157.9 50.8 %collective-permute-start.11 = (bf16[4,384,128]{2,1,0:T(8,128)(2,1)}, bf16[4,384,128]{2,1,0:T(8,128)(2,1)S(1)}, u32[]{:S(2)}, u32[]{:S(2)}) collective-permute-start(bf16[4,384,128]{2,1,0:T(8,128)(2,1)} %get-tuple-element.63), channel_id=1, source_target_pairs={{0,96},{1,97},{2,98},{3,99},{4,100},{5,101},{6,102},{7,103},{8,104... | collective-permute-start | bytes 1179656 | tf_op jit(solution)/shard_map/ppermute | solution.py:356
  162.9 45.9 %collective-permute-start.12 = (bf16[4,384,128]{2,1,0:T(8,128)(2,1)}, bf16[4,384,128]{2,1,0:T(8,128)(2,1)S(1)}, u32[]{:S(2)}, u32[]{:S(2)}) collective-permute-start(bf16[4,384,128]{2,1,0:T(8,128)(2,1)} %get-tuple-element.61), channel_id=1, source_target_pairs={{0,32},{1,33},{2,34},{3,35},{4,36},{5,37},{6,38},{7,39},{8,40},{9,... | collective-permute-start | bytes 1179656 | tf_op jit(solution)/shard_map/ppermute | solution.py:356
  162.9 29.9 %collective-permute-start.22 = (bf16[4,384,128]{2,1,0:T(8,128)(2,1)S(1)}, bf16[4,384,128]{2,1,0:T(8,128)(2,1)S(1)}, u32[]{:S(2)}, u32[]{:S(2)}) collective-permute-start(bf16[4,384,128]{2,1,0:T(8,128)(2,1)S(1)} %get-tuple-element.56), channel_id=1, source_target_pairs={{0,64},{1,65},{2,66},{3,67},{4,68},{5,69},{6,70},{7,71},{8,72},{9,... | collective-permute-start | bytes 1179656 | tf_op jit(solution)/shard_map/ppermute | solution.py:378
  167.0 41.8 %collective-permute-start.13 = (bf16[4,384,128]{2,1,0:T(8,128)(2,1)}, bf16[4,384,128]{2,1,0:T(8,128)(2,1)S(1)}, u32[]{:S(2)}, u32[]{:S(2)}) collective-permute-start(bf16[4,384,128]{2,1,0:T(8,128)(2,1)} %get-tuple-element.60), channel_id=1, source_target_pairs={{0,96},{1,97},{2,98},{3,99},{4,100},{5,101},{6,102},{7,103},{8,104... | collective-permute-start | bytes 1179656 | tf_op jit(solution)/shard_map/ppermute | solution.py:356
  193.6 49.2 %all-to-all-start.5 = ((bf16[16,384,128]{2,1,0:T(8,128)(2,1)}), bf16[16,384,128]{2,1,0:T(8,128)(2,1)}, u32[]{:S(2)}, u32[]{:S(2)}) async-start(bf16[16,384,128]{2,1,0:T(8,128)(2,1)} %bitcast.44), calls=%async_computation.5 | async-start | bytes 3145728 | tf_op jit(solution)/shard_map/all_to_all | solution.py:307
  199.6 22.4 %collective-permute-start.16 = (bf16[4,384,128]{2,1,0:T(8,128)(2,1)S(1)}, bf16[4,384,128]{2,1,0:T(8,128)(2,1)S(1)}, u32[]{:S(2)}, u32[]{:S(2)}) collective-permute-start(bf16[4,384,128]{2,1,0:T(8,128)(2,1)S(1)} %copy-done.2), channel_id=1, source_target_pairs={{0,64},{1,65},{2,66},{3,67},{4,68},{5,69},{6,70},{7,71},{8,72},{9,... | collective-permute-start | bytes 1179656 | tf_op jit(solution)/shard_map/ppermute | solution.py:356
  208.6 13.4 %collective-permute-start.17 = (bf16[4,384,128]{2,1,0:T(8,128)(2,1)S(1)}, bf16[4,384,128]{2,1,0:T(8,128)(2,1)S(1)}, u32[]{:S(2)}, u32[]{:S(2)}) collective-permute-start(bf16[4,384,128]{2,1,0:T(8,128)(2,1)S(1)} %copy-done.3), channel_id=1, source_target_pairs={{0,64},{1,65},{2,66},{3,67},{4,68},{5,69},{6,70},{7,71},{8,72},{9,... | collective-permute-start | bytes 1179656 | tf_op jit(solution)/shard_map/ppermute | solution.py:356
  220.5 11.4 %collective-permute-start.14 = (bf16[4,384,128]{2,1,0:T(8,128)(2,1)S(1)}, bf16[4,384,128]{2,1,0:T(8,128)(2,1)S(1)}, u32[]{:S(2)}, u32[]{:S(2)}) collective-permute-start(bf16[4,384,128]{2,1,0:T(8,128)(2,1)S(1)} %get-tuple-element.48), channel_id=1, source_target_pairs={{0,96},{1,97},{2,98},{3,99},{4,100},{5,101},{6,102},{7,103},{8,104... | collective-permute-start | bytes 1179656 | tf_op jit(solution)/shard_map/ppermute | solution.py:378
  220.5 12.1 %collective-permute-start.15 = (bf16[4,384,128]{2,1,0:T(8,128)(2,1)S(1)}, bf16[4,384,128]{2,1,0:T(8,128)(2,1)S(1)}, u32[]{:S(2)}, u32[]{:S(2)}) collective-permute-start(bf16[4,384,128]{2,1,0:T(8,128)(2,1)S(1)} %get-tuple-element.49), channel_id=1, source_target_pairs={{0,32},{1,33},{2,34},{3,35},{4,36},{5,37},{6,38},{7,39},{8,40},{9,... | collective-permute-start | bytes 1179656 | tf_op jit(solution)/shard_map/ppermute | solution.py:378
  228.0 14.1 %collective-permute-start.18 = (bf16[4,384,128]{2,1,0:T(8,128)(2,1)S(1)}, bf16[4,384,128]{2,1,0:T(8,128)(2,1)S(1)}, u32[]{:S(2)}, u32[]{:S(2)}) collective-permute-start(bf16[4,384,128]{2,1,0:T(8,128)(2,1)S(1)} %get-tuple-element.52), channel_id=1, source_target_pairs={{0,64},{1,65},{2,66},{3,67},{4,68},{5,69},{6,70},{7,71},{8,72},{9,... | collective-permute-start | bytes 1179656 | tf_op jit(solution)/shard_map/ppermute | solution.py:378
  242.8 26.0 %all-to-all-start.4 = ((bf16[16,384,128]{2,1,0:T(8,128)(2,1)}), bf16[16,384,128]{2,1,0:T(8,128)(2,1)S(1)}, u32[]{:S(2)}, u32[]{:S(2)}) async-start(bf16[16,384,128]{2,1,0:T(8,128)(2,1)} %bitcast.38), calls=%async_computation.4 | async-start | bytes 3145728 | tf_op jit(solution)/shard_map/all_to_all | solution.py:307
  249.4 21.1 %collective-permute-start.23 = (bf16[4,2,384,128]{3,2,1,0:T(8,128)(2,1)S(1)}, bf16[4,2,384,128]{3,2,1,0:T(8,128)(2,1)}, u32[]{:S(2)}, u32[]{:S(2)}) collective-permute-start(bf16[4,2,384,128]{3,2,1,0:T(8,128)(2,1)S(1)} %slice_bitcast_fusion), channel_id=1, source_target_pairs={{0,1},{1,0},{2,3},{3,2},{4,5},{5,4},{6,7},{7,6},{8,9},{9,8},{10,11... | collective-permute-start | bytes 2359304 | tf_op jit(solution)/shard_map/ppermute | solution.py:382
  268.8 4.0 %collective-permute-start.19 = (bf16[4,2,384,128]{3,2,1,0:T(8,128)(2,1)S(1)}, bf16[4,2,384,128]{3,2,1,0:T(8,128)(2,1)S(1)}, u32[]{:S(2)}, u32[]{:S(2)}) collective-permute-start(bf16[4,2,384,128]{3,2,1,0:T(8,128)(2,1)S(1)} %slice_bitcast_fusion.1), channel_id=1, source_target_pairs={{0,1},{1,0},{2,3},{3,2},{4,5},{5,4},{6,7},{7,6},{8,9},{9,8},{10,11... | collective-permute-start | bytes 2359304 | tf_op jit(solution)/shard_map/ppermute | solution.py:382
  (8 other events, 34.5 us)

commit v4 on v3

--- a/solution.py
+++ b/solution.py
@@ -150,7 +150,7 @@
     bf16 = jnp.bfloat16
     return pl.pallas_call(
         functools.partial(attention_kernel, head, own, parts),
-        compiler_params=pltpu.CompilerParams(vmem_limit_bytes=50 << 20),
+        compiler_params=pltpu.CompilerParams(vmem_limit_bytes=51 << 20),
         grid_spec=pltpu.PrefetchScalarGridSpec(
             num_scalar_prefetch=1,
             grid=(1,),
@@ -217,7 +217,7 @@
     block = (2, count, RES, HEAD_DIM)
     return pl.pallas_call(
         functools.partial(pack_kernel, heads),
-        compiler_params=pltpu.CompilerParams(vmem_limit_bytes=58 << 20),
+        compiler_params=pltpu.CompilerParams(vmem_limit_bytes=51 << 20),
         grid_spec=pltpu.PrefetchScalarGridSpec(
             num_scalar_prefetch=1,
             grid=(1,),
@@ -269,7 +269,7 @@
     hbm_spec = pl.BlockSpec(memory_space=pltpu.HBM)
     return pl.pallas_call(
         functools.partial(unpack_kernel, head),
-        compiler_params=pltpu.CompilerParams(vmem_limit_bytes=58 << 20),
+        compiler_params=pltpu.CompilerParams(vmem_limit_bytes=51 << 20),
         grid_spec=pltpu.PrefetchScalarGridSpec(
             num_scalar_prefetch=1,
             grid=(1,),
@@ -340,10 +340,11 @@
         field = plane_exchange(joined.reshape(16, len(fields), RES, HEAD_DIM))
         return field.reshape(RING, RING, len(fields), RES, HEAD_DIM)
 
+    late_queries, infos = lax.optimization_barrier((queries, infos))
     landed = [
         into((queries,), (0,)),
         into((grad_out,), (0,)),
-        into((queries,), (1,)),
+        into((late_queries,), (1,)),
         into((grad_out,), (1,)),
     ]
 

time: 278 us -> 273 us (0.982)
  waiting for transfers between devices: 122 us -> 115 us
  starting transfers between devices: 65.9 us -> 70.6 us
  Pallas kernels: 61.5 us -> 65.9 us
  other arithmetic: 4.52 us -> 0.28 us
    ppermute x12, waiting for transfers between devices: 22 us -> 15.4 us  [spread(): chunks[s] = lax.ppermute(piece, BOTH, shift(s))]
    ppermute x2, starting transfers between devices: 1.75 us -> 6.37 us  [body(): got = lax.ppermute(home[:, 1], BOTH, SWAP)]
    all_to_all x6, waiting for transfers between devices: 59.6 us -> 56.7 us  [plane_exchange(): lax.all_to_all(field, BOTH, 0, 0, axis_index_groups=PLANES, tiled=True)]
  transfers between devices with their start and end apart: 30 -> 30, of which waited for: 13 -> 17; matrix products, arithmetic and copies ran while one was open for 9% -> 5% of each run, Pallas kernels for 21% -> 22%
where the time goes in v4:
time: 273 us; the launch traced here: 272 us
  waiting for transfers between devices  115 us (42%)
  starting transfers between devices  70.6 us (26%)
  Pallas kernels  65.9 us (24%)
  local copies, waits for them, and re-layouts  18.8 us (7%)
    all_to_all x6, waiting for transfers between devices, plane_exchange(): lax.all_to_all(field, BOTH, 0, 0, axis_index_groups=PLANES, tiled=True)  56.7 us
    pallas_call x6, Pallas kernels, attention_backward(): pl.pallas_call(functools.partial(attention_kernel, head, own, parts), com...  47.1 us
    all_to_all x6, starting transfers between devices, plane_exchange(): lax.all_to_all(field, BOTH, 0, 0, axis_index_groups=PLANES, tiled=True)  38.6 us
    ppermute x6, waiting for transfers between devices, body(): dq = lax.ppermute(dq, BOTH, shift(-s))  34.3 us
    ppermute x12, waiting for transfers between devices, spread(): chunks[s] = lax.ppermute(piece, BOTH, shift(s))  15.4 us
    ppermute x12, starting transfers between devices, spread(): chunks[s] = lax.ppermute(piece, BOTH, shift(s))  14.4 us
    pallas_call x4, Pallas kernels, pack(): pl.pallas_call(functools.partial(pack_kernel, heads), compiler_params=plt...  12.1 us
    ppermute x6, starting transfers between devices, body(): dq = lax.ppermute(dq, BOTH, shift(-s))  9.56 us
  transfers between devices with their start and end apart: 30, of which 17 were waited for; matrix products, arithmetic and copies ran while one was open for 5% of the time, Pallas kernels for 22%

profile of v4, /device:TPU:1, one launch (start us, length us, event | category | flops | bytes accessed | tf_op | source)
XLA Modules:
  0.0 272.0 jit_solution(2474476587371578887)
XLA Ops:
  3.2 3.0 %shard_map.85 = (bf16[4,2,2,1,384,128]{5,4,3,2,1,0:T(8,128)(2,1)}, bf16[4,2,1,384,128]{4,3,2,1,0:T(8,128)(2,1)S(1)}) custom-call(s32[1]{0:T(128)} %bitcast.core, bf16[8,384,512]{2,1,0:T(8,128)(2,1)} %bitcast.90), custom_call_target="tpu_custom_call" | custom-call | tf_op jit(solution)/shard_map/pallas_call | solution.py:218
  10.6 9.0 %all-to-all-start = ((bf16[16,1,384,128]{3,2,1,0:T(8,128)(2,1)}), bf16[16,1,384,128]{3,2,1,0:T(8,128)(2,1)S(1)}, u32[]{:S(2)}, u32[]{:S(2)}) async-start(bf16[16,1,384,128]{3,2,1,0:T(8,128)(2,1)} %bitcast.5), calls=%async_computation | async-start | bytes 3145728 | tf_op jit(solution)/shard_map/all_to_all | solution.py:307
  19.6 3.0 %shard_map.87 = (bf16[4,2,2,1,384,128]{5,4,3,2,1,0:T(8,128)(2,1)}, bf16[4,2,1,384,128]{4,3,2,1,0:T(8,128)(2,1)S(1)}) custom-call(s32[1]{0:T(128)} %bitcast.core, bf16[8,384,512]{2,1,0:T(8,128)(2,1)} %bitcast.91), custom_call_target="tpu_custom_call" | custom-call | tf_op jit(solution)/shard_map/pallas_call | solution.py:218
  22.7 2.3 collective-permute-done.2
  26.0 13.9 %all-to-all-done = bf16[16,1,384,128]{3,2,1,0:T(8,128)(2,1)S(1)} async-done(((bf16[16,1,384,128]{3,2,1,0:T(8,128)(2,1)}), bf16[16,1,384,128]{3,2,1,0:T(8,128)(2,1)S(1)}, u32[]{:S(2)}, u32[]{:S(2)}) %all-to-all-start) | async-done | bytes 1572896 | tf_op jit(solution)/shard_map/all_to_all | solution.py:307
  39.9 7.0 %all-to-all-start.2 = ((bf16[16,1,384,128]{3,2,1,0:T(8,128)(2,1)}), bf16[16,1,384,128]{3,2,1,0:T(8,128)(2,1)}, u32[]{:S(2)}, u32[]{:S(2)}) async-start(bf16[16,1,384,128]{3,2,1,0:T(8,128)(2,1)} %bitcast.17), calls=%async_computation.2 | async-start | bytes 3145728 | tf_op jit(solution)/shard_map/all_to_all | solution.py:307
  46.8 3.0 %shard_map.88 = (bf16[4,2,2,1,384,128]{5,4,3,2,1,0:T(8,128)(2,1)}, bf16[4,2,1,384,128]{4,3,2,1,0:T(8,128)(2,1)S(1)}) custom-call(s32[1]{0:T(128)} %bitcast.core, bf16[8,384,512]{2,1,0:T(8,128)(2,1)} %bitcast.92), custom_call_target="tpu_custom_call" | custom-call | tf_op jit(solution)/shard_map/pallas_call | solution.py:218
  53.2 14.1 %all-to-all-done.2 = bf16[16,1,384,128]{3,2,1,0:T(8,128)(2,1)} async-done(((bf16[16,1,384,128]{3,2,1,0:T(8,128)(2,1)}), bf16[16,1,384,128]{3,2,1,0:T(8,128)(2,1)}, u32[]{:S(2)}, u32[]{:S(2)}) %all-to-all-start.2) | async-done | bytes 1572896 | tf_op jit(solution)/shard_map/all_to_all | solution.py:307
  67.3 6.8 %all-to-all-start.3 = ((bf16[16,1,384,128]{3,2,1,0:T(8,128)(2,1)}), bf16[16,1,384,128]{3,2,1,0:T(8,128)(2,1)}, u32[]{:S(2)}, u32[]{:S(2)}) async-start(bf16[16,1,384,128]{3,2,1,0:T(8,128)(2,1)} %bitcast.24), calls=%async_computation.3 | async-start | bytes 3145728 | tf_op jit(solution)/shard_map/all_to_all | solution.py:307
  74.2 3.0 %shard_map.86 = (bf16[4,2,2,1,384,128]{5,4,3,2,1,0:T(8,128)(2,1)}, bf16[4,2,1,384,128]{4,3,2,1,0:T(8,128)(2,1)S(1)}) custom-call(s32[1]{0:T(128)} %bitcast.core, bf16[8,384,512]{2,1,0:T(8,128)(2,1)} %bitcast.93), custom_call_target="tpu_custom_call" | custom-call | tf_op jit(solution)/shard_map/pallas_call | solution.py:218
  80.6 14.0 %all-to-all-done.3 = bf16[16,1,384,128]{3,2,1,0:T(8,128)(2,1)} async-done(((bf16[16,1,384,128]{3,2,1,0:T(8,128)(2,1)}), bf16[16,1,384,128]{3,2,1,0:T(8,128)(2,1)}, u32[]{:S(2)}, u32[]{:S(2)}) %all-to-all-start.3) | async-done | bytes 1572896 | tf_op jit(solution)/shard_map/all_to_all | solution.py:307
  94.6 6.7 %all-to-all-start.1 = ((bf16[16,1,384,128]{3,2,1,0:T(8,128)(2,1)}), bf16[16,1,384,128]{3,2,1,0:T(8,128)(2,1)}, u32[]{:S(2)}, u32[]{:S(2)}) async-start(bf16[16,1,384,128]{3,2,1,0:T(8,128)(2,1)} %bitcast.11), calls=%async_computation.1 | async-start | bytes 3145728 | tf_op jit(solution)/shard_map/all_to_all | solution.py:307
  110.4 4.8 %collective-permute-done.8.refs_0_ = bf16[4,384,128]{2,1,0:T(8,128)(2,1)S(1)} collective-permute-done((bf16[4,384,128]{2,1,0:T(8,128)(2,1)S(1)}, bf16[4,384,128]{2,1,0:T(8,128)(2,1)S(1)}, u32[]{:S(2)}, u32[]{:S(2)}) %collective-permute-start.8) | collective-permute-done | bytes 393248 | tf_op jit(solution)/shard_map/ppermute | solution.py:357
  116.7 6.2 %shard_map.89 = (bf16[4,4,384,128]{3,2,1,0:T(8,128)(2,1)}, bf16[7168,256]{1,0:T(8,128)(2,1)}, bf16[7168,256]{1,0:T(8,128)(2,1)}) custom-call(s32[4,4]{1,0:T(4,128)S(1)} %pad_add_fusion.2.info, bf16[4,4,1,384,128]{4,3,2,1,0:T(8,128)(2,1)} %bitcast.18.refs_0_, bf16[4,4,1,384,128]{4,3,2,1,0:T(8,128)(2,1)} %bitcast.25.refs_1_, bf16[7168,256]{1,0:T(8,128)(2,1)} %refs_2_.7, ...), custom_call_target="tpu_custom_call" | custom-call | flops 880803840 | bytes 2752512 | tf_op jit(solution)/shard_map/pallas_call | solution.py:151
  123.3 6.7 %shard_map.90 = (bf16[4,384,128]{2,1,0:T(8,128)(2,1)S(1)}, bf16[7168,256]{1,0:T(8,128)(2,1)}, bf16[7168,256]{1,0:T(8,128)(2,1)}) custom-call(s32[4,4]{1,0:T(4,128)S(1)} %get-tuple-element.48.info, bf16[4,384,128]{2,1,0:T(8,128)(2,1)S(1)} %collective-permute-done.8.refs_0_, ...), custom_call_target="tpu_custom_call", output_to_operand_aliasing={{1}: (5, {}), {2}: (6, {})} | custom-call | flops 880803840 | bytes 2752512 | tf_op jit(solution)/shard_map/pallas_call | solution.py:151
  134.1 7.0 %collective-permute-done.7.refs_3_ = bf16[4,384,128]{2,1,0:T(8,128)(2,1)S(1)} collective-permute-done((bf16[4,384,128]{2,1,0:T(8,128)(2,1)S(1)}, bf16[4,384,128]{2,1,0:T(8,128)(2,1)S(1)}, u32[]{:S(2)}, u32[]{:S(2)}) %collective-permute-start.7) | collective-permute-done | bytes 393248 | tf_op jit(solution)/shard_map/ppermute | solution.py:357
  141.1 10.9 %shard_map.91 = (bf16[4,384,128]{2,1,0:T(8,128)(2,1)S(1)}, bf16[4,384,128]{2,1,0:T(8,128)(2,1)S(1)}, bf16[7168,256]{1,0:T(8,128)(2,1)}, bf16[7168,256]{1,0:T(8,128)(2,1)}) custom-call(s32[4,8]{1,0:T(4,128)S(1)} %fusion.1.info, bf16[4,384,128]{2,1,0:T(8,128)(2,1)S(1)} %collective-permute-done.3.refs_0_, ...), custom_call_target="tpu_custom_call", output_to_operand_aliasing={{2}: (7, {}), {3}: (8, {})} | custom-call | flops 1761607680 | bytes 5505024 | tf_op jit(solution)/shard_map/pallas_call | solution.py:151
  152.0 2.7 collective-permute-start.21
  155.8 2.6 collective-permute-start.11
  158.4 2.3 dynamic-slice_bitcast_fusion
  168.7 23.1 %collective-permute-done.22 = bf16[4,384,128]{2,1,0:T(8,128)(2,1)S(1)} collective-permute-done((bf16[4,384,128]{2,1,0:T(8,128)(2,1)S(1)}, bf16[4,384,128]{2,1,0:T(8,128)(2,1)S(1)}, u32[]{:S(2)}, u32[]{:S(2)}) %collective-permute-start.22) | collective-permute-done | bytes 393248 | tf_op jit(solution)/shard_map/ppermute | solution.py:379
  192.6 4.6 %all-to-all-start.5 = ((bf16[16,384,128]{2,1,0:T(8,128)(2,1)}), bf16[16,384,128]{2,1,0:T(8,128)(2,1)S(1)}, u32[]{:S(2)}, u32[]{:S(2)}) async-start(bf16[16,384,128]{2,1,0:T(8,128)(2,1)} %bitcast.45), calls=%async_computation.5 | async-start | bytes 3145728 | tf_op jit(solution)/shard_map/all_to_all | solution.py:307
  198.0 6.7 %shard_map.92 = (bf16[4,4,384,128]{3,2,1,0:T(8,128)(2,1)S(1)}, bf16[7168,256]{1,0:T(8,128)(2,1)}, bf16[7168,256]{1,0:T(8,128)(2,1)}) custom-call(s32[4,4]{1,0:T(4,128)S(1)} %pad_add_fusion.2.info, bf16[4,4,1,384,128]{4,3,2,1,0:T(8,128)(2,1)} %bitcast.96, bf16[4,4,1,384,128]{4,3,2,1,0:T(8,128)(2,1)} %bitcast.12.refs_1_, ...), custom_call_target="tpu_custom_call", output_to_operand_aliasing={{1}: (5, {}), {2}: (6, {})} | custom-call | flops 880803840 | bytes 2752512 | tf_op jit(solution)/shard_map/pallas_call | solution.py:151
  206.1 10.7 %shard_map.93 = (bf16[4,384,128]{2,1,0:T(8,128)(2,1)S(1)}, bf16[4,384,128]{2,1,0:T(8,128)(2,1)S(1)}, bf16[7168,256]{1,0:T(8,128)(2,1)}, bf16[7168,256]{1,0:T(8,128)(2,1)}) custom-call(s32[4,8]{1,0:T(4,128)S(1)} %fusion.info, bf16[4,384,128]{2,1,0:T(8,128)(2,1)S(1)} %collective-permute-done.10.refs_0_, ...), custom_call_target="tpu_custom_call", output_to_operand_aliasing={{2}: (7, {}), {3}: (8, {})} | custom-call | flops 1761607680 | bytes 5505024 | tf_op jit(solution)/shard_map/pallas_call | solution.py:151
  218.4 5.9 %shard_map.94 = (bf16[4,384,128]{2,1,0:T(8,128)(2,1)S(1)}, bf16[7168,256]{1,0:T(8,128)(2,1)}, bf16[7168,256]{1,0:T(8,128)(2,1)}) custom-call(s32[4,4]{1,0:T(4,128)S(1)} %get-tuple-element.61.info, bf16[4,384,128]{2,1,0:T(8,128)(2,1)S(1)} %collective-permute-done.16.refs_0_, ...), custom_call_target="tpu_custom_call", output_to_operand_aliasing={{1}: (5, {}), {2}: (6, {})} | custom-call | flops 880803840 | bytes 2752512 | tf_op jit(solution)/shard_map/pallas_call | solution.py:151
  224.3 2.7 collective-permute-start.18
  228.4 8.9 %collective-permute-done.18 = bf16[4,384,128]{2,1,0:T(8,128)(2,1)S(1)} collective-permute-done((bf16[4,384,128]{2,1,0:T(8,128)(2,1)S(1)}, bf16[4,384,128]{2,1,0:T(8,128)(2,1)S(1)}, u32[]{:S(2)}, u32[]{:S(2)}) %collective-permute-start.18) | collective-permute-done | bytes 393248 | tf_op jit(solution)/shard_map/ppermute | solution.py:379
  238.5 4.6 %all-to-all-start.4 = ((bf16[16,384,128]{2,1,0:T(8,128)(2,1)}), bf16[16,384,128]{2,1,0:T(8,128)(2,1)S(1)}, u32[]{:S(2)}, u32[]{:S(2)}) async-start(bf16[16,384,128]{2,1,0:T(8,128)(2,1)} %bitcast.89), calls=%async_computation.4 | async-start | bytes 3145728 | tf_op jit(solution)/shard_map/all_to_all | solution.py:307
  245.3 14.6 %all-to-all-done.4 = bf16[16,384,128]{2,1,0:T(8,128)(2,1)S(1)} async-done(((bf16[16,384,128]{2,1,0:T(8,128)(2,1)}), bf16[16,384,128]{2,1,0:T(8,128)(2,1)S(1)}, u32[]{:S(2)}, u32[]{:S(2)}) %all-to-all-start.4) | async-done | bytes 1572896 | tf_op jit(solution)/shard_map/all_to_all | solution.py:307
  260.0 5.1 %collective-permute-start.19 = (bf16[4,2,384,128]{3,2,1,0:T(8,128)(2,1)S(1)}, bf16[4,2,384,128]{3,2,1,0:T(8,128)(2,1)S(1)}, u32[]{:S(2)}, u32[]{:S(2)}) collective-permute-start(bf16[4,2,384,128]{3,2,1,0:T(8,128)(2,1)S(1)} %slice_bitcast_fusion.1), channel_id=1, source_target_pairs={{0,1},{1,0},{2,3},{3,2},{4,5},{5,4},{6,7},{7,6},{8,9},{9,8},{10,11... | collective-permute-start | bytes 2359304 | tf_op jit(solution)/shard_map/ppermute | solution.py:383
  265.0 3.4 %shard_map.95.rest_0_ = bf16[8,384,512]{2,1,0:T(8,128)(2,1)} custom-call(s32[1]{0:T(128)} %bitcast.core, bf16[4,2,2,384,128]{4,3,2,1,0:T(8,128)(2,1)S(1)} %bitcast.86, bf16[4,2,384,128]{3,2,1,0:T(8,128)(2,1)} %collective-permute-done.23.got_ref), custom_call_target="tpu_custom_call" | custom-call | tf_op jit(solution)/shard_map/pallas_call | solution.py:270
  268.4 3.4 %shard_map.96 = bf16[8,384,512]{2,1,0:T(8,128)(2,1)} custom-call(s32[1]{0:T(128)} %bitcast.core, bf16[4,2,2,384,128]{4,3,2,1,0:T(8,128)(2,1)S(1)} %bitcast.88, bf16[4,2,384,128]{3,2,1,0:T(8,128)(2,1)S(1)} %collective-permute-done.19.got_ref, bf16[8,384,512]{2,1,0:T(8,128)(2,1)} %shard_map.95.rest_0_), custom_call_target="tpu_custom_call", output_to_operand_aliasing={{}: (3, {})} | custom-call | tf_op jit(solution)/shard_map/pallas_call | solution.py:270
  (78 shorter events, 48.2 us)
Async XLA Ops:
  6.2 3.4 %collective-permute-start = (bf16[4,2,1,384,128]{4,3,2,1,0:T(8,128)(2,1)S(1)}, bf16[4,2,1,384,128]{4,3,2,1,0:T(8,128)(2,1)S(1)}, u32[]{:S(2)}, u32[]{:S(2)}) collective-permute-start(bf16[4,2,1,384,128]{4,3,2,1,0:T(8,128)(2,1)S(1)} %get-tuple-element.40), channel_id=1, source_target_pairs={{0,1},{1,0},{2,3},{3,2},{4,5},{5,4},{6,7},{7,6},{8,9},{9,8},{10,11... | collective-permute-start | bytes 2359304 | tf_op jit(solution)/shard_map/ppermute | solution.py:338
  10.6 29.3 %all-to-all-start = ((bf16[16,1,384,128]{3,2,1,0:T(8,128)(2,1)}), bf16[16,1,384,128]{3,2,1,0:T(8,128)(2,1)S(1)}, u32[]{:S(2)}, u32[]{:S(2)}) async-start(bf16[16,1,384,128]{3,2,1,0:T(8,128)(2,1)} %bitcast.5), calls=%async_computation | async-start | bytes 3145728 | tf_op jit(solution)/shard_map/all_to_all | solution.py:307
  22.6 2.4 collective-permute-start.2
  39.9 114.8 %copy-start.1 = (bf16[16,1,384,128]{3,2,1,0:T(8,128)(2,1)}, bf16[16,1,384,128]{3,2,1,0:T(8,128)(2,1)S(1)}, u32[]{:S(2)}) copy-start(bf16[16,1,384,128]{3,2,1,0:T(8,128)(2,1)S(1)} %all-to-all-done) | copy-start | bytes 4718596
  39.9 27.5 %all-to-all-start.2 = ((bf16[16,1,384,128]{3,2,1,0:T(8,128)(2,1)}), bf16[16,1,384,128]{3,2,1,0:T(8,128)(2,1)}, u32[]{:S(2)}, u32[]{:S(2)}) async-start(bf16[16,1,384,128]{3,2,1,0:T(8,128)(2,1)} %bitcast.17), calls=%async_computation.2 | async-start | bytes 3145728 | tf_op jit(solution)/shard_map/all_to_all | solution.py:307
  49.8 2.4 collective-permute-start.5
  67.3 27.3 %all-to-all-start.3 = ((bf16[16,1,384,128]{3,2,1,0:T(8,128)(2,1)}), bf16[16,1,384,128]{3,2,1,0:T(8,128)(2,1)}, u32[]{:S(2)}, u32[]{:S(2)}) async-start(bf16[16,1,384,128]{3,2,1,0:T(8,128)(2,1)} %bitcast.24), calls=%async_computation.3 | async-start | bytes 3145728 | tf_op jit(solution)/shard_map/all_to_all | solution.py:307
  77.2 2.4 collective-permute-start.1
  94.6 63.8 %all-to-all-start.1 = ((bf16[16,1,384,128]{3,2,1,0:T(8,128)(2,1)}), bf16[16,1,384,128]{3,2,1,0:T(8,128)(2,1)}, u32[]{:S(2)}, u32[]{:S(2)}) async-start(bf16[16,1,384,128]{3,2,1,0:T(8,128)(2,1)} %bitcast.11), calls=%async_computation.1 | async-start | bytes 3145728 | tf_op jit(solution)/shard_map/all_to_all | solution.py:307
  102.7 12.5 %collective-permute-start.8 = (bf16[4,384,128]{2,1,0:T(8,128)(2,1)S(1)}, bf16[4,384,128]{2,1,0:T(8,128)(2,1)S(1)}, u32[]{:S(2)}, u32[]{:S(2)}) collective-permute-start(bf16[4,384,128]{2,1,0:T(8,128)(2,1)S(1)} %get-tuple-element.80), channel_id=1, source_target_pairs={{0,32},{1,33},{2,34},{3,35},{4,36},{5,37},{6,38},{7,39},{8,40},{9,... | collective-permute-start | bytes 1179656 | tf_op jit(solution)/shard_map/ppermute | solution.py:357
  105.3 18.0 %collective-permute-start.9 = (bf16[4,384,128]{2,1,0:T(8,128)(2,1)S(1)}, bf16[4,384,128]{2,1,0:T(8,128)(2,1)S(1)}, u32[]{:S(2)}, u32[]{:S(2)}) collective-permute-start(bf16[4,384,128]{2,1,0:T(8,128)(2,1)S(1)} %get-tuple-element.77), channel_id=1, source_target_pairs={{0,32},{1,33},{2,34},{3,35},{4,36},{5,37},{6,38},{7,39},{8,40},{9,... | collective-permute-start | bytes 1179656 | tf_op jit(solution)/shard_map/ppermute | solution.py:357
  106.5 24.3 %collective-permute-start.3 = (bf16[4,384,128]{2,1,0:T(8,128)(2,1)S(1)}, bf16[4,384,128]{2,1,0:T(8,128)(2,1)S(1)}, u32[]{:S(2)}, u32[]{:S(2)}) collective-permute-start(bf16[4,384,128]{2,1,0:T(8,128)(2,1)S(1)} %get-tuple-element.82), channel_id=1, source_target_pairs={{0,96},{1,97},{2,98},{3,99},{4,100},{5,101},{6,102},{7,103},{8,104... | collective-permute-start | bytes 1179656 | tf_op jit(solution)/shard_map/ppermute | solution.py:357
  108.0 24.9 %collective-permute-start.4 = (bf16[4,384,128]{2,1,0:T(8,128)(2,1)S(1)}, bf16[4,384,128]{2,1,0:T(8,128)(2,1)S(1)}, u32[]{:S(2)}, u32[]{:S(2)}) collective-permute-start(bf16[4,384,128]{2,1,0:T(8,128)(2,1)S(1)} %get-tuple-element.81), channel_id=1, source_target_pairs={{0,64},{1,65},{2,66},{3,67},{4,68},{5,69},{6,70},{7,71},{8,72},{9,... | collective-permute-start | bytes 1179656 | tf_op jit(solution)/shard_map/ppermute | solution.py:357
  109.2 24.9 %collective-permute-start.6 = (bf16[4,384,128]{2,1,0:T(8,128)(2,1)S(1)}, bf16[4,384,128]{2,1,0:T(8,128)(2,1)S(1)}, u32[]{:S(2)}, u32[]{:S(2)}) collective-permute-start(bf16[4,384,128]{2,1,0:T(8,128)(2,1)S(1)} %get-tuple-element.79), channel_id=1, source_target_pairs={{0,96},{1,97},{2,98},{3,99},{4,100},{5,101},{6,102},{7,103},{8,104... | collective-permute-start | bytes 1179656 | tf_op jit(solution)/shard_map/ppermute | solution.py:357
  115.2 25.9 %collective-permute-start.7 = (bf16[4,384,128]{2,1,0:T(8,128)(2,1)S(1)}, bf16[4,384,128]{2,1,0:T(8,128)(2,1)S(1)}, u32[]{:S(2)}, u32[]{:S(2)}) collective-permute-start(bf16[4,384,128]{2,1,0:T(8,128)(2,1)S(1)} %get-tuple-element.78), channel_id=1, source_target_pairs={{0,64},{1,65},{2,66},{3,67},{4,68},{5,69},{6,70},{7,71},{8,72},{9,... | collective-permute-start | bytes 1179656 | tf_op jit(solution)/shard_map/ppermute | solution.py:357
  130.0 31.2 %collective-permute-start.20 = (bf16[4,384,128]{2,1,0:T(8,128)(2,1)S(1)}, bf16[4,384,128]{2,1,0:T(8,128)(2,1)}, u32[]{:S(2)}, u32[]{:S(2)}) collective-permute-start(bf16[4,384,128]{2,1,0:T(8,128)(2,1)S(1)} %get-tuple-element.66), channel_id=1, source_target_pairs={{0,96},{1,97},{2,98},{3,99},{4,100},{5,101},{6,102},{7,103},{8,104... | collective-permute-start | bytes 1179656 | tf_op jit(solution)/shard_map/ppermute | solution.py:379
  152.0 13.8 %collective-permute-start.21 = (bf16[4,384,128]{2,1,0:T(8,128)(2,1)S(1)}, bf16[4,384,128]{2,1,0:T(8,128)(2,1)}, u32[]{:S(2)}, u32[]{:S(2)}) collective-permute-start(bf16[4,384,128]{2,1,0:T(8,128)(2,1)S(1)} %get-tuple-element.67), channel_id=1, source_target_pairs={{0,32},{1,33},{2,34},{3,35},{4,36},{5,37},{6,38},{7,39},{8,40},{9,... | collective-permute-start | bytes 1179656 | tf_op jit(solution)/shard_map/ppermute | solution.py:379
  155.8 48.9 %collective-permute-start.10 = (bf16[4,384,128]{2,1,0:T(8,128)(2,1)}, bf16[4,384,128]{2,1,0:T(8,128)(2,1)S(1)}, u32[]{:S(2)}, u32[]{:S(2)}) collective-permute-start(bf16[4,384,128]{2,1,0:T(8,128)(2,1)} %get-tuple-element.76), channel_id=1, source_target_pairs={{0,32},{1,33},{2,34},{3,35},{4,36},{5,37},{6,38},{7,39},{8,40},{9,... | collective-permute-start | bytes 1179656 | tf_op jit(solution)/shard_map/ppermute | solution.py:357
  155.8 50.3 %collective-permute-start.11 = (bf16[4,384,128]{2,1,0:T(8,128)(2,1)}, bf16[4,384,128]{2,1,0:T(8,128)(2,1)}, u32[]{:S(2)}, u32[]{:S(2)}) collective-permute-start(bf16[4,384,128]{2,1,0:T(8,128)(2,1)} %get-tuple-element.75), channel_id=1, source_target_pairs={{0,96},{1,97},{2,98},{3,99},{4,100},{5,101},{6,102},{7,103},{8,104... | collective-permute-start | bytes 1179656 | tf_op jit(solution)/shard_map/ppermute | solution.py:357
  160.7 45.4 %collective-permute-start.12 = (bf16[4,384,128]{2,1,0:T(8,128)(2,1)}, bf16[4,384,128]{2,1,0:T(8,128)(2,1)}, u32[]{:S(2)}, u32[]{:S(2)}) collective-permute-start(bf16[4,384,128]{2,1,0:T(8,128)(2,1)} %get-tuple-element.73), channel_id=1, source_target_pairs={{0,32},{1,33},{2,34},{3,35},{4,36},{5,37},{6,38},{7,39},{8,40},{9,... | collective-permute-start | bytes 1179656 | tf_op jit(solution)/shard_map/ppermute | solution.py:357
  161.1 30.7 %collective-permute-start.22 = (bf16[4,384,128]{2,1,0:T(8,128)(2,1)S(1)}, bf16[4,384,128]{2,1,0:T(8,128)(2,1)S(1)}, u32[]{:S(2)}, u32[]{:S(2)}) collective-permute-start(bf16[4,384,128]{2,1,0:T(8,128)(2,1)S(1)} %get-tuple-element.68), channel_id=1, source_target_pairs={{0,64},{1,65},{2,66},{3,67},{4,68},{5,69},{6,70},{7,71},{8,72},{9,... | collective-permute-start | bytes 1179656 | tf_op jit(solution)/shard_map/ppermute | solution.py:379
  165.8 40.3 %collective-permute-start.13 = (bf16[4,384,128]{2,1,0:T(8,128)(2,1)}, bf16[4,384,128]{2,1,0:T(8,128)(2,1)}, u32[]{:S(2)}, u32[]{:S(2)}) collective-permute-start(bf16[4,384,128]{2,1,0:T(8,128)(2,1)} %get-tuple-element.72), channel_id=1, source_target_pairs={{0,96},{1,97},{2,98},{3,99},{4,100},{5,101},{6,102},{7,103},{8,104... | collective-permute-start | bytes 1179656 | tf_op jit(solution)/shard_map/ppermute | solution.py:357
  192.6 44.7 %all-to-all-start.5 = ((bf16[16,384,128]{2,1,0:T(8,128)(2,1)}), bf16[16,384,128]{2,1,0:T(8,128)(2,1)S(1)}, u32[]{:S(2)}, u32[]{:S(2)}) async-start(bf16[16,384,128]{2,1,0:T(8,128)(2,1)} %bitcast.45), calls=%async_computation.5 | async-start | bytes 3145728 | tf_op jit(solution)/shard_map/all_to_all | solution.py:307
  197.2 21.1 %collective-permute-start.16 = (bf16[4,384,128]{2,1,0:T(8,128)(2,1)}, bf16[4,384,128]{2,1,0:T(8,128)(2,1)S(1)}, u32[]{:S(2)}, u32[]{:S(2)}) collective-permute-start(bf16[4,384,128]{2,1,0:T(8,128)(2,1)} %get-tuple-element.74), channel_id=1, source_target_pairs={{0,64},{1,65},{2,66},{3,67},{4,68},{5,69},{6,70},{7,71},{8,72},{9,... | collective-permute-start | bytes 1179656 | tf_op jit(solution)/shard_map/ppermute | solution.py:357
  198.0 6.7 %copy-start.2 = (bf16[4,384,128]{2,1,0:T(8,128)(2,1)S(1)}, bf16[4,384,128]{2,1,0:T(8,128)(2,1)}, u32[]{:S(2)}) copy-start(bf16[4,384,128]{2,1,0:T(8,128)(2,1)} %get-tuple-element.71) | copy-start | bytes 1179652
  204.7 13.7 %collective-permute-start.17 = (bf16[4,384,128]{2,1,0:T(8,128)(2,1)S(1)}, bf16[4,384,128]{2,1,0:T(8,128)(2,1)S(1)}, u32[]{:S(2)}, u32[]{:S(2)}) collective-permute-start(bf16[4,384,128]{2,1,0:T(8,128)(2,1)S(1)} %copy-done.2), channel_id=1, source_target_pairs={{0,64},{1,65},{2,66},{3,67},{4,68},{5,69},{6,70},{7,71},{8,72},{9,... | collective-permute-start | bytes 1179656 | tf_op jit(solution)/shard_map/ppermute | solution.py:357
  216.8 10.1 %collective-permute-start.14 = (bf16[4,384,128]{2,1,0:T(8,128)(2,1)S(1)}, bf16[4,384,128]{2,1,0:T(8,128)(2,1)S(1)}, u32[]{:S(2)}, u32[]{:S(2)}) collective-permute-start(bf16[4,384,128]{2,1,0:T(8,128)(2,1)S(1)} %get-tuple-element.59), channel_id=1, source_target_pairs={{0,96},{1,97},{2,98},{3,99},{4,100},{5,101},{6,102},{7,103},{8,104... | collective-permute-start | bytes 1179656 | tf_op jit(solution)/shard_map/ppermute | solution.py:379
  216.9 11.4 %collective-permute-start.15 = (bf16[4,384,128]{2,1,0:T(8,128)(2,1)S(1)}, bf16[4,384,128]{2,1,0:T(8,128)(2,1)S(1)}, u32[]{:S(2)}, u32[]{:S(2)}) collective-permute-start(bf16[4,384,128]{2,1,0:T(8,128)(2,1)S(1)} %get-tuple-element.60), channel_id=1, source_target_pairs={{0,32},{1,33},{2,34},{3,35},{4,36},{5,37},{6,38},{7,39},{8,40},{9,... | collective-permute-start | bytes 1179656 | tf_op jit(solution)/shard_map/ppermute | solution.py:379
  224.3 13.0 %collective-permute-start.18 = (bf16[4,384,128]{2,1,0:T(8,128)(2,1)S(1)}, bf16[4,384,128]{2,1,0:T(8,128)(2,1)S(1)}, u32[]{:S(2)}, u32[]{:S(2)}) collective-permute-start(bf16[4,384,128]{2,1,0:T(8,128)(2,1)S(1)} %get-tuple-element.64), channel_id=1, source_target_pairs={{0,64},{1,65},{2,66},{3,67},{4,68},{5,69},{6,70},{7,71},{8,72},{9,... | collective-permute-start | bytes 1179656 | tf_op jit(solution)/shard_map/ppermute | solution.py:379
  238.5 21.4 %all-to-all-start.4 = ((bf16[16,384,128]{2,1,0:T(8,128)(2,1)}), bf16[16,384,128]{2,1,0:T(8,128)(2,1)S(1)}, u32[]{:S(2)}, u32[]{:S(2)}) async-start(bf16[16,384,128]{2,1,0:T(8,128)(2,1)} %bitcast.89), calls=%async_computation.4 | async-start | bytes 3145728 | tf_op jit(solution)/shard_map/all_to_all | solution.py:307
  244.0 21.1 %collective-permute-start.23 = (bf16[4,2,384,128]{3,2,1,0:T(8,128)(2,1)}, bf16[4,2,384,128]{3,2,1,0:T(8,128)(2,1)}, u32[]{:S(2)}, u32[]{:S(2)}) collective-permute-start(bf16[4,2,384,128]{3,2,1,0:T(8,128)(2,1)} %slice_bitcast_fusion), channel_id=1, source_target_pairs={{0,1},{1,0},{2,3},{3,2},{4,5},{5,4},{6,7},{7,6},{8,9},{9,8},{10,11... | collective-permute-start | bytes 2359304 | tf_op jit(solution)/shard_map/ppermute | solution.py:383
  260.0 8.5 %collective-permute-start.19 = (bf16[4,2,384,128]{3,2,1,0:T(8,128)(2,1)S(1)}, bf16[4,2,384,128]{3,2,1,0:T(8,128)(2,1)S(1)}, u32[]{:S(2)}, u32[]{:S(2)}) collective-permute-start(bf16[4,2,384,128]{3,2,1,0:T(8,128)(2,1)S(1)} %slice_bitcast_fusion.1), channel_id=1, source_target_pairs={{0,1},{1,0},{2,3},{3,2},{4,5},{5,4},{6,7},{7,6},{8,9},{9,8},{10,11... | collective-permute-start | bytes 2359304 | tf_op jit(solution)/shard_map/ppermute | solution.py:383
  (1 other events, 1.1 us)

commit v5 on v4

--- a/solution.py
+++ b/solution.py
@@ -236,25 +236,24 @@
     )(core, *[field.reshape(8, RES, -1) for field in fields])
 
 
-def unpack_kernel(head, core, home_ref, got_ref, *rest):
+def unpack_kernel(head, own, core, field_ref, *rest):
     out_ref, held, sems_in, sems_out = rest[-4:]
     c = core[0]
-    steps = [(w, y) for w in range(2) for y in range(RING)]
     ins, outs = [], []
-    for n, (w, y) in enumerate(steps):
+    for y in range(RING):
         ins.append(
             pltpu.make_async_copy(
-                home_ref.at[y, 0] if w == 0 else got_ref.at[y], held.at[w, y], sems_in.at[n]
+                field_ref.at[y, 0] if own else field_ref.at[y], held.at[y], sems_in.at[y]
             )
         )
         ins[-1].start()
-    for n, (w, y) in enumerate(steps):
+    for n in range(RING):
         ins[n].wait()
-        t = 2 * y + (c if w == 0 else 1 - c)
+        t = 2 * n + (c if own else 1 - c)
         for b in range(2):
             outs.append(
                 pltpu.make_async_copy(
-                    held.at[w, y, b],
+                    held.at[n, b],
                     out_ref.at[t, :, (2 * b + head) * HEAD_DIM : (2 * b + head + 1) * HEAD_DIM],
                     sems_out.at[n, b],
                 )
@@ -264,26 +263,26 @@
         out.wait()
 
 
-def unpack(core, head, home, got, shape, held):
+def unpack(core, head, own, field, shape, held):
     any_spec = pl.BlockSpec(memory_space=pl.ANY)
     hbm_spec = pl.BlockSpec(memory_space=pltpu.HBM)
     return pl.pallas_call(
-        functools.partial(unpack_kernel, head),
+        functools.partial(unpack_kernel, head, own),
         compiler_params=pltpu.CompilerParams(vmem_limit_bytes=51 << 20),
         grid_spec=pltpu.PrefetchScalarGridSpec(
             num_scalar_prefetch=1,
             grid=(1,),
-            in_specs=[any_spec] * 2 + [hbm_spec] * len(held),
+            in_specs=[any_spec] + [hbm_spec] * len(held),
             out_specs=hbm_spec,
             scratch_shapes=[
-                pltpu.VMEM((2, RING, 2, RES, HEAD_DIM), jnp.bfloat16),
-                pltpu.SemaphoreType.DMA((2 * RING,)),
-                pltpu.SemaphoreType.DMA((2 * RING, 2)),
+                pltpu.VMEM((RING, 2, RES, HEAD_DIM), jnp.bfloat16),
+                pltpu.SemaphoreType.DMA((RING,)),
+                pltpu.SemaphoreType.DMA((RING, 2)),
             ],
         ),
         out_shape=jax.ShapeDtypeStruct((8, RES, shape[1]), jnp.bfloat16),
-        input_output_aliases={3: 0} if held else {},
-    )(core, home, got, *held)
+        input_output_aliases={2: 0} if held else {},
+    )(core, field, *held)
 
 
 def device(x, y, z, core):
@@ -381,7 +380,8 @@
         home = plane_exchange(back.reshape(16, RES, HEAD_DIM))
         home = home.reshape(RING, 2, 2, RES, HEAD_DIM)
         got = lax.ppermute(home[:, 1], BOTH, SWAP)
-        query_grads = (unpack(core, h, home, got, queries.shape, query_grads),)
+        query_grads = (unpack(core, h, True, home, queries.shape, query_grads),)
+        query_grads = (unpack(core, h, False, got, queries.shape, query_grads),)
     return (query_grads[0].reshape(queries.shape), *grads)
 
 

time: 273 us -> 274 us (level)
    pallas_call x2 -> x4, Pallas kernels: 6.74 us -> 7.93 us  [unpack(): pl.pallas_call(functools.partial(unpack_kernel, head, own), compiler_para...]
  transfers between devices with their start and end apart: 30 -> 30, of which waited for: 17 -> 17; matrix products, arithmetic and copies ran while one was open for 5% -> 5% of each run, Pallas kernels for 22% -> 23%
where the time goes in v5:
time: 274 us; the launch traced here: 273 us
  waiting for transfers between devices  115 us (42%)
  starting transfers between devices  70.6 us (26%)
  Pallas kernels  67.1 us (24%)
  local copies, waits for them, and re-layouts  18.8 us (7%)
    all_to_all x6, waiting for transfers between devices, plane_exchange(): lax.all_to_all(field, BOTH, 0, 0, axis_index_groups=PLANES, tiled=True)  56.7 us
    pallas_call x6, Pallas kernels, attention_backward(): pl.pallas_call(functools.partial(attention_kernel, head, own, parts), com...  47.1 us
    all_to_all x6, starting transfers between devices, plane_exchange(): lax.all_to_all(field, BOTH, 0, 0, axis_index_groups=PLANES, tiled=True)  38.6 us
    ppermute x6, waiting for transfers between devices, body(): dq = lax.ppermute(dq, BOTH, shift(-s))  34.3 us
    ppermute x12, waiting for transfers between devices, spread(): chunks[s] = lax.ppermute(piece, BOTH, shift(s))  15.4 us
    ppermute x12, starting transfers between devices, spread(): chunks[s] = lax.ppermute(piece, BOTH, shift(s))  14.4 us
    pallas_call x4, Pallas kernels, pack(): pl.pallas_call(functools.partial(pack_kernel, heads), compiler_params=plt...  12.1 us
    ppermute x6, starting transfers between devices, body(): dq = lax.ppermute(dq, BOTH, shift(-s))  9.56 us
  transfers between devices with their start and end apart: 30, of which 17 were waited for; matrix products, arithmetic and copies ran while one was open for 5% of the time, Pallas kernels for 23%

profile of v5, /device:TPU:1, one launch (start us, length us, event | category | flops | bytes accessed | tf_op | source)
XLA Modules:
  0.0 273.2 jit_solution(1283963214034896831)
XLA Ops:
  3.2 3.0 %shard_map.85 = (bf16[4,2,2,1,384,128]{5,4,3,2,1,0:T(8,128)(2,1)}, bf16[4,2,1,384,128]{4,3,2,1,0:T(8,128)(2,1)S(1)}) custom-call(s32[1]{0:T(128)} %bitcast.core, bf16[8,384,512]{2,1,0:T(8,128)(2,1)} %bitcast.91), custom_call_target="tpu_custom_call" | custom-call | tf_op jit(solution)/shard_map/pallas_call | solution.py:218
  10.6 9.0 %all-to-all-start = ((bf16[16,1,384,128]{3,2,1,0:T(8,128)(2,1)}), bf16[16,1,384,128]{3,2,1,0:T(8,128)(2,1)S(1)}, u32[]{:S(2)}, u32[]{:S(2)}) async-start(bf16[16,1,384,128]{3,2,1,0:T(8,128)(2,1)} %bitcast.5), calls=%async_computation | async-start | bytes 3145728 | tf_op jit(solution)/shard_map/all_to_all | solution.py:306
  19.6 3.0 %shard_map.87 = (bf16[4,2,2,1,384,128]{5,4,3,2,1,0:T(8,128)(2,1)}, bf16[4,2,1,384,128]{4,3,2,1,0:T(8,128)(2,1)S(1)}) custom-call(s32[1]{0:T(128)} %bitcast.core, bf16[8,384,512]{2,1,0:T(8,128)(2,1)} %bitcast.92), custom_call_target="tpu_custom_call" | custom-call | tf_op jit(solution)/shard_map/pallas_call | solution.py:218
  22.7 2.3 collective-permute-done.2
  26.0 13.9 %all-to-all-done = bf16[16,1,384,128]{3,2,1,0:T(8,128)(2,1)S(1)} async-done(((bf16[16,1,384,128]{3,2,1,0:T(8,128)(2,1)}), bf16[16,1,384,128]{3,2,1,0:T(8,128)(2,1)S(1)}, u32[]{:S(2)}, u32[]{:S(2)}) %all-to-all-start) | async-done | bytes 1572896 | tf_op jit(solution)/shard_map/all_to_all | solution.py:306
  39.9 7.0 %all-to-all-start.2 = ((bf16[16,1,384,128]{3,2,1,0:T(8,128)(2,1)}), bf16[16,1,384,128]{3,2,1,0:T(8,128)(2,1)}, u32[]{:S(2)}, u32[]{:S(2)}) async-start(bf16[16,1,384,128]{3,2,1,0:T(8,128)(2,1)} %bitcast.17), calls=%async_computation.2 | async-start | bytes 3145728 | tf_op jit(solution)/shard_map/all_to_all | solution.py:306
  46.8 3.0 %shard_map.88 = (bf16[4,2,2,1,384,128]{5,4,3,2,1,0:T(8,128)(2,1)}, bf16[4,2,1,384,128]{4,3,2,1,0:T(8,128)(2,1)S(1)}) custom-call(s32[1]{0:T(128)} %bitcast.core, bf16[8,384,512]{2,1,0:T(8,128)(2,1)} %bitcast.93), custom_call_target="tpu_custom_call" | custom-call | tf_op jit(solution)/shard_map/pallas_call | solution.py:218
  49.9 2.3 collective-permute-done.5
  53.2 14.1 %all-to-all-done.2 = bf16[16,1,384,128]{3,2,1,0:T(8,128)(2,1)} async-done(((bf16[16,1,384,128]{3,2,1,0:T(8,128)(2,1)}), bf16[16,1,384,128]{3,2,1,0:T(8,128)(2,1)}, u32[]{:S(2)}, u32[]{:S(2)}) %all-to-all-start.2) | async-done | bytes 1572896 | tf_op jit(solution)/shard_map/all_to_all | solution.py:306
  67.3 6.8 %all-to-all-start.3 = ((bf16[16,1,384,128]{3,2,1,0:T(8,128)(2,1)}), bf16[16,1,384,128]{3,2,1,0:T(8,128)(2,1)}, u32[]{:S(2)}, u32[]{:S(2)}) async-start(bf16[16,1,384,128]{3,2,1,0:T(8,128)(2,1)} %bitcast.24), calls=%async_computation.3 | async-start | bytes 3145728 | tf_op jit(solution)/shard_map/all_to_all | solution.py:306
  74.2 3.0 %shard_map.86 = (bf16[4,2,2,1,384,128]{5,4,3,2,1,0:T(8,128)(2,1)}, bf16[4,2,1,384,128]{4,3,2,1,0:T(8,128)(2,1)S(1)}) custom-call(s32[1]{0:T(128)} %bitcast.core, bf16[8,384,512]{2,1,0:T(8,128)(2,1)} %bitcast.94), custom_call_target="tpu_custom_call" | custom-call | tf_op jit(solution)/shard_map/pallas_call | solution.py:218
  77.3 2.3 collective-permute-done.1
  80.6 14.0 %all-to-all-done.3 = bf16[16,1,384,128]{3,2,1,0:T(8,128)(2,1)} async-done(((bf16[16,1,384,128]{3,2,1,0:T(8,128)(2,1)}), bf16[16,1,384,128]{3,2,1,0:T(8,128)(2,1)}, u32[]{:S(2)}, u32[]{:S(2)}) %all-to-all-start.3) | async-done | bytes 1572896 | tf_op jit(solution)/shard_map/all_to_all | solution.py:306
  94.6 6.7 %all-to-all-start.1 = ((bf16[16,1,384,128]{3,2,1,0:T(8,128)(2,1)}), bf16[16,1,384,128]{3,2,1,0:T(8,128)(2,1)}, u32[]{:S(2)}, u32[]{:S(2)}) async-start(bf16[16,1,384,128]{3,2,1,0:T(8,128)(2,1)} %bitcast.11), calls=%async_computation.1 | async-start | bytes 3145728 | tf_op jit(solution)/shard_map/all_to_all | solution.py:306
  110.4 4.8 %collective-permute-done.8.refs_0_ = bf16[4,384,128]{2,1,0:T(8,128)(2,1)S(1)} collective-permute-done((bf16[4,384,128]{2,1,0:T(8,128)(2,1)S(1)}, bf16[4,384,128]{2,1,0:T(8,128)(2,1)S(1)}, u32[]{:S(2)}, u32[]{:S(2)}) %collective-permute-start.8) | collective-permute-done | bytes 393248 | tf_op jit(solution)/shard_map/ppermute | solution.py:356
  116.7 6.2 %shard_map.89 = (bf16[4,4,384,128]{3,2,1,0:T(8,128)(2,1)}, bf16[7168,256]{1,0:T(8,128)(2,1)}, bf16[7168,256]{1,0:T(8,128)(2,1)}) custom-call(s32[4,4]{1,0:T(4,128)S(1)} %pad_add_fusion.2.info, bf16[4,4,1,384,128]{4,3,2,1,0:T(8,128)(2,1)} %bitcast.18.refs_0_, bf16[4,4,1,384,128]{4,3,2,1,0:T(8,128)(2,1)} %bitcast.25.refs_1_, bf16[7168,256]{1,0:T(8,128)(2,1)} %refs_2_.7, ...), custom_call_target="tpu_custom_call" | custom-call | flops 880803840 | bytes 2752512 | tf_op jit(solution)/shard_map/pallas_call | solution.py:151
  123.3 6.7 %shard_map.90 = (bf16[4,384,128]{2,1,0:T(8,128)(2,1)S(1)}, bf16[7168,256]{1,0:T(8,128)(2,1)}, bf16[7168,256]{1,0:T(8,128)(2,1)}) custom-call(s32[4,4]{1,0:T(4,128)S(1)} %get-tuple-element.48.info, bf16[4,384,128]{2,1,0:T(8,128)(2,1)S(1)} %collective-permute-done.8.refs_0_, ...), custom_call_target="tpu_custom_call", output_to_operand_aliasing={{1}: (5, {}), {2}: (6, {})} | custom-call | flops 880803840 | bytes 2752512 | tf_op jit(solution)/shard_map/pallas_call | solution.py:151
  134.1 7.0 %collective-permute-done.7.refs_3_ = bf16[4,384,128]{2,1,0:T(8,128)(2,1)S(1)} collective-permute-done((bf16[4,384,128]{2,1,0:T(8,128)(2,1)S(1)}, bf16[4,384,128]{2,1,0:T(8,128)(2,1)S(1)}, u32[]{:S(2)}, u32[]{:S(2)}) %collective-permute-start.7) | collective-permute-done | bytes 393248 | tf_op jit(solution)/shard_map/ppermute | solution.py:356
  141.1 10.9 %shard_map.91 = (bf16[4,384,128]{2,1,0:T(8,128)(2,1)S(1)}, bf16[4,384,128]{2,1,0:T(8,128)(2,1)S(1)}, bf16[7168,256]{1,0:T(8,128)(2,1)}, bf16[7168,256]{1,0:T(8,128)(2,1)}) custom-call(s32[4,8]{1,0:T(4,128)S(1)} %fusion.1.info, bf16[4,384,128]{2,1,0:T(8,128)(2,1)S(1)} %collective-permute-done.3.refs_0_, ...), custom_call_target="tpu_custom_call", output_to_operand_aliasing={{2}: (7, {}), {3}: (8, {})} | custom-call | flops 1761607680 | bytes 5505024 | tf_op jit(solution)/shard_map/pallas_call | solution.py:151
  152.0 2.7 collective-permute-start.21
  155.8 2.6 collective-permute-start.11
  158.4 2.3 dynamic-slice_bitcast_fusion
  168.7 23.1 %collective-permute-done.22 = bf16[4,384,128]{2,1,0:T(8,128)(2,1)S(1)} collective-permute-done((bf16[4,384,128]{2,1,0:T(8,128)(2,1)S(1)}, bf16[4,384,128]{2,1,0:T(8,128)(2,1)S(1)}, u32[]{:S(2)}, u32[]{:S(2)}) %collective-permute-start.22) | collective-permute-done | bytes 393248 | tf_op jit(solution)/shard_map/ppermute | solution.py:378
  192.6 4.6 %all-to-all-start.5 = ((bf16[16,384,128]{2,1,0:T(8,128)(2,1)}), bf16[16,384,128]{2,1,0:T(8,128)(2,1)S(1)}, u32[]{:S(2)}, u32[]{:S(2)}) async-start(bf16[16,384,128]{2,1,0:T(8,128)(2,1)} %bitcast.45), calls=%async_computation.5 | async-start | bytes 3145728 | tf_op jit(solution)/shard_map/all_to_all | solution.py:306
  198.0 6.7 %shard_map.92 = (bf16[4,4,384,128]{3,2,1,0:T(8,128)(2,1)S(1)}, bf16[7168,256]{1,0:T(8,128)(2,1)}, bf16[7168,256]{1,0:T(8,128)(2,1)}) custom-call(s32[4,4]{1,0:T(4,128)S(1)} %pad_add_fusion.2.info, bf16[4,4,1,384,128]{4,3,2,1,0:T(8,128)(2,1)} %bitcast.96, bf16[4,4,1,384,128]{4,3,2,1,0:T(8,128)(2,1)} %bitcast.12.refs_1_, ...), custom_call_target="tpu_custom_call", output_to_operand_aliasing={{1}: (5, {}), {2}: (6, {})} | custom-call | flops 880803840 | bytes 2752512 | tf_op jit(solution)/shard_map/pallas_call | solution.py:151
  206.1 10.7 %shard_map.93 = (bf16[4,384,128]{2,1,0:T(8,128)(2,1)S(1)}, bf16[4,384,128]{2,1,0:T(8,128)(2,1)S(1)}, bf16[7168,256]{1,0:T(8,128)(2,1)}, bf16[7168,256]{1,0:T(8,128)(2,1)}) custom-call(s32[4,8]{1,0:T(4,128)S(1)} %fusion.info, bf16[4,384,128]{2,1,0:T(8,128)(2,1)S(1)} %collective-permute-done.10.refs_0_, ...), custom_call_target="tpu_custom_call", output_to_operand_aliasing={{2}: (7, {}), {3}: (8, {})} | custom-call | flops 1761607680 | bytes 5505024 | tf_op jit(solution)/shard_map/pallas_call | solution.py:151
  218.4 5.9 %shard_map.94 = (bf16[4,384,128]{2,1,0:T(8,128)(2,1)S(1)}, bf16[7168,256]{1,0:T(8,128)(2,1)}, bf16[7168,256]{1,0:T(8,128)(2,1)}) custom-call(s32[4,4]{1,0:T(4,128)S(1)} %get-tuple-element.61.info, bf16[4,384,128]{2,1,0:T(8,128)(2,1)S(1)} %collective-permute-done.16.refs_0_, ...), custom_call_target="tpu_custom_call", output_to_operand_aliasing={{1}: (5, {}), {2}: (6, {})} | custom-call | flops 880803840 | bytes 2752512 | tf_op jit(solution)/shard_map/pallas_call | solution.py:151
  224.3 2.7 collective-permute-start.18
  228.4 8.9 %collective-permute-done.18 = bf16[4,384,128]{2,1,0:T(8,128)(2,1)S(1)} collective-permute-done((bf16[4,384,128]{2,1,0:T(8,128)(2,1)S(1)}, bf16[4,384,128]{2,1,0:T(8,128)(2,1)S(1)}, u32[]{:S(2)}, u32[]{:S(2)}) %collective-permute-start.18) | collective-permute-done | bytes 393248 | tf_op jit(solution)/shard_map/ppermute | solution.py:378
  238.5 4.6 %all-to-all-start.4 = ((bf16[16,384,128]{2,1,0:T(8,128)(2,1)}), bf16[16,384,128]{2,1,0:T(8,128)(2,1)S(1)}, u32[]{:S(2)}, u32[]{:S(2)}) async-start(bf16[16,384,128]{2,1,0:T(8,128)(2,1)} %bitcast.89), calls=%async_computation.4 | async-start | bytes 3145728 | tf_op jit(solution)/shard_map/all_to_all | solution.py:306
  245.3 14.6 %all-to-all-done.4 = bf16[16,384,128]{2,1,0:T(8,128)(2,1)S(1)} async-done(((bf16[16,384,128]{2,1,0:T(8,128)(2,1)}), bf16[16,384,128]{2,1,0:T(8,128)(2,1)S(1)}, u32[]{:S(2)}, u32[]{:S(2)}) %all-to-all-start.4) | async-done | bytes 1572896 | tf_op jit(solution)/shard_map/all_to_all | solution.py:306
  260.0 5.1 %collective-permute-start.19 = (bf16[4,2,384,128]{3,2,1,0:T(8,128)(2,1)S(1)}, bf16[4,2,384,128]{3,2,1,0:T(8,128)(2,1)S(1)}, u32[]{:S(2)}, u32[]{:S(2)}) collective-permute-start(bf16[4,2,384,128]{3,2,1,0:T(8,128)(2,1)S(1)} %slice_bitcast_fusion.1), channel_id=1, source_target_pairs={{0,1},{1,0},{2,3},{3,2},{4,5},{5,4},{6,7},{7,6},{8,9},{9,8},{10,11... | collective-permute-start | bytes 2359304 | tf_op jit(solution)/shard_map/ppermute | solution.py:382
  (80 shorter events, 51.6 us)
Async XLA Ops:
  6.2 3.4 %collective-permute-start = (bf16[4,2,1,384,128]{4,3,2,1,0:T(8,128)(2,1)S(1)}, bf16[4,2,1,384,128]{4,3,2,1,0:T(8,128)(2,1)S(1)}, u32[]{:S(2)}, u32[]{:S(2)}) collective-permute-start(bf16[4,2,1,384,128]{4,3,2,1,0:T(8,128)(2,1)S(1)} %get-tuple-element.40), channel_id=1, source_target_pairs={{0,1},{1,0},{2,3},{3,2},{4,5},{5,4},{6,7},{7,6},{8,9},{9,8},{10,11... | collective-permute-start | bytes 2359304 | tf_op jit(solution)/shard_map/ppermute | solution.py:337
  10.6 29.3 %all-to-all-start = ((bf16[16,1,384,128]{3,2,1,0:T(8,128)(2,1)}), bf16[16,1,384,128]{3,2,1,0:T(8,128)(2,1)S(1)}, u32[]{:S(2)}, u32[]{:S(2)}) async-start(bf16[16,1,384,128]{3,2,1,0:T(8,128)(2,1)} %bitcast.5), calls=%async_computation | async-start | bytes 3145728 | tf_op jit(solution)/shard_map/all_to_all | solution.py:306
  22.6 2.4 collective-permute-start.2
  39.9 114.8 %copy-start.1 = (bf16[16,1,384,128]{3,2,1,0:T(8,128)(2,1)}, bf16[16,1,384,128]{3,2,1,0:T(8,128)(2,1)S(1)}, u32[]{:S(2)}) copy-start(bf16[16,1,384,128]{3,2,1,0:T(8,128)(2,1)S(1)} %all-to-all-done) | copy-start | bytes 4718596
  39.9 27.5 %all-to-all-start.2 = ((bf16[16,1,384,128]{3,2,1,0:T(8,128)(2,1)}), bf16[16,1,384,128]{3,2,1,0:T(8,128)(2,1)}, u32[]{:S(2)}, u32[]{:S(2)}) async-start(bf16[16,1,384,128]{3,2,1,0:T(8,128)(2,1)} %bitcast.17), calls=%async_computation.2 | async-start | bytes 3145728 | tf_op jit(solution)/shard_map/all_to_all | solution.py:306
  49.8 2.4 collective-permute-start.5
  67.3 27.3 %all-to-all-start.3 = ((bf16[16,1,384,128]{3,2,1,0:T(8,128)(2,1)}), bf16[16,1,384,128]{3,2,1,0:T(8,128)(2,1)}, u32[]{:S(2)}, u32[]{:S(2)}) async-start(bf16[16,1,384,128]{3,2,1,0:T(8,128)(2,1)} %bitcast.24), calls=%async_computation.3 | async-start | bytes 3145728 | tf_op jit(solution)/shard_map/all_to_all | solution.py:306
  77.2 2.4 collective-permute-start.1
  94.6 63.8 %all-to-all-start.1 = ((bf16[16,1,384,128]{3,2,1,0:T(8,128)(2,1)}), bf16[16,1,384,128]{3,2,1,0:T(8,128)(2,1)}, u32[]{:S(2)}, u32[]{:S(2)}) async-start(bf16[16,1,384,128]{3,2,1,0:T(8,128)(2,1)} %bitcast.11), calls=%async_computation.1 | async-start | bytes 3145728 | tf_op jit(solution)/shard_map/all_to_all | solution.py:306
  102.7 12.5 %collective-permute-start.8 = (bf16[4,384,128]{2,1,0:T(8,128)(2,1)S(1)}, bf16[4,384,128]{2,1,0:T(8,128)(2,1)S(1)}, u32[]{:S(2)}, u32[]{:S(2)}) collective-permute-start(bf16[4,384,128]{2,1,0:T(8,128)(2,1)S(1)} %get-tuple-element.80), channel_id=1, source_target_pairs={{0,32},{1,33},{2,34},{3,35},{4,36},{5,37},{6,38},{7,39},{8,40},{9,... | collective-permute-start | bytes 1179656 | tf_op jit(solution)/shard_map/ppermute | solution.py:356
  105.3 18.0 %collective-permute-start.9 = (bf16[4,384,128]{2,1,0:T(8,128)(2,1)S(1)}, bf16[4,384,128]{2,1,0:T(8,128)(2,1)S(1)}, u32[]{:S(2)}, u32[]{:S(2)}) collective-permute-start(bf16[4,384,128]{2,1,0:T(8,128)(2,1)S(1)} %get-tuple-element.77), channel_id=1, source_target_pairs={{0,32},{1,33},{2,34},{3,35},{4,36},{5,37},{6,38},{7,39},{8,40},{9,... | collective-permute-start | bytes 1179656 | tf_op jit(solution)/shard_map/ppermute | solution.py:356
  106.5 24.3 %collective-permute-start.3 = (bf16[4,384,128]{2,1,0:T(8,128)(2,1)S(1)}, bf16[4,384,128]{2,1,0:T(8,128)(2,1)S(1)}, u32[]{:S(2)}, u32[]{:S(2)}) collective-permute-start(bf16[4,384,128]{2,1,0:T(8,128)(2,1)S(1)} %get-tuple-element.82), channel_id=1, source_target_pairs={{0,96},{1,97},{2,98},{3,99},{4,100},{5,101},{6,102},{7,103},{8,104... | collective-permute-start | bytes 1179656 | tf_op jit(solution)/shard_map/ppermute | solution.py:356
  108.0 24.9 %collective-permute-start.4 = (bf16[4,384,128]{2,1,0:T(8,128)(2,1)S(1)}, bf16[4,384,128]{2,1,0:T(8,128)(2,1)S(1)}, u32[]{:S(2)}, u32[]{:S(2)}) collective-permute-start(bf16[4,384,128]{2,1,0:T(8,128)(2,1)S(1)} %get-tuple-element.81), channel_id=1, source_target_pairs={{0,64},{1,65},{2,66},{3,67},{4,68},{5,69},{6,70},{7,71},{8,72},{9,... | collective-permute-start | bytes 1179656 | tf_op jit(solution)/shard_map/ppermute | solution.py:356
  109.2 24.9 %collective-permute-start.6 = (bf16[4,384,128]{2,1,0:T(8,128)(2,1)S(1)}, bf16[4,384,128]{2,1,0:T(8,128)(2,1)S(1)}, u32[]{:S(2)}, u32[]{:S(2)}) collective-permute-start(bf16[4,384,128]{2,1,0:T(8,128)(2,1)S(1)} %get-tuple-element.79), channel_id=1, source_target_pairs={{0,96},{1,97},{2,98},{3,99},{4,100},{5,101},{6,102},{7,103},{8,104... | collective-permute-start | bytes 1179656 | tf_op jit(solution)/shard_map/ppermute | solution.py:356
  115.2 25.9 %collective-permute-start.7 = (bf16[4,384,128]{2,1,0:T(8,128)(2,1)S(1)}, bf16[4,384,128]{2,1,0:T(8,128)(2,1)S(1)}, u32[]{:S(2)}, u32[]{:S(2)}) collective-permute-start(bf16[4,384,128]{2,1,0:T(8,128)(2,1)S(1)} %get-tuple-element.78), channel_id=1, source_target_pairs={{0,64},{1,65},{2,66},{3,67},{4,68},{5,69},{6,70},{7,71},{8,72},{9,... | collective-permute-start | bytes 1179656 | tf_op jit(solution)/shard_map/ppermute | solution.py:356
  130.0 31.2 %collective-permute-start.20 = (bf16[4,384,128]{2,1,0:T(8,128)(2,1)S(1)}, bf16[4,384,128]{2,1,0:T(8,128)(2,1)}, u32[]{:S(2)}, u32[]{:S(2)}) collective-permute-start(bf16[4,384,128]{2,1,0:T(8,128)(2,1)S(1)} %get-tuple-element.66), channel_id=1, source_target_pairs={{0,96},{1,97},{2,98},{3,99},{4,100},{5,101},{6,102},{7,103},{8,104... | collective-permute-start | bytes 1179656 | tf_op jit(solution)/shard_map/ppermute | solution.py:378
  152.0 13.8 %collective-permute-start.21 = (bf16[4,384,128]{2,1,0:T(8,128)(2,1)S(1)}, bf16[4,384,128]{2,1,0:T(8,128)(2,1)}, u32[]{:S(2)}, u32[]{:S(2)}) collective-permute-start(bf16[4,384,128]{2,1,0:T(8,128)(2,1)S(1)} %get-tuple-element.67), channel_id=1, source_target_pairs={{0,32},{1,33},{2,34},{3,35},{4,36},{5,37},{6,38},{7,39},{8,40},{9,... | collective-permute-start | bytes 1179656 | tf_op jit(solution)/shard_map/ppermute | solution.py:378
  155.8 48.9 %collective-permute-start.10 = (bf16[4,384,128]{2,1,0:T(8,128)(2,1)}, bf16[4,384,128]{2,1,0:T(8,128)(2,1)S(1)}, u32[]{:S(2)}, u32[]{:S(2)}) collective-permute-start(bf16[4,384,128]{2,1,0:T(8,128)(2,1)} %get-tuple-element.76), channel_id=1, source_target_pairs={{0,32},{1,33},{2,34},{3,35},{4,36},{5,37},{6,38},{7,39},{8,40},{9,... | collective-permute-start | bytes 1179656 | tf_op jit(solution)/shard_map/ppermute | solution.py:356
  155.8 50.3 %collective-permute-start.11 = (bf16[4,384,128]{2,1,0:T(8,128)(2,1)}, bf16[4,384,128]{2,1,0:T(8,128)(2,1)}, u32[]{:S(2)}, u32[]{:S(2)}) collective-permute-start(bf16[4,384,128]{2,1,0:T(8,128)(2,1)} %get-tuple-element.75), channel_id=1, source_target_pairs={{0,96},{1,97},{2,98},{3,99},{4,100},{5,101},{6,102},{7,103},{8,104... | collective-permute-start | bytes 1179656 | tf_op jit(solution)/shard_map/ppermute | solution.py:356
  160.7 45.4 %collective-permute-start.12 = (bf16[4,384,128]{2,1,0:T(8,128)(2,1)}, bf16[4,384,128]{2,1,0:T(8,128)(2,1)}, u32[]{:S(2)}, u32[]{:S(2)}) collective-permute-start(bf16[4,384,128]{2,1,0:T(8,128)(2,1)} %get-tuple-element.73), channel_id=1, source_target_pairs={{0,32},{1,33},{2,34},{3,35},{4,36},{5,37},{6,38},{7,39},{8,40},{9,... | collective-permute-start | bytes 1179656 | tf_op jit(solution)/shard_map/ppermute | solution.py:356
  161.1 30.7 %collective-permute-start.22 = (bf16[4,384,128]{2,1,0:T(8,128)(2,1)S(1)}, bf16[4,384,128]{2,1,0:T(8,128)(2,1)S(1)}, u32[]{:S(2)}, u32[]{:S(2)}) collective-permute-start(bf16[4,384,128]{2,1,0:T(8,128)(2,1)S(1)} %get-tuple-element.68), channel_id=1, source_target_pairs={{0,64},{1,65},{2,66},{3,67},{4,68},{5,69},{6,70},{7,71},{8,72},{9,... | collective-permute-start | bytes 1179656 | tf_op jit(solution)/shard_map/ppermute | solution.py:378
  165.8 40.3 %collective-permute-start.13 = (bf16[4,384,128]{2,1,0:T(8,128)(2,1)}, bf16[4,384,128]{2,1,0:T(8,128)(2,1)}, u32[]{:S(2)}, u32[]{:S(2)}) collective-permute-start(bf16[4,384,128]{2,1,0:T(8,128)(2,1)} %get-tuple-element.72), channel_id=1, source_target_pairs={{0,96},{1,97},{2,98},{3,99},{4,100},{5,101},{6,102},{7,103},{8,104... | collective-permute-start | bytes 1179656 | tf_op jit(solution)/shard_map/ppermute | solution.py:356
  192.6 44.7 %all-to-all-start.5 = ((bf16[16,384,128]{2,1,0:T(8,128)(2,1)}), bf16[16,384,128]{2,1,0:T(8,128)(2,1)S(1)}, u32[]{:S(2)}, u32[]{:S(2)}) async-start(bf16[16,384,128]{2,1,0:T(8,128)(2,1)} %bitcast.45), calls=%async_computation.5 | async-start | bytes 3145728 | tf_op jit(solution)/shard_map/all_to_all | solution.py:306
  197.2 21.1 %collective-permute-start.16 = (bf16[4,384,128]{2,1,0:T(8,128)(2,1)}, bf16[4,384,128]{2,1,0:T(8,128)(2,1)S(1)}, u32[]{:S(2)}, u32[]{:S(2)}) collective-permute-start(bf16[4,384,128]{2,1,0:T(8,128)(2,1)} %get-tuple-element.74), channel_id=1, source_target_pairs={{0,64},{1,65},{2,66},{3,67},{4,68},{5,69},{6,70},{7,71},{8,72},{9,... | collective-permute-start | bytes 1179656 | tf_op jit(solution)/shard_map/ppermute | solution.py:356
  198.0 6.7 %copy-start.2 = (bf16[4,384,128]{2,1,0:T(8,128)(2,1)S(1)}, bf16[4,384,128]{2,1,0:T(8,128)(2,1)}, u32[]{:S(2)}) copy-start(bf16[4,384,128]{2,1,0:T(8,128)(2,1)} %get-tuple-element.71) | copy-start | bytes 1179652
  204.7 13.7 %collective-permute-start.17 = (bf16[4,384,128]{2,1,0:T(8,128)(2,1)S(1)}, bf16[4,384,128]{2,1,0:T(8,128)(2,1)S(1)}, u32[]{:S(2)}, u32[]{:S(2)}) collective-permute-start(bf16[4,384,128]{2,1,0:T(8,128)(2,1)S(1)} %copy-done.2), channel_id=1, source_target_pairs={{0,64},{1,65},{2,66},{3,67},{4,68},{5,69},{6,70},{7,71},{8,72},{9,... | collective-permute-start | bytes 1179656 | tf_op jit(solution)/shard_map/ppermute | solution.py:356
  216.8 10.1 %collective-permute-start.14 = (bf16[4,384,128]{2,1,0:T(8,128)(2,1)S(1)}, bf16[4,384,128]{2,1,0:T(8,128)(2,1)S(1)}, u32[]{:S(2)}, u32[]{:S(2)}) collective-permute-start(bf16[4,384,128]{2,1,0:T(8,128)(2,1)S(1)} %get-tuple-element.59), channel_id=1, source_target_pairs={{0,96},{1,97},{2,98},{3,99},{4,100},{5,101},{6,102},{7,103},{8,104... | collective-permute-start | bytes 1179656 | tf_op jit(solution)/shard_map/ppermute | solution.py:378
  216.9 11.4 %collective-permute-start.15 = (bf16[4,384,128]{2,1,0:T(8,128)(2,1)S(1)}, bf16[4,384,128]{2,1,0:T(8,128)(2,1)S(1)}, u32[]{:S(2)}, u32[]{:S(2)}) collective-permute-start(bf16[4,384,128]{2,1,0:T(8,128)(2,1)S(1)} %get-tuple-element.60), channel_id=1, source_target_pairs={{0,32},{1,33},{2,34},{3,35},{4,36},{5,37},{6,38},{7,39},{8,40},{9,... | collective-permute-start | bytes 1179656 | tf_op jit(solution)/shard_map/ppermute | solution.py:378
  224.3 13.0 %collective-permute-start.18 = (bf16[4,384,128]{2,1,0:T(8,128)(2,1)S(1)}, bf16[4,384,128]{2,1,0:T(8,128)(2,1)S(1)}, u32[]{:S(2)}, u32[]{:S(2)}) collective-permute-start(bf16[4,384,128]{2,1,0:T(8,128)(2,1)S(1)} %get-tuple-element.64), channel_id=1, source_target_pairs={{0,64},{1,65},{2,66},{3,67},{4,68},{5,69},{6,70},{7,71},{8,72},{9,... | collective-permute-start | bytes 1179656 | tf_op jit(solution)/shard_map/ppermute | solution.py:378
  238.5 21.4 %all-to-all-start.4 = ((bf16[16,384,128]{2,1,0:T(8,128)(2,1)}), bf16[16,384,128]{2,1,0:T(8,128)(2,1)S(1)}, u32[]{:S(2)}, u32[]{:S(2)}) async-start(bf16[16,384,128]{2,1,0:T(8,128)(2,1)} %bitcast.89), calls=%async_computation.4 | async-start | bytes 3145728 | tf_op jit(solution)/shard_map/all_to_all | solution.py:306
  244.0 23.0 %collective-permute-start.23 = (bf16[4,2,384,128]{3,2,1,0:T(8,128)(2,1)}, bf16[4,2,384,128]{3,2,1,0:T(8,128)(2,1)}, u32[]{:S(2)}, u32[]{:S(2)}) collective-permute-start(bf16[4,2,384,128]{3,2,1,0:T(8,128)(2,1)} %slice_bitcast_fusion), channel_id=1, source_target_pairs={{0,1},{1,0},{2,3},{3,2},{4,5},{5,4},{6,7},{7,6},{8,9},{9,8},{10,11... | collective-permute-start | bytes 2359304 | tf_op jit(solution)/shard_map/ppermute | solution.py:382
  260.0 11.1 %collective-permute-start.19 = (bf16[4,2,384,128]{3,2,1,0:T(8,128)(2,1)S(1)}, bf16[4,2,384,128]{3,2,1,0:T(8,128)(2,1)S(1)}, u32[]{:S(2)}, u32[]{:S(2)}) collective-permute-start(bf16[4,2,384,128]{3,2,1,0:T(8,128)(2,1)S(1)} %slice_bitcast_fusion.1), channel_id=1, source_target_pairs={{0,1},{1,0},{2,3},{3,2},{4,5},{5,4},{6,7},{7,6},{8,9},{9,8},{10,11... | collective-permute-start | bytes 2359304 | tf_op jit(solution)/shard_map/ppermute | solution.py:382
  (1 other events, 1.1 us)
